TPU v7x, 768 devices: a whole 4x8x12 slice. The times are simulated.
768 devices in a mesh: dp: 12 (over z), seq: 64 (over y, x, core).
Axes of the slice: x: 4, y: 8, z: 12, core: 2. Of those that a mesh axis runs over, the one named last changes fastest.
Arguments:
- hidden: bfloat16 [12, 16384, 1024], P('dp', 'seq'), may hold values from -6 to 6
- segment_ids: int32 [12, 16384], P('dp'), may hold values from 0 to 255, never falling along the last dimension, each value on 1 to 512 neighbouring positions
- kernel: float32 [31, 1024], replicated, may hold values from -1 to 1
- norm_gain: float32 [1024], replicated, may hold values from 0.5 to 1.5
- projection: bfloat16 [1024, 1024], replicated, may hold values from -0.1875 to 0.1875
- cotangent: bfloat16 [12, 16384, 1024], P('dp', 'seq'), may hold values from -16 to 16
Outputs:
- conv_out: bfloat16 [12, 16384, 1024], P('dp', 'seq')
- grad_hidden: bfloat16 [12, 16384, 1024], P('dp', 'seq')
- grad_projection: float32 [1024, 1024], P('seq')
- grad_kernel: float32 [1024, 31], P('seq')
- grad_gain: float32 [1024], P('seq')
Inputs may be any that keep to these rules, and one draw needn't show every extreme that they name: `segment_ids`: within a row utterance numbers never fall, every number 0 to 255 occurs, each utterance spans 1 to 512 frames and one spans exactly 512.
All inputs are finite; a program needn't handle non-finite values.
Results may differ from a plain program's by a relative error of at most 0.005.
Values may be sent and summed in bfloat16 or wider, within the bound.
No kernel may reach another device: no remote copies, remote signals or barrier semaphores. Data moves between devices by JAX's collectives and lax.ppermute only.
A program may use at most 64 MiB of HBM per device.

v0:
```python
import math

import jax
import jax.numpy as jnp
from jax import lax
from jax.sharding import PartitionSpec as P

EPS = 1e-05


def padded_2(value, sides, width):
    for axis, dim in sides:
        count, length = (lax.axis_size(axis), value.shape[dim])
        up = [(i, (i + 1) % count) for i in range(count - 1)]
        down = [(j, i) for i, j in up]
        last = lax.slice_in_dim(value, length - width, length, axis=dim)
        first = lax.slice_in_dim(value, 0, width, axis=dim)
        before = lax.ppermute(last, axis, up)
        after = lax.ppermute(first, axis, down)
        value = jnp.concatenate([before, value, after], axis=dim)
    return value


def from_behind(value, axis, steps):
    count = lax.axis_size(axis)
    first, last = (max(0, -steps), min(count, count - steps))
    return lax.ppermute(value, axis, [(source, source + steps) for source in range(first, last)])


def from_everyone(value, axis):
    copies = jnp.broadcast_to(value, (lax.axis_size(axis), *value.shape))
    return lax.all_to_all(copies, axis, split_axis=0, concat_axis=0, tiled=True)


def over_copies(value, axis):
    return from_everyone(value, axis).sum(axis=0)


def depth_forward(padded, segs, kernel, length):
    reach = kernel.shape[0] // 2
    total = jnp.zeros((length, kernel.shape[1]), jnp.float32)
    centre = segs[reach : reach + length]
    for offset in range(kernel.shape[0]):
        same = (segs[offset : offset + length] == centre).astype(jnp.float32)[:, None]
        total = total + kernel[offset] * padded[offset : offset + length].astype(jnp.float32) * same
    return total


def kernel_terms(grad, padded, segs, length, taps):
    reach = taps // 2
    centre = segs[reach : reach + length]
    rows_out = []
    for offset in range(taps):
        same = (segs[offset : offset + length] == centre).astype(jnp.float32)[:, None]
        rows_out.append(
            jnp.sum(grad * padded[offset : offset + length].astype(jnp.float32) * same, 0)
        )
    return jnp.stack(rows_out, 0)


def spread_back(grid, segs, kernel, length):
    reach = kernel.shape[0] // 2
    total = jnp.zeros((length, kernel.shape[1]), jnp.float32)
    centre = segs[reach : reach + length]
    for offset in range(kernel.shape[0]):
        lower = 2 * reach - offset
        same = (segs[lower : lower + length] == centre).astype(jnp.float32)[:, None]
        total = total + kernel[offset] * grid[lower : lower + length] * same
    return total


def norm_forward(mixed, norm_gain):
    centred = mixed - jnp.mean(mixed, -1, keepdims=True)
    variance = jnp.mean(centred * centred, -1, keepdims=True)
    scale_inv = lax.rsqrt(variance + EPS)
    normed = centred * scale_inv
    gated = normed * norm_gain
    sigma = jax.nn.sigmoid(gated)
    act = (gated * sigma).astype(jnp.bfloat16)
    return (normed, scale_inv, gated, sigma, act)


def norm_backward(grad_act, normed, scale_inv, gated, sigma, norm_gain):
    grad_gated = grad_act * sigma * (1.0 + gated * (1.0 - sigma))
    grad_normed = grad_gated * norm_gain
    grad_mixed = scale_inv * (
        grad_normed
        - jnp.mean(grad_normed, -1, keepdims=True)
        - normed * jnp.mean(grad_normed * normed, -1, keepdims=True)
    )
    return (grad_gated, grad_mixed)


def body(hidden, segment_ids, kernel, norm_gain, projection, cotangent):
    frames_local = hidden[0]
    length = frames_local.shape[0]
    width = frames_local.shape[1]
    taps = kernel.shape[0]
    reach = taps // 2
    start = lax.axis_index("seq") * length
    seg_row = jnp.pad(segment_ids[0], 2 * reach, constant_values=-1)
    seg_wide = lax.dynamic_slice_in_dim(seg_row, start, length + 4 * reach)
    seg_near = seg_wide[reach : reach + length + 2 * reach]
    grad_out = cotangent[0]
    received = padded_2(frames_local, (("seq", 0),), reach)
    mixed = depth_forward(received, seg_near, kernel, length)
    normed, scale_inv, gated, sigma, act = norm_forward(mixed, norm_gain)
    conv_out = jnp.dot(act, projection.T, preferred_element_type=jnp.float32).astype(jnp.bfloat16)
    grad_act = jnp.dot(grad_out, projection, preferred_element_type=jnp.float32)
    grad_gated, grad_mixed = norm_backward(grad_act, normed, scale_inv, gated, sigma, norm_gain)
    zeroed = jnp.pad(grad_mixed, ((2 * reach, 2 * reach), (0, 0)))
    partial_back = spread_back(zeroed, seg_wide, kernel, length + 2 * reach)
    from_lower = from_behind(partial_back[length + reach :].astype(jnp.bfloat16), "seq", 1).astype(
        jnp.float32
    )
    from_upper = from_behind(partial_back[:reach].astype(jnp.bfloat16), "seq", -1).astype(
        jnp.float32
    )
    inner = partial_back[reach : reach + length]
    grad_frames = inner.at[:reach].add(from_lower).at[length - reach :].add(from_upper)
    kernel_grad = kernel_terms(grad_mixed, received, seg_near, length, taps)
    gain_grad = jnp.sum(grad_gated * normed, 0)
    grad_hidden = grad_frames.astype(jnp.bfloat16)
    small_grads = jnp.concatenate([kernel_grad.T, gain_grad[:, None]], 1)
    weight_part = jnp.dot(grad_out.T, act, preferred_element_type=jnp.float32)
    shares = lax.psum_scatter(
        jnp.concatenate([weight_part, small_grads], 1), "seq", scatter_dimension=0, tiled=True
    )
    totals = over_copies(shares, "dp")
    factor = 1.0 / math.sqrt(length * lax.axis_size("seq") * lax.axis_size("dp"))
    totals = totals * factor
    return (
        conv_out[None],
        grad_hidden[None],
        totals[:, :width],
        totals[:, width : width + taps],
        totals[:, width + taps],
    )


def solution(mesh):
    in_specs = (P("dp", "seq", None), P("dp", None), P(), P(), P(), P("dp", "seq", None))
    out_specs = (
        P("dp", "seq", None),
        P("dp", "seq", None),
        P("seq", None),
        P("seq", None),
        P("seq"),
    )
    return jax.shard_map(body, mesh=mesh, in_specs=in_specs, out_specs=out_specs, check_vma=False)
```

profile of v0, /device:TPU:89, one launch (start us, length us, event | category | flops | bytes accessed | tf_op | source)
XLA Modules:
  0.0 355.4 jit_solution(12654320270951042774)
XLA Ops:
  7.2 0.0 all-reduce.5.cloned.1.call-start
  7.2 0.9 slice_bitcast_fusion.1
  8.2 2.6 collective-permute-start.1
  10.7 3.0 collective-permute-start
  13.8 1.1 fusion.280
  14.9 1.3 fusion.279
  16.2 0.8 pad_dynamic-slice_fusion
  17.0 0.1 compare_convert_fusion.29
  17.1 0.1 compare_convert_fusion.28
  17.2 0.1 compare_convert_fusion.27
  17.2 0.1 compare_convert_fusion.26
  17.4 22.3 %fusion.276 = (f32[256]{0:T(256)S(1)}, f32[256,1024]{1,0:T(8,128)S(1)}) fusion(f32[256]{0:T(256)S(1)} %get-tuple-element.136, bf16[15,1024]{1,0:T(8,128)(2,1)S(1)} %collective-permute-done.1, bf16[256,1024]{1,0:T(8,128)(2,1)} %bitcast.89, f32[1024]{0:T(1024)S(1)} %bitcast.117, f32[256]{0:T(256)S(1)} %get-tuple-element.137, f32[1024]{0:T(1024)S(1)} %bitcast.119, ...), kind=kLoop, calls=%fused_computation.482 | loop fusion | flops 55836416 | bytes 1793024 | tf_op jit(solution)/shard_map/reduce_sum | solution.py:73
  39.7 0.2 multiply_reduce_fusion.2
  40.0 2.9 convolution_bitcast_fusion
  42.9 1.7 multiply_reduce_fusion
  44.7 3.4 fusion.213
  48.1 0.2 fusion.162
  48.3 2.0 fusion.171
  50.3 1.9 fusion.143
  52.2 1.5 fusion.161
  53.7 3.3 fusion.189
  57.0 1.0 stack.127
  57.9 12.2 %concatenate.44 = f32[1024,1056]{0,1:T(8,128)} concatenate(f32[1024,1024]{0,1:T(8,128)} %convolution_bitcast_fusion, f32[1024,31]{0,1:T(8,128)S(1)} %bitcast.95, f32[1024,1]{0,1:T(1,128)} %bitcast.190), dimensions={1} | concatenate | bytes 8650752 | tf_op jit(solution)/shard_map/concatenate | solution.py:127
  70.1 0.0 all-reduce.5.cloned.1.call-update
  70.1 1.3 dynamic-slice.16
  72.0 0.1 fusion.247
  72.1 0.1 fusion.244
  72.2 0.1 fusion.245
  72.3 0.1 fusion.246
  72.3 224.0 %all-reduce.5.cloned.1.call-done = f32[1024,1056]{0,1:T(8,128)} async-done(((f32[1024,1056]{0,1:T(8,128)}), f32[1024,1056]{0,1:T(8,128)}) %all-reduce.5.cloned.1.call-update) | async-done | bytes 4325392
  296.4 2.1 constant_dynamic-slice_fusion
  298.5 1.2 copy.14
  299.7 1.0 broadcast_in_dim.11
  300.7 10.0 %all-to-all-start = ((f32[12,16,1056]{2,1,0:T(8,128)}), f32[12,16,1056]{2,1,0:T(8,128)}, u32[]{:S(2)}, u32[]{:S(2)}) async-start(f32[12,16,1056]{2,1,0:T(8,128)} %broadcast_in_dim.11), calls=%async_computation | async-start | bytes 1769472 | tf_op jit(solution)/shard_map/all_to_all | solution.py:32
  310.7 7.0 %fusion.274 = (bf16[286,1024]{1,0:T(8,128)(2,1)S(1)}, f32[286,1024]{1,0:T(8,128)S(1)}) fusion(f32[286]{0:T(512)S(1)} %get-tuple-element.133, f32[1024]{0:T(1024)S(1)} %bitcast.118, f32[286]{0:T(512)S(1)} %get-tuple-element.134, f32[1024]{0:T(1024)S(1)} %bitcast.120, f32[286]{0:T(512)S(1)} %get-tuple-element.106, f32[1024]{0:T(1024)S(1)} %bitcast.124, ...), kind=kLoop, calls=%fused_computation.481 | loop fusion | flops 26943488 | bytes 2967056 | tf_op jit(solution)/shard_map/convert.1
  317.7 1.9 collective-permute-start.2
  319.7 1.7 fusion.1
  321.3 0.1 slice.912
  321.5 2.4 collective-permute-start.3
  323.9 0.6 scatter-add.6
  324.5 2.6 collective-permute-done.3
  327.1 0.3 scatter-add.9
  327.5 0.9 convert_bitcast_fusion
  328.3 17.0 %all-to-all-done = f32[12,16,1056]{2,1,0:T(8,128)} async-done(((f32[12,16,1056]{2,1,0:T(8,128)}), f32[12,16,1056]{2,1,0:T(8,128)}, u32[]{:S(2)}, u32[]{:S(2)}) %all-to-all-start) | async-done | bytes 811040 | tf_op jit(solution)/shard_map/all_to_all | solution.py:32
  345.4 1.2 reduce_sum.369
  346.6 0.6 slice.917
  347.2 0.6 slice.918
  347.8 0.7 slice_reduce_fusion
  (32 shorter events, 0.1 us)
Async XLA Ops:
  7.2 35.7 %copy-start = (bf16[1024,1024]{1,0:T(8,128)(2,1)S(1)}, bf16[1024,1024]{1,0:T(8,128)(2,1)}, u32[]{:S(2)}) copy-start(bf16[1024,1024]{1,0:T(8,128)(2,1)} %param.14) | copy-start | bytes 6291460
  7.2 289.2 %all-reduce.5.cloned.1.call-start = ((), (), s32[]{:S(2)}) async-start(), calls=%async_computation.1 | async-start | bytes 8650752
  8.2 9.2 %collective-permute-start.1 = (bf16[15,1024]{1,0:T(8,128)(2,1)S(1)}, bf16[15,1024]{1,0:T(8,128)(2,1)S(1)}, u32[]{:S(2)}, u32[]{:S(2)}) collective-permute-start(bf16[15,1024]{1,0:T(8,128)(2,1)S(1)} %get-tuple-element.73), channel_id=1, source_target_pairs={{1,0},{2,1},{3,2},{4,3},{5,4},{6,5},{7,6},{8,7},{9,8},{10,9},{11,1... | collective-permute-start | bytes 92168 | tf_op jit(solution)/shard_map/ppermute | solution.py:19
  10.7 6.6 %collective-permute-start = (bf16[15,1024]{1,0:T(8,128)(2,1)S(1)}, bf16[15,1024]{1,0:T(8,128)(2,1)S(1)}, u32[]{:S(2)}, u32[]{:S(2)}) collective-permute-start(bf16[15,1024]{1,0:T(8,128)(2,1)S(1)} %get-tuple-element.72), channel_id=1, source_target_pairs={{0,1},{1,2},{2,3},{3,4},{4,5},{5,6},{6,7},{7,8},{8,9},{9,10},{10,1... | collective-permute-start | bytes 92168 | tf_op jit(solution)/shard_map/ppermute | solution.py:18
  17.3 22.7 %copy-start.6 = (f32[1024]{0:T(1024)S(1)}, f32[1024]{0:T(1024)}, u32[]{:S(2)}) copy-start(f32[1024]{0:T(1024)} %param.13) | copy-start | bytes 12292
  17.3 22.7 %copy-start.10 = (bf16[1,256,1024]{2,1,0:T(8,128)(2,1)S(1)}, bf16[1,256,1024]{2,1,0:T(8,128)(2,1)}, u32[]{:S(2)}) copy-start(bf16[1,256,1024]{2,1,0:T(8,128)(2,1)} %param.15) | copy-start | bytes 1572868
  39.7 5.0 %copy-start.2 = (f32[256,1024]{1,0:T(8,128)}, f32[256,1024]{1,0:T(8,128)S(1)}, u32[]{:S(2)}) copy-start(f32[256,1024]{1,0:T(8,128)S(1)} %get-tuple-element.69) | copy-start | bytes 3145732
  39.7 4.9 %copy-start.4 = (f32[256]{0:T(256)}, f32[256]{0:T(256)S(1)}, u32[]{:S(2)}) copy-start(f32[256]{0:T(256)S(1)} %broadcast_multiply_fusion.3) | copy-start | bytes 3076
  40.0 4.7 %copy-start.8 = (f32[256]{0:T(256)}, f32[256]{0:T(256)S(1)}, u32[]{:S(2)}) copy-start(f32[256]{0:T(256)S(1)} %add_rsqrt_fusion) | copy-start | bytes 3076
  42.9 1.8 copy-start.1
  300.7 44.7 %all-to-all-start = ((f32[12,16,1056]{2,1,0:T(8,128)}), f32[12,16,1056]{2,1,0:T(8,128)}, u32[]{:S(2)}, u32[]{:S(2)}) async-start(f32[12,16,1056]{2,1,0:T(8,128)} %broadcast_in_dim.11), calls=%async_computation | async-start | bytes 1769472 | tf_op jit(solution)/shard_map/all_to_all | solution.py:32
  310.7 9.0 %copy-start.3 = (f32[256,1024]{1,0:T(8,128)S(1)}, f32[256,1024]{1,0:T(8,128)}, u32[]{:S(2)}) copy-start(f32[256,1024]{1,0:T(8,128)} %copy-done.2) | copy-start | bytes 3145732
  310.7 9.0 %copy-start.5 = (f32[256]{0:T(256)S(1)}, f32[256]{0:T(256)}, u32[]{:S(2)}) copy-start(f32[256]{0:T(256)} %copy-done.4) | copy-start | bytes 3076
  310.7 9.0 %copy-start.7 = (f32[1024]{0:T(1024)S(1)}, f32[1024]{0:T(1024)}, u32[]{:S(2)}) copy-start(f32[1024]{0:T(1024)} %param.13) | copy-start | bytes 12292
  310.7 9.0 %copy-start.9 = (f32[256]{0:T(256)S(1)}, f32[256]{0:T(256)}, u32[]{:S(2)}) copy-start(f32[256]{0:T(256)} %copy-done.8) | copy-start | bytes 3076
  317.7 6.2 %collective-permute-start.2 = (bf16[15,1024]{1,0:T(8,128)(2,1)S(1)}, bf16[15,1024]{1,0:T(8,128)(2,1)S(1)}, u32[]{:S(2)}, u32[]{:S(2)}) collective-permute-start(bf16[15,1024]{1,0:T(8,128)(2,1)S(1)} %get-tuple-element.71), channel_id=1, source_target_pairs={{0,1},{1,2},{2,3},{3,4},{4,5},{5,6},{6,7},{7,8},{8,9},{9,10},{10,1... | collective-permute-start | bytes 92168 | tf_op jit(solution)/shard_map/ppermute | solution.py:27
  321.5 5.6 %collective-permute-start.3 = (bf16[15,1024]{1,0:T(8,128)(2,1)S(1)}, bf16[15,1024]{1,0:T(8,128)(2,1)S(1)}, u32[]{:S(2)}, u32[]{:S(2)}) collective-permute-start(bf16[15,1024]{1,0:T(8,128)(2,1)S(1)} %get-tuple-element.70), channel_id=1, source_target_pairs={{1,0},{2,1},{3,2},{4,3},{5,4},{6,5},{7,6},{8,7},{9,8},{10,9},{11,1... | collective-permute-start | bytes 92168 | tf_op jit(solution)/shard_map/ppermute | solution.py:27
Sparse Core Ops, SparseCore 0:
  70.2 226.1 all-reduce.4
where the time goes:
time: 357 us; the launch traced here: 355 us
  waiting for transfers between devices  244 us (68%)
  other arithmetic  44.6 us (12%)
  local copies, waits for them, and re-layouts  25.8 us (7%)
  starting transfers between devices  19.9 us (6%)
  between operations  15 us (4%)
  matrix products  6.29 us (2%)
    unnamed x2, waiting for transfers between devices  224 us
    reduce_sum x1, other arithmetic, norm_forward(): centred = mixed - jnp.mean(mixed, -1, keepdims=True)  22.3 us
    all_to_all x1, waiting for transfers between devices, from_everyone(): return lax.all_to_all(copies, axis, split_axis=0, concat_axis=0, tiled=True)  17 us
    reduce_sum x6, other arithmetic, kernel_terms(): jnp.sum(grad * padded[offset:offset + length].astype(jnp.float32) * same, 0)  12.2 us
    concatenate x1, local copies, waits for them, and re-layouts, body(): jnp.concatenate([weight_part, small_grads], 1)  12.2 us
    all_to_all x1, starting transfers between devices, from_everyone(): return lax.all_to_all(copies, axis, split_axis=0, concat_axis=0, tiled=True)  9.97 us
  transfers between devices with their start and end apart: 6, of which 3 were waited for; matrix products, arithmetic and copies ran while one was open for 4% of the time, Pallas kernels for 0%

commit v1 on v0

v1 whole, which is shorter than its diff:
```python
import math
from functools import partial

import jax
import jax.numpy as jnp
from jax import lax
from jax.experimental import pallas as pl
from jax.experimental.pallas import tpu as pltpu
from jax.sharding import Mesh
from jax.sharding import PartitionSpec as P


EPS = 1e-05
LANES = 128
HALO = 16
ROWS = 32
BF = jnp.bfloat16
F32 = jnp.float32


def call(kernel, outs, scratch=(), flops=0, moved=0, trans=0, smem=()):
    def run(*args):
        specs = [
            pl.BlockSpec(memory_space=pltpu.SMEM if i in smem else pltpu.VMEM)
            for i in range(len(args))
        ]
        return pl.pallas_call(
            kernel,
            out_shape=outs,
            in_specs=specs,
            out_specs=jax.tree.map(lambda _: pl.BlockSpec(memory_space=pltpu.VMEM), outs),
            scratch_shapes=list(scratch),
            compiler_params=pltpu.CompilerParams(vmem_limit_bytes=18 * 1024 * 1024),
            cost_estimate=pl.CostEstimate(flops=flops, bytes_accessed=moved, transcendentals=trans),
        )(*args)

    return run


def deal(core, b, turned, own, cols, mine_ref, other_ref):
    pairs = LANES // (2 * own)
    rows = mine_ref.shape[0] // own // cols
    for j in range(pairs):
        even = turned[2 * own * j : 2 * own * j + own]
        odd = turned[2 * own * j + own : 2 * own * j + 2 * own]
        y, x = divmod(b * pairs + j, cols)
        at = (x * rows + y) * own
        mine_ref[at : at + own, :] = jnp.where(core == 0, even, odd)
        other_ref[at : at + own, :] = jnp.where(core == 0, odd, even)


def split_kernel(own, cols, core_ref, cot_ref, mine_ref, other_ref):
    for b in range(cot_ref.shape[1] // LANES):
        turned = cot_ref[:, b * LANES : (b + 1) * LANES].T
        deal(core_ref[0], b, turned, own, cols, mine_ref, other_ref)


def spread(dst, before, middle, after):
    blocks, rows = dst.shape[0], dst.shape[1]
    for b in range(blocks):
        lanes = slice(b * LANES, (b + 1) * LANES)
        dst[b, 0:HALO, :] = before[:, lanes].astype(F32)
        dst[b, HALO : rows - HALO, :] = middle[:, lanes].astype(F32)
        dst[b, rows - HALO : rows, :] = after[:, lanes].astype(F32)


def forward_kernel(hid_ref, bef_ref, aft_ref, seg_ref, kern_ref, gain_ref, act_ref, norm_ref, inv_ref, win):
    taps, width = kern_ref.shape
    length = hid_ref.shape[0]
    blocks = width // LANES
    spread(win, bef_ref, hid_ref, aft_ref)

    def step(i, carry):
        r0 = pl.multiple_of(i * ROWS, ROWS)
        centre = seg_ref[pl.ds(r0 + HALO, ROWS), :]
        acc = [jnp.zeros((ROWS, LANES), F32) for _ in range(blocks)]
        for k in range(taps):
            same = seg_ref[pl.ds(r0 + k + 1, ROWS), :] == centre
            for b in range(blocks):
                w = kern_ref[k : k + 1, b * LANES : (b + 1) * LANES]
                term = win[b, pl.ds(r0 + k + 1, ROWS), :] * w
                acc[b] = acc[b] + jnp.where(same, term, 0.0)
        total = acc[0]
        for b in range(1, blocks):
            total = total + acc[b]
        mean = jnp.sum(total, axis=1, keepdims=True) * (1.0 / width)
        acc = [a - mean for a in acc]
        total = acc[0] * acc[0]
        for b in range(1, blocks):
            total = total + acc[b] * acc[b]
        inv = lax.rsqrt(jnp.sum(total, axis=1, keepdims=True) * (1.0 / width) + EPS)
        inv_ref[pl.ds(r0, ROWS), :] = jnp.broadcast_to(inv, (ROWS, LANES))
        for b in range(blocks):
            lanes = slice(b * LANES, (b + 1) * LANES)
            normed = acc[b] * inv
            norm_ref[pl.ds(r0, ROWS), lanes] = normed
            gated = normed * gain_ref[:, lanes]
            act_ref[pl.ds(r0, ROWS), lanes] = (gated * jax.nn.sigmoid(gated)).astype(BF)
        return carry

    lax.fori_loop(0, length // ROWS, step, 0)


def product_kernel(mine_ref, got_ref, act_ref, act2_ref, out_ref):
    rows = mine_ref.shape[0]
    part = 128

    def step(i, carry):
        at = pl.ds(pl.multiple_of(i * part, part), part)
        total = jnp.dot(mine_ref[at, :], act_ref[...], preferred_element_type=F32)
        total = total + jnp.dot(got_ref[at, :], act2_ref[...], preferred_element_type=F32)
        out_ref[at, :] = total.astype(BF)
        return carry

    lax.fori_loop(0, rows // part, step, 0)


def norm_kernel(cot_ref, proj_ref, act_ref, norm_ref, inv_ref, gain_ref, out_ref, gm_ref, first_ref, last_ref, gg_ref):
    length, width = norm_ref.shape
    part = 64
    blocks = width // LANES
    nt = (((1,), (1,)), ((), ()))

    def step(i, carry):
        at = pl.ds(pl.multiple_of(i * part, part), part)
        out_ref[at, :] = lax.dot_general(act_ref[at, :], proj_ref[...], nt, preferred_element_type=F32).astype(BF)
        gm_ref[at, :] = jnp.dot(cot_ref[at, :], proj_ref[...], preferred_element_type=F32)
        return carry

    lax.fori_loop(0, length // part, step, 0)
    gg_ref[...] = jnp.zeros(gg_ref.shape, F32)

    def back(i, carry):
        at = pl.ds(pl.multiple_of(i * ROWS, ROWS), ROWS)
        sum_a = jnp.zeros((ROWS, LANES), F32)
        sum_b = jnp.zeros((ROWS, LANES), F32)
        kept = []
        for b in range(blocks):
            lanes = slice(b * LANES, (b + 1) * LANES)
            gain = gain_ref[:, lanes]
            normed = norm_ref[at, lanes]
            gated = normed * gain
            sigma = jax.nn.sigmoid(gated)
            gg = gm_ref[at, lanes] * sigma * (1.0 + gated * (1.0 - sigma))
            both = gg * normed
            rows8 = both[0:8]
            for r in range(8, ROWS, 8):
                rows8 = rows8 + both[r : r + 8]
            gg_ref[:, lanes] = gg_ref[:, lanes] + rows8
            gn = gg * gain
            sum_a = sum_a + gn
            sum_b = sum_b + gn * normed
            kept.append(gn)
        mean_a = jnp.sum(sum_a, axis=1, keepdims=True) * (1.0 / width)
        mean_b = jnp.sum(sum_b, axis=1, keepdims=True) * (1.0 / width)
        inv = inv_ref[at, :]
        for b in range(blocks):
            lanes = slice(b * LANES, (b + 1) * LANES)
            gm_ref[at, lanes] = inv * (kept[b] - mean_a - norm_ref[at, lanes] * mean_b)
        return carry

    lax.fori_loop(0, length // ROWS, back, 0)
    first_ref[...] = gm_ref[0:HALO, :]
    last_ref[...] = gm_ref[length - HALO : length, :]


def backward_kernel(
    own_rows, cols, core_ref, gm_ref, bef_ref, aft_ref, seg_ref, hid_ref, kern_ref, gg_ref, gh_ref, mine_ref, other_ref, win, kacc
):
    taps, width = kern_ref.shape
    length = hid_ref.shape[0]
    blocks = width // LANES
    group = 4
    spread(win, bef_ref, gm_ref, aft_ref)
    kacc[...] = jnp.zeros(kacc.shape, F32)

    def step(i, carry):
        r0 = pl.multiple_of(i * ROWS, ROWS)
        centre = seg_ref[pl.ds(r0 + HALO, ROWS), :]
        for g in range(blocks // group):
            own = range(g * group, (g + 1) * group)
            acc = {b: jnp.zeros((ROWS, LANES), F32) for b in own}
            hid = {b: hid_ref[pl.ds(r0, ROWS), b * LANES : (b + 1) * LANES].astype(F32) for b in own}
            for k in range(taps):
                same = seg_ref[pl.ds(r0 + taps - k, ROWS), :] == centre
                for b in own:
                    lanes = slice(b * LANES, (b + 1) * LANES)
                    grad = jnp.where(same, win[b, pl.ds(r0 + taps - k, ROWS), :], 0.0)
                    acc[b] = acc[b] + grad * kern_ref[k : k + 1, lanes]
                    prod = grad * hid[b]
                    rows8 = prod[0:8]
                    for r in range(8, ROWS, 8):
                        rows8 = rows8 + prod[r : r + 8]
                    kacc[k, :, lanes] = kacc[k, :, lanes] + rows8
            for b in own:
                gh_ref[pl.ds(r0, ROWS), b * LANES : (b + 1) * LANES] = acc[b].astype(BF)
        return carry

    lax.fori_loop(0, length // ROWS, step, 0)
    for b in range(blocks):
        lanes = slice(b * LANES, (b + 1) * LANES)
        rows = [jnp.sum(kacc[k, :, lanes], axis=0, keepdims=True) for k in range(taps)]
        rows.append(jnp.sum(gg_ref[:, lanes], axis=0, keepdims=True))
        rows.append(jnp.zeros((LANES - taps - 1, LANES), F32))
        deal(core_ref[0], b, jnp.concatenate(rows, axis=0).T, own_rows, cols, mine_ref, other_ref)


def join_kernel(landed_ref, t0_ref, t1_ref, t2_ref, t3_ref, out_ref):
    count, rows, width = landed_ref.shape

    def step(i, carry):
        at = pl.ds(pl.multiple_of(i * ROWS, ROWS), ROWS)
        total = landed_ref[0, at, :].astype(F32)
        for j in range(1, count):
            total = total + landed_ref[j, at, :].astype(F32)
        out_ref[at, :width] = total.astype(BF)
        out_ref[at, width:] = ((t0_ref[at, :] + t1_ref[at, :]) + (t2_ref[at, :] + t3_ref[at, :])).astype(BF)
        return carry

    lax.fori_loop(0, rows // ROWS, step, 0)


def final_kernel(factor, taps, a_ref, b_ref, c_ref, weight_ref, small_ref, gain_ref):
    low, high = jnp.minimum(a_ref[...], b_ref[...]), jnp.maximum(a_ref[...], b_ref[...])
    middle = jnp.maximum(low, jnp.minimum(high, c_ref[...]))
    total = ((jnp.minimum(low, c_ref[...]) + jnp.maximum(high, c_ref[...])) + middle) * factor
    width = weight_ref.shape[1]
    weight_ref[...] = total[:, :width]
    small_ref[...] = total[:, width : width + taps]
    gain_ref[...] = total[:, width:].T[taps : taps + 1, :]


SEQ = ("y", "x", "core")


def shifted(value, steps):
    count = lax.axis_size("y") * lax.axis_size("x") * lax.axis_size("core")
    first, last = max(0, -steps), min(count, count - steps)
    return lax.ppermute(value, SEQ, [(i, i + steps) for i in range(first, last)])


def over_groups(value):
    count = lax.axis_size("dp")

    def partner(mask):
        return lax.ppermute(value, "dp", [(i, i ^ mask) for i in range(count)])

    one, two, three = partner(1), partner(2), partner(3)
    value = (value + one) + (two + three)

    def ahead(by):
        return lax.ppermute(value, "dp", [(i, (i + by) % count) for i in range(count)])

    return value, ahead(4), ahead(count - 4)


def inner(hidden, segment_ids, kernel, norm_gain, projection, cotangent):
    frames = hidden[0]
    length, width = frames.shape
    taps = kernel.shape[0]
    cot = cotangent[0]
    ny, nx = lax.axis_size("y"), lax.axis_size("x")
    core = lax.axis_index("core")
    index = (lax.axis_index("y") * nx + lax.axis_index("x")) * 2 + core
    seg_row = jnp.pad(segment_ids[0], HALO, constant_values=-1)
    seg = lax.dynamic_slice_in_dim(seg_row, index * length, length + 2 * HALO)
    seg = jnp.broadcast_to(seg[:, None], (length + 2 * HALO, LANES))
    gain = norm_gain[None, :]
    swap = [(0, 1), (1, 0)]
    own = width // (ny * nx * 2)
    place = core[None]
    big = 2 * length * width * width
    vec = length * width * taps

    before = shifted(frames[length - HALO :], 1)
    after = shifted(frames[:HALO], -1)
    half = jax.ShapeDtypeStruct((width // 2, length), BF)
    mine, other = call(partial(split_kernel, own, nx), (half, half), smem=(0,), moved=4 * length * width)(place, cot)
    got = lax.ppermute(other, "core", swap)

    rows_win = length + 2 * HALO
    window = pltpu.VMEM((width // LANES, rows_win, LANES), F32)
    act, normed, inv = call(
        forward_kernel,
        (
            jax.ShapeDtypeStruct((length, width), BF),
            jax.ShapeDtypeStruct((length, width), F32),
            jax.ShapeDtypeStruct((length, LANES), F32),
        ),
        [window],
        flops=3 * vec,
        moved=8 * length * width,
        trans=2 * length * width,
    )(frames, before, after, seg, kernel, gain)
    act2 = lax.ppermute(act, "core", swap)
    weight = call(
        product_kernel,
        jax.ShapeDtypeStruct((width // 2, width), BF),
        flops=big,
        moved=2 * (width * width + 3 * length * width),
    )(mine, got, act, act2)
    landed = lax.all_to_all(weight.reshape(nx, ny * own, width), "x", split_axis=0, concat_axis=0, tiled=True)

    edge = jax.ShapeDtypeStruct((HALO, width), F32)
    conv_out, grad_mixed, first, last, gain_part = call(
        norm_kernel,
        (
            jax.ShapeDtypeStruct((length, width), BF),
            jax.ShapeDtypeStruct((length, width), F32),
            edge,
            edge,
            jax.ShapeDtypeStruct((8, width), F32),
        ),
        flops=2 * big,
        moved=16 * length * width,
        trans=2 * length * width,
    )(cot, projection, act, normed, inv, gain)
    gm_before = shifted(last, 1)
    gm_after = shifted(first, -1)
    dealt = jax.ShapeDtypeStruct((width // 2, LANES), F32)
    grad_hidden, small, small_other = call(
        partial(backward_kernel, own, nx),
        (jax.ShapeDtypeStruct((length, width), BF), dealt, dealt),
        [window, pltpu.VMEM((taps, 8, width), F32)],
        flops=5 * vec,
        moved=12 * length * width,
        smem=(0,),
    )(place, grad_mixed, gm_before, gm_after, seg, frames, kernel, gain_part)
    small = (small + lax.ppermute(small_other, "core", swap)).reshape(nx, ny, own, LANES)
    column = lax.axis_index("x")
    pieces = [lax.dynamic_index_in_dim(small, column ^ m, 0, keepdims=False) for m in range(nx)]
    for m in range(1, nx):
        pieces[m] = lax.ppermute(pieces[m], "x", [(i, i ^ m) for i in range(nx)])
    pieces = [piece.reshape(ny * own, LANES) for piece in pieces]

    weight = call(
        join_kernel,
        jax.ShapeDtypeStruct((ny * own, width + LANES), BF),
        moved=12 * ny * own * width,
    )(landed, *pieces).reshape(ny, own, width + LANES)
    landed = lax.all_to_all(weight, "y", split_axis=0, concat_axis=0, tiled=True)
    share = jnp.sum(landed.astype(F32), axis=0)
    factor = 1.0 / math.sqrt(length * ny * nx * 2 * lax.axis_size("dp"))
    grad_weight, grad_kernel, grad_gain = call(
        partial(final_kernel, factor, taps),
        (
            jax.ShapeDtypeStruct((own, width), F32),
            jax.ShapeDtypeStruct((own, taps), F32),
            jax.ShapeDtypeStruct((1, own), F32),
        ),
        moved=16 * own * width,
    )(*over_groups(share))
    return conv_out[None], grad_hidden[None], grad_weight, grad_kernel, grad_gain[0]


def solution(mesh):
    dp, seq = mesh.devices.shape
    fine = Mesh(mesh.devices.reshape(dp, 8, seq // 16, 2), ("dp",) + SEQ)
    rows = P("dp", SEQ, None)
    in_specs = (rows, P("dp", None), P(), P(), P(), rows)
    out_specs = (rows, rows, P(SEQ, None), P(SEQ, None), P(SEQ))
    return jax.shard_map(inner, mesh=fine, in_specs=in_specs, out_specs=out_specs, check_vma=False)
```

time: 357 us -> 138 us (0.39)
  the two profiles are of different devices: /device:TPU:89 before, /device:TPU:8 now
where the time goes in v1:
time: 138 us; the launch traced here: 137 us
  starting transfers between devices  64.6 us (47%)
  waiting for transfers between devices  24.3 us (18%)
  Pallas kernels  22.9 us (17%)
  blocking collectives  17.2 us (12%)
  local copies, waits for them, and re-layouts  6.96 us (5%)
    pallas_call x7, Pallas kernels, run(): pl.pallas_call(kernel, out_shape=outs, in_specs=specs, out_specs=jax.tree...  22.9 us
    all_to_all x1, blocking collectives, inner(): lax.all_to_all(weight, 'y', split_axis=0, concat_axis=0, tiled=True)  17.2 us
    ppermute x4, starting transfers between devices, shifted(): lax.ppermute(value, SEQ, [(i, i + steps) for i in range(first, last)])  16.4 us
    ppermute x2, starting transfers between devices, ahead(): lax.ppermute(value, 'dp', [(i, (i + by) % count) for i in range(count)])  13.8 us
    ppermute x3, starting transfers between devices, partner(): return lax.ppermute(value, 'dp', [(i, i ^ mask) for i in range(count)])  12.3 us
    ppermute x3, starting transfers between devices, inner(): pieces[m] = lax.ppermute(pieces[m], 'x', [(i, i ^ m) for i in range(nx)])  10.4 us
    ppermute x2, waiting for transfers between devices, ahead(): lax.ppermute(value, 'dp', [(i, (i + by) % count) for i in range(count)])  7.77 us
    ppermute x3, waiting for transfers between devices, partner(): return lax.ppermute(value, 'dp', [(i, i ^ mask) for i in range(count)])  6.11 us
  transfers between devices with their start and end apart: 16, of which 10 were waited for; matrix products, arithmetic and copies ran while one was open for 1% of the time, Pallas kernels for 10%

profile of v1, /device:TPU:8, one launch (start us, length us, event | category | flops | bytes accessed | tf_op | source)
XLA Modules:
  0.0 136.9 jit_solution(16078738101098800653)
XLA Ops:
  0.6 0.8 slice_bitcast_fusion
  1.4 1.9 %collective-permute-start = (bf16[16,1024]{1,0:T(8,128)(2,1)S(1)}, bf16[16,1024]{1,0:T(8,128)(2,1)S(1)}, u32[]{:S(2)}, u32[]{:S(2)}) collective-permute-start(bf16[16,1024]{1,0:T(8,128)(2,1)S(1)} %get-tuple-element.38), channel_id=1, source_target_pairs={{0,1},{1,2},{2,3},{3,4},{4,5},{5,6},{6,7},{7,8},{8,9},{9,10},{10,1... | collective-permute-start | bytes 98312 | tf_op jit(solution)/shard_map/ppermute | solution.py:239
  3.3 5.8 %collective-permute-start.1 = (bf16[16,1024]{1,0:T(8,128)(2,1)S(1)}, bf16[16,1024]{1,0:T(8,128)(2,1)S(1)}, u32[]{:S(2)}, u32[]{:S(2)}) collective-permute-start(bf16[16,1024]{1,0:T(8,128)(2,1)S(1)} %get-tuple-element.37), channel_id=1, source_target_pairs={{1,0},{2,1},{3,2},{4,3},{5,4},{6,5},{7,6},{8,7},{9,8},{10,9},{11,1... | collective-permute-start | bytes 98312 | tf_op jit(solution)/shard_map/ppermute | solution.py:239
  9.1 0.8 pad_dynamic-slice_fusion
  9.9 0.0 collective-permute-done.bef_ref
  9.9 0.8 collective-permute-done.1.aft_ref
  10.7 0.1 broadcast_in_dim.18.seg_ref
  10.8 0.0 copy-start.3
  10.8 1.0 copy-done.3
  11.8 0.9 copy-done.5
  12.7 0.7 copy-done.7
  13.4 6.4 %shard_map.101 = (bf16[256,1024]{1,0:T(8,128)(2,1)S(1)}, f32[256,1024]{1,0:T(8,128)S(1)}, f32[256,128]{1,0:T(8,128)S(1)}) custom-call(bf16[256,1024]{1,0:T(8,128)(2,1)S(1)} %bitcast.28, bf16[16,1024]{1,0:T(8,128)(2,1)S(1)} %collective-permute-done.bef_ref, bf16[16,1024]{1,0:T(8,128)(2,1)S(1)} %collective-permute-done.1.aft_ref, ...), custom_call_target="tpu_custom_call" | custom-call | flops 24379392 | bytes 2097152 | tf_op jit(solution)/shard_map/pallas_call | solution.py:27
  19.9 1.9 %collective-permute-start.5 = (bf16[256,1024]{1,0:T(8,128)(2,1)S(1)}, bf16[256,1024]{1,0:T(8,128)(2,1)S(1)}, u32[]{:S(2)}, u32[]{:S(2)}) collective-permute-start(bf16[256,1024]{1,0:T(8,128)(2,1)S(1)} %get-tuple-element.21.act_ref), channel_id=1, source_target_pairs={{0,1},{1,0},{2,3},{3,2},{4,5},{5,4},{6,7},{7,6},{8,9},{9,8},{10,11... | collective-permute-start | bytes 1572872 | tf_op jit(solution)/shard_map/ppermute | solution.py:295
  21.8 0.0 copy-start.1
  21.8 1.0 copy-done.1
  22.8 0.2 shard_map.104
  23.0 2.4 %collective-permute-start.4 = (bf16[512,256]{1,0:T(8,128)(2,1)S(1)}, bf16[512,256]{1,0:T(8,128)(2,1)S(1)}, u32[]{:S(2)}, u32[]{:S(2)}) collective-permute-start(bf16[512,256]{1,0:T(8,128)(2,1)S(1)} %get-tuple-element.31), channel_id=1, source_target_pairs={{0,1},{1,0},{2,3},{3,2},{4,5},{5,4},{6,7},{7,6},{8,9},{9,8},{10,11... | collective-permute-start | bytes 786440 | tf_op jit(solution)/shard_map/ppermute | solution.py:279
  25.4 1.1 collective-permute-done.4.got_ref
  26.6 0.0 collective-permute-done.5.act2_ref
  26.6 2.3 %shard_map.105 = bf16[512,1024]{1,0:T(8,128)(2,1)} custom-call(bf16[512,256]{1,0:T(8,128)(2,1)S(1)} %get-tuple-element.30.mine_ref, bf16[512,256]{1,0:T(8,128)(2,1)S(1)} %collective-permute-done.4.got_ref, bf16[256,1024]{1,0:T(8,128)(2,1)S(1)} %get-tuple-element.21.act_ref, bf16[256,1024]{1,0:T(8,128)(2,1)S(1)} %collective-permute-done.5.act2_ref), custom_call_target="tpu_custom_call" | custom-call | flops 536870912 | bytes 3670016 | tf_op jit(solution)/shard_map/pallas_call | solution.py:27
  28.9 5.5 %all-to-all-start = ((bf16[4,128,1024]{2,1,0:T(8,128)(2,1)}), bf16[4,128,1024]{2,1,0:T(8,128)(2,1)S(1)}, u32[]{:S(2)}, u32[]{:S(2)}) async-start(bf16[4,128,1024]{2,1,0:T(8,128)(2,1)} %bitcast.9), calls=%async_computation | async-start | bytes 2097152 | tf_op jit(solution)/shard_map/all_to_all | solution.py:302
  34.4 1.6 %copy-done = bf16[1024,1024]{1,0:T(8,128)(2,1)S(1)} copy-done((bf16[1024,1024]{1,0:T(8,128)(2,1)S(1)}, bf16[1024,1024]{1,0:T(8,128)(2,1)}, u32[]{:S(2)}) %copy-start) | copy-done | bytes 2097176
  36.0 6.5 %shard_map.102 = (bf16[256,1024]{1,0:T(8,128)(2,1)}, f32[256,1024]{1,0:T(8,128)S(1)}, f32[16,1024]{1,0:T(8,128)S(1)}, f32[16,1024]{1,0:T(8,128)S(1)}, f32[8,1024]{1,0:T(8,128)S(1)}) custom-call(bf16[256,1024]{1,0:T(8,128)(2,1)S(1)} %bitcast.26, bf16[1024,1024]{1,0:T(8,128)(2,1)S(1)} %copy-done, bf16[256,1024]{1,0:T(8,128)(2,1)S(1)} %get-tuple-element.21.act_ref, ...), custom_call_target="tpu_custom_call" | custom-call | flops 1073741824 | bytes 4194304 | tf_op jit(solution)/shard_map/pallas_call | solution.py:27
  42.5 1.9 %collective-permute-start.2 = (f32[16,1024]{1,0:T(8,128)S(1)}, f32[16,1024]{1,0:T(8,128)S(1)}, u32[]{:S(2)}, u32[]{:S(2)}) collective-permute-start(f32[16,1024]{1,0:T(8,128)S(1)} %get-tuple-element.26), channel_id=1, source_target_pairs={{0,1},{1,2},{2,3},{3,4},{4,5},{5,6},{6,7},{7,8},{8,9},{9,10},{10,1... | collective-permute-start | bytes 196616 | tf_op jit(solution)/shard_map/ppermute | solution.py:239
  44.4 6.8 %collective-permute-start.3 = (f32[16,1024]{1,0:T(8,128)S(1)}, f32[16,1024]{1,0:T(8,128)S(1)}, u32[]{:S(2)}, u32[]{:S(2)}) collective-permute-start(f32[16,1024]{1,0:T(8,128)S(1)} %get-tuple-element.27), channel_id=1, source_target_pairs={{1,0},{2,1},{3,2},{4,3},{5,4},{6,5},{7,6},{8,7},{9,8},{10,9},{11,1... | collective-permute-start | bytes 196616 | tf_op jit(solution)/shard_map/ppermute | solution.py:239
  51.2 0.0 collective-permute-done.2.bef_ref
  51.2 1.9 %collective-permute-done.3.aft_ref = f32[16,1024]{1,0:T(8,128)S(1)} collective-permute-done((f32[16,1024]{1,0:T(8,128)S(1)}, f32[16,1024]{1,0:T(8,128)S(1)}, u32[]{:S(2)}, u32[]{:S(2)}) %collective-permute-start.3) | collective-permute-done | bytes 65568 | tf_op jit(solution)/shard_map/ppermute | solution.py:239
  53.1 6.7 %shard_map.103 = (bf16[256,1024]{1,0:T(8,128)(2,1)}, f32[512,128]{1,0:T(8,128)S(1)}, f32[512,128]{1,0:T(8,128)S(1)}) custom-call(s32[1]{0:T(128)} %bitcast.7.core_ref, f32[256,1024]{1,0:T(8,128)S(1)} %get-tuple-element.25.gm_ref, f32[16,1024]{1,0:T(8,128)S(1)} %collective-permute-done.2.bef_ref, f32[16,1024]{1,0:T(8,128)S(1)} %collective-permute-done.3.aft_ref, ...), custom_call_target="tpu_custom_call" | custom-call | flops 40632320 | bytes 3145728 | tf_op jit(solution)/shard_map/pallas_call | solution.py:27
  59.8 1.9 %collective-permute-start.6 = (f32[512,128]{1,0:T(8,128)S(1)}, f32[512,128]{1,0:T(8,128)S(1)}, u32[]{:S(2)}, u32[]{:S(2)}) collective-permute-start(f32[512,128]{1,0:T(8,128)S(1)} %get-tuple-element.33), channel_id=1, source_target_pairs={{0,1},{1,0},{2,3},{3,2},{4,5},{5,4},{6,7},{7,6},{8,9},{9,8},{10,11... | collective-permute-start | bytes 786440 | tf_op jit(solution)/shard_map/ppermute | solution.py:329
  61.7 1.5 %collective-permute-done.6 = f32[512,128]{1,0:T(8,128)S(1)} collective-permute-done((f32[512,128]{1,0:T(8,128)S(1)}, f32[512,128]{1,0:T(8,128)S(1)}, u32[]{:S(2)}, u32[]{:S(2)}) %collective-permute-start.6) | collective-permute-done | bytes 262176 | tf_op jit(solution)/shard_map/ppermute | solution.py:329
  63.2 2.0 %collective-permute-start.7 = (f32[8,16,128]{2,1,0:T(8,128)S(1)}, f32[8,16,128]{2,1,0:T(8,128)S(1)}, u32[]{:S(2)}, u32[]{:S(2)}) collective-permute-start(f32[8,16,128]{2,1,0:T(8,128)S(1)} %get-tuple-element.41), channel_id=1, source_target_pairs={{0,2},{2,0},{4,6},{6,4},{1,3},{3,1},{5,7},{7,5},{8,10},{10,8},{12,... | collective-permute-start | bytes 196616 | tf_op jit(solution)/shard_map/ppermute | solution.py:333
  65.3 6.2 %collective-permute-start.8 = (f32[8,16,128]{2,1,0:T(8,128)S(1)}, f32[8,16,128]{2,1,0:T(8,128)S(1)}, u32[]{:S(2)}, u32[]{:S(2)}) collective-permute-start(f32[8,16,128]{2,1,0:T(8,128)S(1)} %get-tuple-element.40), channel_id=1, source_target_pairs={{0,4},{2,6},{4,0},{6,2},{1,5},{3,7},{5,1},{7,3},{8,12},{10,14},{12... | collective-permute-start | bytes 196616 | tf_op jit(solution)/shard_map/ppermute | solution.py:333
  71.5 2.2 %collective-permute-start.9 = (f32[8,16,128]{2,1,0:T(8,128)S(1)}, f32[8,16,128]{2,1,0:T(8,128)S(1)}, u32[]{:S(2)}, u32[]{:S(2)}) collective-permute-start(f32[8,16,128]{2,1,0:T(8,128)S(1)} %get-tuple-element.39), channel_id=1, source_target_pairs={{0,6},{2,4},{4,2},{6,0},{1,7},{3,5},{5,3},{7,1},{8,14},{10,12},{12... | collective-permute-start | bytes 196616 | tf_op jit(solution)/shard_map/ppermute | solution.py:333
  73.7 0.0 collective-permute-done.7
  73.7 0.1 collective-permute-done.8
  73.8 5.0 %collective-permute-done.9 = f32[8,16,128]{2,1,0:T(8,128)S(1)} collective-permute-done((f32[8,16,128]{2,1,0:T(8,128)S(1)}, f32[8,16,128]{2,1,0:T(8,128)S(1)}, u32[]{:S(2)}, u32[]{:S(2)}) %collective-permute-start.9) | collective-permute-done | bytes 65568 | tf_op jit(solution)/shard_map/ppermute | solution.py:333
  78.9 0.2 shard_map.106
  79.0 17.2 %all_to_all.10 = bf16[8,16,1152]{2,1,0:T(8,128)(2,1)S(1)} all-to-all(bf16[8,16,1152]{2,1,0:T(8,128)(2,1)S(1)} %bitcast.27), channel_id=1, replica_groups=mesh['dp'=12,'y'=8,'x'=4,'core'=2] {'y'}, dimensions={0} | all-to-all | bytes 589824 | tf_op jit(solution)/shard_map/all_to_all | solution.py:341
  96.2 4.3 %collective-permute-start.10 = (f32[16,1152]{1,0:T(8,128)S(1)}, f32[16,1152]{1,0:T(8,128)S(1)}, u32[]{:S(2)}, u32[]{:S(2)}) collective-permute-start(f32[16,1152]{1,0:T(8,128)S(1)} %convert_reduce_fusion), channel_id=1, source_target_pairs={{0,64},{64,0},{128,192},{192,128},{256,320},{320,256},{384,448},{4... | collective-permute-start | bytes 221192 | tf_op jit(solution)/shard_map/ppermute | solution.py:246
  100.5 6.1 %collective-permute-start.11 = (f32[16,1152]{1,0:T(8,128)S(1)}, f32[16,1152]{1,0:T(8,128)S(1)}, u32[]{:S(2)}, u32[]{:S(2)}) collective-permute-start(f32[16,1152]{1,0:T(8,128)S(1)} %convert_reduce_fusion), channel_id=1, source_target_pairs={{0,128},{64,192},{128,0},{192,64},{256,384},{320,448},{384,256},{4... | collective-permute-start | bytes 221192 | tf_op jit(solution)/shard_map/ppermute | solution.py:246
  106.6 1.9 %collective-permute-start.12 = (f32[16,1152]{1,0:T(8,128)S(1)}, f32[16,1152]{1,0:T(8,128)S(1)}, u32[]{:S(2)}, u32[]{:S(2)}) collective-permute-start(f32[16,1152]{1,0:T(8,128)S(1)} %convert_reduce_fusion), channel_id=1, source_target_pairs={{0,192},{64,128},{128,64},{192,0},{256,448},{320,384},{384,320},{4... | collective-permute-start | bytes 221192 | tf_op jit(solution)/shard_map/ppermute | solution.py:246
  108.6 1.6 %collective-permute-done.11 = f32[16,1152]{1,0:T(8,128)S(1)} collective-permute-done((f32[16,1152]{1,0:T(8,128)S(1)}, f32[16,1152]{1,0:T(8,128)S(1)}, u32[]{:S(2)}, u32[]{:S(2)}) %collective-permute-start.11) | collective-permute-done | bytes 73760 | tf_op jit(solution)/shard_map/ppermute | solution.py:246
  110.1 4.5 %collective-permute-done.12 = f32[16,1152]{1,0:T(8,128)S(1)} collective-permute-done((f32[16,1152]{1,0:T(8,128)S(1)}, f32[16,1152]{1,0:T(8,128)S(1)}, u32[]{:S(2)}, u32[]{:S(2)}) %collective-permute-start.12) | collective-permute-done | bytes 73760 | tf_op jit(solution)/shard_map/ppermute | solution.py:246
  114.7 10.6 %collective-permute-start.13 = (f32[16,1152]{1,0:T(8,128)S(1)}, f32[16,1152]{1,0:T(8,128)S(1)}, u32[]{:S(2)}, u32[]{:S(2)}) collective-permute-start(f32[16,1152]{1,0:T(8,128)S(1)} %add_add_fusion.a_ref), channel_id=1, source_target_pairs={{0,256},{64,320},{128,384},{192,448},{256,512},{320,576},{384,640}... | collective-permute-start | bytes 221192 | tf_op jit(solution)/shard_map/ppermute | solution.py:252
  125.3 3.2 %collective-permute-start.14 = (f32[16,1152]{1,0:T(8,128)S(1)}, f32[16,1152]{1,0:T(8,128)S(1)}, u32[]{:S(2)}, u32[]{:S(2)}) collective-permute-start(f32[16,1152]{1,0:T(8,128)S(1)} %add_add_fusion.a_ref), channel_id=1, source_target_pairs={{0,512},{64,576},{128,640},{192,704},{256,0},{320,64},{384,128},{4... | collective-permute-start | bytes 221192 | tf_op jit(solution)/shard_map/ppermute | solution.py:252
  128.5 0.4 collective-permute-done.13.b_ref
  128.9 7.4 %collective-permute-done.14.c_ref = f32[16,1152]{1,0:T(8,128)S(1)} collective-permute-done((f32[16,1152]{1,0:T(8,128)S(1)}, f32[16,1152]{1,0:T(8,128)S(1)}, u32[]{:S(2)}, u32[]{:S(2)}) %collective-permute-start.14) | collective-permute-done | bytes 73760 | tf_op jit(solution)/shard_map/ppermute | solution.py:252
  136.3 0.7 shard_map.107
  (17 shorter events, 0.1 us)
Async XLA Ops:
  1.4 8.5 %collective-permute-start = (bf16[16,1024]{1,0:T(8,128)(2,1)S(1)}, bf16[16,1024]{1,0:T(8,128)(2,1)S(1)}, u32[]{:S(2)}, u32[]{:S(2)}) collective-permute-start(bf16[16,1024]{1,0:T(8,128)(2,1)S(1)} %get-tuple-element.38), channel_id=1, source_target_pairs={{0,1},{1,2},{2,3},{3,4},{4,5},{5,6},{6,7},{7,8},{8,9},{9,10},{10,1... | collective-permute-start | bytes 98312 | tf_op jit(solution)/shard_map/ppermute | solution.py:239
  3.3 7.3 %collective-permute-start.1 = (bf16[16,1024]{1,0:T(8,128)(2,1)S(1)}, bf16[16,1024]{1,0:T(8,128)(2,1)S(1)}, u32[]{:S(2)}, u32[]{:S(2)}) collective-permute-start(bf16[16,1024]{1,0:T(8,128)(2,1)S(1)} %get-tuple-element.37), channel_id=1, source_target_pairs={{1,0},{2,1},{3,2},{4,3},{5,4},{6,5},{7,6},{8,7},{9,8},{10,9},{11,1... | collective-permute-start | bytes 98312 | tf_op jit(solution)/shard_map/ppermute | solution.py:239
  10.8 1.0 copy-start.3
  11.8 0.9 copy-start.5
  12.7 0.7 copy-start.7
  19.9 6.7 %collective-permute-start.5 = (bf16[256,1024]{1,0:T(8,128)(2,1)S(1)}, bf16[256,1024]{1,0:T(8,128)(2,1)S(1)}, u32[]{:S(2)}, u32[]{:S(2)}) collective-permute-start(bf16[256,1024]{1,0:T(8,128)(2,1)S(1)} %get-tuple-element.21.act_ref), channel_id=1, source_target_pairs={{0,1},{1,0},{2,3},{3,2},{4,5},{5,4},{6,7},{7,6},{8,9},{9,8},{10,11... | collective-permute-start | bytes 1572872 | tf_op jit(solution)/shard_map/ppermute | solution.py:295
  21.8 1.0 copy-start.1
  23.0 3.6 %collective-permute-start.4 = (bf16[512,256]{1,0:T(8,128)(2,1)S(1)}, bf16[512,256]{1,0:T(8,128)(2,1)S(1)}, u32[]{:S(2)}, u32[]{:S(2)}) collective-permute-start(bf16[512,256]{1,0:T(8,128)(2,1)S(1)} %get-tuple-element.31), channel_id=1, source_target_pairs={{0,1},{1,0},{2,3},{3,2},{4,5},{5,4},{6,7},{7,6},{8,9},{9,8},{10,11... | collective-permute-start | bytes 786440 | tf_op jit(solution)/shard_map/ppermute | solution.py:279
  26.6 7.8 %copy-start.2 = (bf16[1,256,1024]{2,1,0:T(8,128)(2,1)S(1)}, bf16[1,256,1024]{2,1,0:T(8,128)(2,1)}, u32[]{:S(2)}) copy-start(bf16[1,256,1024]{2,1,0:T(8,128)(2,1)} %param.11) | copy-start | bytes 1572868
  26.6 7.8 %copy-start.8 = (f32[1024]{0:T(1024)S(1)}, f32[1024]{0:T(1024)}, u32[]{:S(2)}) copy-start(f32[1024]{0:T(1024)} %param.9) | copy-start | bytes 12292
  28.9 50.0 %all-to-all-start = ((bf16[4,128,1024]{2,1,0:T(8,128)(2,1)}), bf16[4,128,1024]{2,1,0:T(8,128)(2,1)S(1)}, u32[]{:S(2)}, u32[]{:S(2)}) async-start(bf16[4,128,1024]{2,1,0:T(8,128)(2,1)} %bitcast.9), calls=%async_computation | async-start | bytes 2097152 | tf_op jit(solution)/shard_map/all_to_all | solution.py:302
  34.4 1.6 %copy-start = (bf16[1024,1024]{1,0:T(8,128)(2,1)S(1)}, bf16[1024,1024]{1,0:T(8,128)(2,1)}, u32[]{:S(2)}) copy-start(bf16[1024,1024]{1,0:T(8,128)(2,1)} %proj_ref.1) | copy-start | bytes 6291460
  36.0 17.1 %copy-start.4 = (bf16[1,256,1024]{2,1,0:T(8,128)(2,1)S(1)}, bf16[1,256,1024]{2,1,0:T(8,128)(2,1)}, u32[]{:S(2)}) copy-start(bf16[1,256,1024]{2,1,0:T(8,128)(2,1)} %param.6) | copy-start | bytes 1572868
  36.0 17.1 %copy-start.6 = (f32[31,1024]{1,0:T(8,128)S(1)}, f32[31,1024]{1,0:T(8,128)}, u32[]{:S(2)}) copy-start(f32[31,1024]{1,0:T(8,128)} %kern_ref.3) | copy-start | bytes 380932
  42.5 8.7 %collective-permute-start.2 = (f32[16,1024]{1,0:T(8,128)S(1)}, f32[16,1024]{1,0:T(8,128)S(1)}, u32[]{:S(2)}, u32[]{:S(2)}) collective-permute-start(f32[16,1024]{1,0:T(8,128)S(1)} %get-tuple-element.26), channel_id=1, source_target_pairs={{0,1},{1,2},{2,3},{3,4},{4,5},{5,6},{6,7},{7,8},{8,9},{9,10},{10,1... | collective-permute-start | bytes 196616 | tf_op jit(solution)/shard_map/ppermute | solution.py:239
  44.4 8.7 %collective-permute-start.3 = (f32[16,1024]{1,0:T(8,128)S(1)}, f32[16,1024]{1,0:T(8,128)S(1)}, u32[]{:S(2)}, u32[]{:S(2)}) collective-permute-start(f32[16,1024]{1,0:T(8,128)S(1)} %get-tuple-element.27), channel_id=1, source_target_pairs={{1,0},{2,1},{3,2},{4,3},{5,4},{6,5},{7,6},{8,7},{9,8},{10,9},{11,1... | collective-permute-start | bytes 196616 | tf_op jit(solution)/shard_map/ppermute | solution.py:239
  59.8 3.4 %collective-permute-start.6 = (f32[512,128]{1,0:T(8,128)S(1)}, f32[512,128]{1,0:T(8,128)S(1)}, u32[]{:S(2)}, u32[]{:S(2)}) collective-permute-start(f32[512,128]{1,0:T(8,128)S(1)} %get-tuple-element.33), channel_id=1, source_target_pairs={{0,1},{1,0},{2,3},{3,2},{4,5},{5,4},{6,7},{7,6},{8,9},{9,8},{10,11... | collective-permute-start | bytes 786440 | tf_op jit(solution)/shard_map/ppermute | solution.py:329
  63.2 10.4 %collective-permute-start.7 = (f32[8,16,128]{2,1,0:T(8,128)S(1)}, f32[8,16,128]{2,1,0:T(8,128)S(1)}, u32[]{:S(2)}, u32[]{:S(2)}) collective-permute-start(f32[8,16,128]{2,1,0:T(8,128)S(1)} %get-tuple-element.41), channel_id=1, source_target_pairs={{0,2},{2,0},{4,6},{6,4},{1,3},{3,1},{5,7},{7,5},{8,10},{10,8},{12,... | collective-permute-start | bytes 196616 | tf_op jit(solution)/shard_map/ppermute | solution.py:333
  65.3 8.6 %collective-permute-start.8 = (f32[8,16,128]{2,1,0:T(8,128)S(1)}, f32[8,16,128]{2,1,0:T(8,128)S(1)}, u32[]{:S(2)}, u32[]{:S(2)}) collective-permute-start(f32[8,16,128]{2,1,0:T(8,128)S(1)} %get-tuple-element.40), channel_id=1, source_target_pairs={{0,4},{2,6},{4,0},{6,2},{1,5},{3,7},{5,1},{7,3},{8,12},{10,14},{12... | collective-permute-start | bytes 196616 | tf_op jit(solution)/shard_map/ppermute | solution.py:333
  71.5 7.4 %collective-permute-start.9 = (f32[8,16,128]{2,1,0:T(8,128)S(1)}, f32[8,16,128]{2,1,0:T(8,128)S(1)}, u32[]{:S(2)}, u32[]{:S(2)}) collective-permute-start(f32[8,16,128]{2,1,0:T(8,128)S(1)} %get-tuple-element.39), channel_id=1, source_target_pairs={{0,6},{2,4},{4,2},{6,0},{1,7},{3,5},{5,3},{7,1},{8,14},{10,12},{12... | collective-permute-start | bytes 196616 | tf_op jit(solution)/shard_map/ppermute | solution.py:333
  96.2 12.3 %collective-permute-start.10 = (f32[16,1152]{1,0:T(8,128)S(1)}, f32[16,1152]{1,0:T(8,128)S(1)}, u32[]{:S(2)}, u32[]{:S(2)}) collective-permute-start(f32[16,1152]{1,0:T(8,128)S(1)} %convert_reduce_fusion), channel_id=1, source_target_pairs={{0,64},{64,0},{128,192},{192,128},{256,320},{320,256},{384,448},{4... | collective-permute-start | bytes 221192 | tf_op jit(solution)/shard_map/ppermute | solution.py:246
  100.5 9.6 %collective-permute-start.11 = (f32[16,1152]{1,0:T(8,128)S(1)}, f32[16,1152]{1,0:T(8,128)S(1)}, u32[]{:S(2)}, u32[]{:S(2)}) collective-permute-start(f32[16,1152]{1,0:T(8,128)S(1)} %convert_reduce_fusion), channel_id=1, source_target_pairs={{0,128},{64,192},{128,0},{192,64},{256,384},{320,448},{384,256},{4... | collective-permute-start | bytes 221192 | tf_op jit(solution)/shard_map/ppermute | solution.py:246
  106.6 8.0 %collective-permute-start.12 = (f32[16,1152]{1,0:T(8,128)S(1)}, f32[16,1152]{1,0:T(8,128)S(1)}, u32[]{:S(2)}, u32[]{:S(2)}) collective-permute-start(f32[16,1152]{1,0:T(8,128)S(1)} %convert_reduce_fusion), channel_id=1, source_target_pairs={{0,192},{64,128},{128,64},{192,0},{256,448},{320,384},{384,320},{4... | collective-permute-start | bytes 221192 | tf_op jit(solution)/shard_map/ppermute | solution.py:246
  114.7 14.2 %collective-permute-start.13 = (f32[16,1152]{1,0:T(8,128)S(1)}, f32[16,1152]{1,0:T(8,128)S(1)}, u32[]{:S(2)}, u32[]{:S(2)}) collective-permute-start(f32[16,1152]{1,0:T(8,128)S(1)} %add_add_fusion.a_ref), channel_id=1, source_target_pairs={{0,256},{64,320},{128,384},{192,448},{256,512},{320,576},{384,640}... | collective-permute-start | bytes 221192 | tf_op jit(solution)/shard_map/ppermute | solution.py:252
  125.3 11.0 %collective-permute-start.14 = (f32[16,1152]{1,0:T(8,128)S(1)}, f32[16,1152]{1,0:T(8,128)S(1)}, u32[]{:S(2)}, u32[]{:S(2)}) collective-permute-start(f32[16,1152]{1,0:T(8,128)S(1)} %add_add_fusion.a_ref), channel_id=1, source_target_pairs={{0,512},{64,576},{128,640},{192,704},{256,0},{320,64},{384,128},{4... | collective-permute-start | bytes 221192 | tf_op jit(solution)/shard_map/ppermute | solution.py:252

commit v2 on v1

v2 whole, which is shorter than its diff:
```python
import math
from functools import partial

import jax
import jax.numpy as jnp
from jax import lax
from jax.experimental import pallas as pl
from jax.experimental.pallas import tpu as pltpu
from jax.sharding import Mesh
from jax.sharding import PartitionSpec as P


EPS = 1e-05
LANES = 128
HALO = 16
ROWS = 32
BF = jnp.bfloat16
F32 = jnp.float32


def call(kernel, outs, scratch=(), flops=0, moved=0, trans=0, hbm=(), far=0, limit=9):
    def run(*args):
        specs = [
            pl.BlockSpec(memory_space=pltpu.HBM if i in hbm else pltpu.VMEM)
            for i in range(len(args))
        ]
        args = [
            pltpu.with_memory_space_constraint(arg, pltpu.HBM) if i in hbm else arg
            for i, arg in enumerate(args)
        ]
        return pl.pallas_call(
            kernel,
            out_shape=outs,
            in_specs=specs,
            out_specs=jax.tree.unflatten(
                jax.tree.structure(outs),
                [
                    pl.BlockSpec(memory_space=pltpu.HBM if i < far else pltpu.VMEM)
                    for i in range(len(jax.tree.leaves(outs)))
                ],
            ),
            scratch_shapes=list(scratch),
            compiler_params=pltpu.CompilerParams(vmem_limit_bytes=limit * 1024 * 1024),
            cost_estimate=pl.CostEstimate(flops=flops, bytes_accessed=moved, transcendentals=trans),
        )(*args)

    return run


def deal(core, b, turned, own, mine_ref, other_ref):
    pairs = LANES // (2 * own)
    for j in range(pairs):
        even = turned[2 * own * j : 2 * own * j + own]
        odd = turned[2 * own * j + own : 2 * own * j + 2 * own]
        at = (b * pairs + j) * own
        mine_ref[at : at + own, :] = jnp.where(core == 0, even, odd)
        other_ref[at : at + own, :] = jnp.where(core == 0, odd, even)


def place_of(axes):
    index = lax.axis_index(axes[0])
    for axis in axes[1:]:
        index = index * lax.axis_size(axis) + lax.axis_index(axis)
    return index


def first_kernel(
    own, ids_hbm, cot_hbm, hid_hbm, proj_hbm, kern_hbm, gain_hbm,
    mine_ref, other_ref, seg_ref, mid_ref, ga_ref, proj_ref, kern_ref, gain_ref,
    ids_ref, cot_ref, hid_ref, sems,
):
    pairs = (
        (cot_hbm, cot_ref), (ids_hbm, ids_ref), (hid_hbm, hid_ref),
        (kern_hbm, kern_ref), (gain_hbm, gain_ref), (proj_hbm, proj_ref),
    )
    copies = [pltpu.make_async_copy(src, dst, sems.at[i]) for i, (src, dst) in enumerate(pairs)]
    for copy in copies:
        copy.start()
    copies[0].wait()
    core = lax.axis_index("core")
    length, width = cot_ref.shape
    for b in range(width // LANES):
        turned = cot_ref[:, b * LANES : (b + 1) * LANES].T
        deal(core, b, turned, own, mine_ref, other_ref)
    copies[1].wait()
    index = place_of(SEQ)
    lines = length // LANES
    last = ids_ref.shape[0] - 1

    def column(line, outside):
        row = ids_ref[pl.ds(jnp.clip(line, 0, last), 1), :].astype(F32)
        square = jnp.broadcast_to(row, (LANES, LANES)).T
        return jnp.where(outside, -1.0, square)

    head = column(lines * index - 1, index == 0)
    seg_ref[0:HALO, :] = head[LANES - HALO :]
    for j in range(lines):
        seg_ref[HALO + j * LANES : HALO + (j + 1) * LANES, :] = column(lines * index + j, False)
    tail = column(lines * index + lines, lines * index + lines > last)
    seg_ref[HALO + length : 2 * HALO + length, :] = tail[:HALO]
    copies[2].wait()
    for b in range(width // LANES):
        mid_ref[b] = hid_ref[:, b * LANES : (b + 1) * LANES].astype(F32)
    for copy in copies[3:]:
        copy.wait()
    part = 64

    def step(i, carry):
        at = pl.ds(pl.multiple_of(i * part, part), part)
        ga_ref[at, :] = jnp.dot(cot_ref[at, :], proj_ref[...], preferred_element_type=F32)
        return carry

    lax.fori_loop(0, length // part, step, 0)


def edges_in(dst, before, after):
    blocks, rows = dst.shape[0], dst.shape[1]
    for b in range(blocks):
        lanes = slice(b * LANES, (b + 1) * LANES)
        dst[b, 0:HALO, :] = before[:, lanes].astype(F32)
        dst[b, rows - HALO : rows, :] = after[:, lanes].astype(F32)


def forward_kernel(mid_ref, bef_ref, aft_ref, seg_ref, kern_ref, gain_ref, act_ref, norm_ref, inv_ref, win):
    taps, width = kern_ref.shape
    length = act_ref.shape[0]
    blocks = width // LANES
    edges_in(win, bef_ref, aft_ref)
    for b in range(blocks):
        win[b, HALO : HALO + length, :] = mid_ref[b]

    def step(i, carry):
        r0 = pl.multiple_of(i * ROWS, ROWS)
        centre = seg_ref[pl.ds(r0 + HALO, ROWS), :]
        acc = [jnp.zeros((ROWS, LANES), F32) for _ in range(blocks)]
        for k in range(taps):
            same = seg_ref[pl.ds(r0 + k + 1, ROWS), :] == centre
            for b in range(blocks):
                w = kern_ref[k : k + 1, b * LANES : (b + 1) * LANES]
                term = win[b, pl.ds(r0 + k + 1, ROWS), :] * w
                acc[b] = acc[b] + jnp.where(same, term, 0.0)
        total = acc[0]
        for b in range(1, blocks):
            total = total + acc[b]
        mean = jnp.sum(total, axis=1, keepdims=True) * (1.0 / width)
        acc = [a - mean for a in acc]
        total = acc[0] * acc[0]
        for b in range(1, blocks):
            total = total + acc[b] * acc[b]
        inv = lax.rsqrt(jnp.sum(total, axis=1, keepdims=True) * (1.0 / width) + EPS)
        inv_ref[pl.ds(r0, ROWS), :] = jnp.broadcast_to(inv, (ROWS, LANES))
        for b in range(blocks):
            lanes = slice(b * LANES, (b + 1) * LANES)
            normed = acc[b] * inv
            norm_ref[pl.ds(r0, ROWS), lanes] = normed
            gated = normed * gain_ref[:, lanes]
            act_ref[pl.ds(r0, ROWS), lanes] = (gated * jax.nn.sigmoid(gated)).astype(BF)
        return carry

    lax.fori_loop(0, length // ROWS, step, 0)


def product_kernel(mine_ref, got_ref, act_ref, act2_ref, small_ref, small2_ref, out_ref):
    rows = mine_ref.shape[0]
    width = act_ref.shape[1]
    part = 128

    def step(i, carry):
        at = pl.ds(pl.multiple_of(i * part, part), part)
        total = jnp.dot(mine_ref[at, :], act_ref[...], preferred_element_type=F32)
        total = total + jnp.dot(got_ref[at, :], act2_ref[...], preferred_element_type=F32)
        out_ref[at, :width] = total.astype(BF)
        out_ref[at, width:] = (small_ref[at, :] + small2_ref[at, :]).astype(BF)
        return carry

    lax.fori_loop(0, rows // part, step, 0)


def taps_kernel(
    own, ga_ref, norm_ref, inv_ref, gain_ref, seg_ref, win,
    gm_hbm, first_hbm, last_hbm, mine_ref, other_ref, kacc, gg_ref, gm_ref, sems,
):
    length, width = norm_ref.shape
    taps = kacc.shape[0]
    blocks = width // LANES
    group = 4
    gg_ref[...] = jnp.zeros(gg_ref.shape, F32)
    kacc[...] = jnp.zeros(kacc.shape, F32)

    def rows_of(value):
        rows8 = value[0:8]
        for r in range(8, ROWS, 8):
            rows8 = rows8 + value[r : r + 8]
        return rows8

    def step(i, carry):
        r0 = pl.multiple_of(i * ROWS, ROWS)
        at = pl.ds(r0, ROWS)
        sum_a = jnp.zeros((ROWS, LANES), F32)
        sum_b = jnp.zeros((ROWS, LANES), F32)
        for b in range(blocks):
            lanes = slice(b * LANES, (b + 1) * LANES)
            gain = gain_ref[:, lanes]
            normed = norm_ref[at, lanes]
            gated = normed * gain
            sigma = jax.nn.sigmoid(gated)
            gg = ga_ref[at, lanes] * sigma * (1.0 + gated * (1.0 - sigma))
            gg_ref[:, lanes] = gg_ref[:, lanes] + rows_of(gg * normed)
            gn = gg * gain
            sum_a = sum_a + gn
            sum_b = sum_b + gn * normed
            gm_ref[at, lanes] = gn
        mean_a = jnp.sum(sum_a, axis=1, keepdims=True) * (1.0 / width)
        mean_b = jnp.sum(sum_b, axis=1, keepdims=True) * (1.0 / width)
        inv = inv_ref[at, :]
        centre = seg_ref[pl.ds(r0 + HALO, ROWS), :]
        for g in range(blocks // group):
            grads = {}
            for b in range(g * group, (g + 1) * group):
                lanes = slice(b * LANES, (b + 1) * LANES)
                grads[b] = inv * (gm_ref[at, lanes] - mean_a - norm_ref[at, lanes] * mean_b)
                gm_ref[at, lanes] = grads[b]
            for k in range(taps):
                same = seg_ref[pl.ds(r0 + k + 1, ROWS), :] == centre
                for b, grad in grads.items():
                    lanes = slice(b * LANES, (b + 1) * LANES)
                    prod = jnp.where(same, win[b, pl.ds(r0 + k + 1, ROWS), :], 0.0) * grad
                    kacc[k, :, lanes] = kacc[k, :, lanes] + rows_of(prod)
        pltpu.make_async_copy(gm_ref.at[at], gm_hbm.at[at], sems.at[i]).start()
        return carry

    count = length // ROWS
    lax.fori_loop(0, count, step, 0)
    ends = (
        pltpu.make_async_copy(gm_ref.at[0:HALO], first_hbm, sems.at[count]),
        pltpu.make_async_copy(gm_ref.at[length - HALO : length], last_hbm, sems.at[count + 1]),
    )
    for copy in ends:
        copy.start()
    core = lax.axis_index("core")
    for b in range(blocks):
        lanes = slice(b * LANES, (b + 1) * LANES)
        rows = [jnp.sum(kacc[k, :, lanes], axis=0, keepdims=True) for k in range(taps)]
        rows.append(jnp.sum(gg_ref[:, lanes], axis=0, keepdims=True))
        rows.append(jnp.zeros((LANES - taps - 1, LANES), F32))
        deal(core, b, jnp.concatenate(rows, axis=0).T, own, mine_ref, other_ref)
    for i in range(count):
        at = pl.ds(i * ROWS, ROWS)
        pltpu.make_async_copy(gm_ref.at[at], gm_hbm.at[at], sems.at[i]).wait()
    for copy in ends:
        copy.wait()


def back_kernel(act_ref, proj_ref, gm_ref, bef_ref, aft_ref, seg_ref, kern_ref, out_ref, gh_ref, win):
    taps, width = kern_ref.shape
    length = act_ref.shape[0]
    blocks = width // LANES
    part = 64
    nt = (((1,), (1,)), ((), ()))
    edges_in(win, bef_ref, aft_ref)
    for b in range(blocks):
        win[b, HALO : HALO + length, :] = gm_ref[:, b * LANES : (b + 1) * LANES]

    def multiply(i, carry):
        at = pl.ds(pl.multiple_of(i * part, part), part)
        out_ref[at, :] = lax.dot_general(act_ref[at, :], proj_ref[...], nt, preferred_element_type=F32).astype(BF)
        return carry

    lax.fori_loop(0, length // part, multiply, 0)

    def step(i, carry):
        r0 = pl.multiple_of(i * ROWS, ROWS)
        centre = seg_ref[pl.ds(r0 + HALO, ROWS), :]
        acc = [jnp.zeros((ROWS, LANES), F32) for _ in range(blocks)]
        for k in range(taps):
            same = seg_ref[pl.ds(r0 + taps - k, ROWS), :] == centre
            for b in range(blocks):
                w = kern_ref[k : k + 1, b * LANES : (b + 1) * LANES]
                term = win[b, pl.ds(r0 + taps - k, ROWS), :] * w
                acc[b] = acc[b] + jnp.where(same, term, 0.0)
        for b in range(blocks):
            gh_ref[pl.ds(r0, ROWS), b * LANES : (b + 1) * LANES] = acc[b].astype(BF)
        return carry

    lax.fori_loop(0, length // ROWS, step, 0)


def add_kernel(landed_ref, out_ref):
    count = landed_ref.shape[0]
    for b in range(out_ref.shape[1] // LANES):
        lanes = slice(b * LANES, (b + 1) * LANES)
        total = landed_ref[0, :, lanes].astype(F32)
        for j in range(1, count):
            total = total + landed_ref[j, :, lanes].astype(F32)
        out_ref[:, lanes] = total


def final_kernel(factor, taps, all_ref, weight_ref, small_ref, gain_ref):
    total = all_ref[0]
    for j in range(1, all_ref.shape[0]):
        total = total + all_ref[j]
    total = total * factor
    width = weight_ref.shape[1]
    weight_ref[...] = total[:, :width]
    small_ref[...] = total[:, width : width + taps]
    gain_ref[...] = total[:, width:].T[taps : taps + 1, :]


SEQ = ("y", "x", "core")


def shifted(value, steps):
    count = lax.axis_size("y") * lax.axis_size("x") * lax.axis_size("core")
    first, last = max(0, -steps), min(count, count - steps)
    return lax.ppermute(value, SEQ, [(i, i + steps) for i in range(first, last)])


def inner(hidden, segment_ids, kernel, norm_gain, projection, cotangent):
    frames = hidden[0]
    length, width = frames.shape
    taps = kernel.shape[0]
    cot = cotangent[0]
    ny, nx = lax.axis_size("y"), lax.axis_size("x")
    own = width // (ny * nx * 2)
    swap = [(0, 1), (1, 0)]
    big = 2 * length * width * width
    vec = length * width * taps
    shape = jax.ShapeDtypeStruct
    rows_win = length + 2 * HALO
    window = (width // LANES, rows_win, LANES)

    before = shifted(frames[length - HALO :], 1)
    after = shifted(frames[:HALO], -1)
    half = shape((width // 2, length), BF)
    ids = segment_ids.reshape(-1, LANES)
    mine, other, seg, mid, grad_act, proj, kern, gain = call(
        partial(first_kernel, own),
        (
            half,
            half,
            shape((rows_win, LANES), F32),
            shape((width // LANES, length, LANES), F32),
            shape((length, width), F32),
            shape((width, width), BF),
            shape((taps, width), F32),
            shape((1, width), F32),
        ),
        [
            pltpu.VMEM(ids.shape, ids.dtype),
            pltpu.VMEM((length, width), BF),
            pltpu.VMEM((length, width), BF),
            pltpu.SemaphoreType.DMA((6,)),
        ],
        flops=big,
        moved=12 * length * width,
        hbm=range(6),
    )(ids, cot, frames, projection, kernel, norm_gain[None, :])
    got = lax.ppermute(other, "core", swap)
    act, normed, inv, win = call(
        forward_kernel,
        (
            shape((length, width), BF),
            shape((length, width), F32),
            shape((length, LANES), F32),
            shape(window, F32),
        ),
        flops=3 * vec,
        moved=8 * length * width,
        trans=2 * length * width,
    )(mid, before, after, seg, kern, gain)
    act2 = lax.ppermute(act, "core", swap)
    far_edge = pltpu.HBM((HALO, width), F32)
    dealt = shape((width // 2, LANES), F32)
    grad_mixed, first, last, small, small_other = call(
        partial(taps_kernel, own),
        (pltpu.HBM((length, width), F32), far_edge, far_edge, dealt, dealt),
        [
            pltpu.VMEM((taps, 8, width), F32),
            pltpu.VMEM((8, width), F32),
            pltpu.VMEM((length, width), F32),
            pltpu.SemaphoreType.DMA((length // ROWS + 2,)),
        ],
        far=3,
        flops=3 * vec,
        moved=16 * length * width,
        trans=2 * length * width,
    )(grad_act, normed, inv, gain, seg, win)
    small2 = lax.ppermute(small_other, "core", swap)
    weight = call(
        product_kernel,
        shape((width // 2, width + LANES), BF),
        flops=big,
        moved=2 * (width * width + 3 * length * width),
    )(mine, got, act, act2, small, small2)
    landed = lax.all_to_all(
        weight.reshape(ny * nx, own, width + LANES), ("y", "x"), split_axis=0, concat_axis=0, tiled=True
    )
    gm_before = shifted(last, 1)
    gm_after = shifted(first, -1)
    conv_out, grad_hidden = call(
        back_kernel,
        (shape((length, width), BF), shape((length, width), BF)),
        [pltpu.VMEM(window, F32)],
        flops=3 * vec + big,
        moved=12 * length * width,
    )(act, proj, grad_mixed, gm_before, gm_after, seg, kern)
    share = call(add_kernel, shape((own, width + LANES), F32), moved=80 * own * width)(landed)
    everyone = lax.all_gather(share, "dp")
    factor = 1.0 / math.sqrt(length * ny * nx * 2 * lax.axis_size("dp"))
    grad_weight, grad_kernel, grad_gain = call(
        partial(final_kernel, factor, taps),
        (shape((own, width), F32), shape((own, taps), F32), shape((1, own), F32)),
        moved=64 * own * width,
    )(everyone)
    return conv_out[None], grad_hidden[None], grad_weight, grad_kernel, grad_gain[0]


def solution(mesh):
    dp, seq = mesh.devices.shape
    fine = Mesh(mesh.devices.reshape(dp, 8, seq // 16, 2), ("dp",) + SEQ)
    rows = P("dp", SEQ, None)
    in_specs = (rows, P("dp", None), P(), P(), P(), rows)
    out_specs = (rows, rows, P(SEQ, None), P(SEQ, None), P(SEQ))
    return jax.shard_map(inner, mesh=fine, in_specs=in_specs, out_specs=out_specs, check_vma=False)
```

time: 138 us -> 125 us (0.906)
  the two profiles are of different devices: /device:TPU:8 before, /device:TPU:40 now
where the time goes in v2:
time: 125 us
  blocking collectives  36.5 us (29%)
  starting transfers between devices  29.5 us (24%)
  Pallas kernels  29.1 us (23%)
  waiting for transfers between devices  25.5 us (20%)
  local copies, waits for them, and re-layouts  3.06 us (2%)
    all_gather x1, blocking collectives, inner(): everyone = lax.all_gather(share, 'dp')  36.5 us
    pallas_call x7, Pallas kernels, run(): pl.pallas_call(kernel, out_shape=outs, in_specs=specs, out_specs=jax.tree...  29.1 us
    ppermute x4, waiting for transfers between devices, shifted(): lax.ppermute(value, SEQ, [(i, i + steps) for i in range(first, last)])  24.1 us
    ppermute x4, starting transfers between devices, shifted(): lax.ppermute(value, SEQ, [(i, i + steps) for i in range(first, last)])  14.5 us
    all_to_all x1, starting transfers between devices, inner(): lax.all_to_all(weight.reshape(ny * nx, own, width + LANES), ('y', 'x'), s...  8.81 us
  transfers between devices with their start and end apart: 8, of which 3 were waited for; matrix products, arithmetic and copies ran while one was open for 0% of the time, Pallas kernels for 15%

profile of v2, /device:TPU:40, one launch (start us, length us, event | category | flops | bytes accessed | tf_op | source)
XLA Modules:
  0.0 124.5 jit_solution(18280384336379253356)
XLA Ops:
  0.6 0.8 slice_bitcast_fusion
  1.4 4.9 %collective-permute-start.1 = (bf16[16,1024]{1,0:T(8,128)(2,1)S(1)}, bf16[16,1024]{1,0:T(8,128)(2,1)S(1)}, u32[]{:S(2)}, u32[]{:S(2)}) collective-permute-start(bf16[16,1024]{1,0:T(8,128)(2,1)S(1)} %get-tuple-element.49), channel_id=1, source_target_pairs={{1,0},{2,1},{3,2},{4,3},{5,4},{6,5},{7,6},{8,7},{9,8},{10,9},{11,1... | collective-permute-start | bytes 98312 | tf_op jit(solution)/shard_map/ppermute | solution.py:315
  6.3 1.9 %collective-permute-start = (bf16[16,1024]{1,0:T(8,128)(2,1)S(1)}, bf16[16,1024]{1,0:T(8,128)(2,1)S(1)}, u32[]{:S(2)}, u32[]{:S(2)}) collective-permute-start(bf16[16,1024]{1,0:T(8,128)(2,1)S(1)} %get-tuple-element.50), channel_id=1, source_target_pairs={{0,1},{1,2},{2,3},{3,4},{4,5},{5,6},{6,7},{7,8},{8,9},{9,10},{10,1... | collective-permute-start | bytes 98312 | tf_op jit(solution)/shard_map/ppermute | solution.py:315
  8.2 4.0 %shard_map.101 = (bf16[512,256]{1,0:T(8,128)(2,1)S(1)}, bf16[512,256]{1,0:T(8,128)(2,1)S(1)}, f32[288,128]{1,0:T(8,128)S(1)}, f32[8,256,128]{2,1,0:T(8,128)S(1)}...) custom-call(s32[128,128]{1,0:T(8,128)} %bitcast.16, ...), custom_call_target="tpu_custom_call" | custom-call | flops 536870912 | bytes 3145728 | tf_op jit(solution)/shard_map/pallas_call | solution.py:31
  12.2 0.0 collective-permute-done.1.aft_ref
  12.2 1.4 %collective-permute-done.bef_ref = bf16[16,1024]{1,0:T(8,128)(2,1)S(1)} collective-permute-done((bf16[16,1024]{1,0:T(8,128)(2,1)S(1)}, bf16[16,1024]{1,0:T(8,128)(2,1)S(1)}, u32[]{:S(2)}, u32[]{:S(2)}) %collective-permute-start) | collective-permute-done | bytes 32800 | tf_op jit(solution)/shard_map/ppermute | solution.py:315
  13.6 7.2 %shard_map.102 = (bf16[256,1024]{1,0:T(8,128)(2,1)S(1)}, f32[256,1024]{1,0:T(8,128)S(1)}, f32[256,128]{1,0:T(8,128)S(1)}, f32[8,288,128]{2,1,0:T(8,128)S(1)}) custom-call(f32[8,256,128]{2,1,0:T(8,128)S(1)} %get-tuple-element.27.mid_ref, bf16[16,1024]{1,0:T(8,128)(2,1)S(1)} %collective-permute-done.bef_ref, ...), custom_call_target="tpu_custom_call" | custom-call | flops 24379392 | bytes 2097152 | tf_op jit(solution)/shard_map/pallas_call | solution.py:31
  20.9 0.0 copy-start
  20.9 1.9 %collective-permute-start.5 = (bf16[256,1024]{1,0:T(8,128)(2,1)S(1)}, bf16[256,1024]{1,0:T(8,128)(2,1)S(1)}, u32[]{:S(2)}, u32[]{:S(2)}) collective-permute-start(bf16[256,1024]{1,0:T(8,128)(2,1)S(1)} %get-tuple-element.31.act_ref), channel_id=1, source_target_pairs={{0,1},{1,0},{2,3},{3,2},{4,5},{5,4},{6,7},{7,6},{8,9},{9,8},{10,11... | collective-permute-start | bytes 1572872 | tf_op jit(solution)/shard_map/ppermute | solution.py:371
  22.8 2.4 %collective-permute-start.4 = (bf16[512,256]{1,0:T(8,128)(2,1)S(1)}, bf16[512,256]{1,0:T(8,128)(2,1)S(1)}, u32[]{:S(2)}, u32[]{:S(2)}) collective-permute-start(bf16[512,256]{1,0:T(8,128)(2,1)S(1)} %get-tuple-element.43), channel_id=1, source_target_pairs={{0,1},{1,0},{2,3},{3,2},{4,5},{5,4},{6,7},{7,6},{8,9},{9,8},{10,11... | collective-permute-start | bytes 786440 | tf_op jit(solution)/shard_map/ppermute | solution.py:358
  25.3 6.0 %shard_map.103 = (f32[256,1024]{1,0:T(8,128)}, f32[16,1024]{1,0:T(8,128)}, f32[16,1024]{1,0:T(8,128)}, f32[512,128]{1,0:T(8,128)S(1)}, f32[512,128]{1,0:T(8,128)S(1)}) custom-call(f32[256,1024]{1,0:T(8,128)S(1)} %get-tuple-element.33.ga_ref, f32[256,1024]{1,0:T(8,128)S(1)} %get-tuple-element.34.norm_ref, f32[256,128]{1,0:T(8,128)S(1)} %get-tuple-element.35.inv_ref, ...), custom_call_target="tpu_custom_call" | custom-call | flops 24379392 | bytes 4194304 | tf_op jit(solution)/shard_map/pallas_call | solution.py:31
  31.3 1.9 %collective-permute-start.6 = (f32[512,128]{1,0:T(8,128)S(1)}, f32[512,128]{1,0:T(8,128)S(1)}, u32[]{:S(2)}, u32[]{:S(2)}) collective-permute-start(f32[512,128]{1,0:T(8,128)S(1)} %get-tuple-element.45), channel_id=1, source_target_pairs={{0,1},{1,0},{2,3},{3,2},{4,5},{5,4},{6,7},{7,6},{8,9},{9,8},{10,11... | collective-permute-start | bytes 786440 | tf_op jit(solution)/shard_map/ppermute | solution.py:388
  33.2 0.0 collective-permute-done.4.got_ref
  33.2 1.5 %collective-permute-done.6.small2_ref = f32[512,128]{1,0:T(8,128)S(1)} collective-permute-done((f32[512,128]{1,0:T(8,128)S(1)}, f32[512,128]{1,0:T(8,128)S(1)}, u32[]{:S(2)}, u32[]{:S(2)}) %collective-permute-start.6) | collective-permute-done | bytes 262176 | tf_op jit(solution)/shard_map/ppermute | solution.py:388
  34.7 0.0 collective-permute-done.5.act2_ref
  34.7 0.0 copy-done
  34.7 2.3 %shard_map.105 = bf16[512,1152]{1,0:T(8,128)(2,1)} custom-call(bf16[512,256]{1,0:T(8,128)(2,1)S(1)} %get-tuple-element.42.mine_ref, bf16[512,256]{1,0:T(8,128)(2,1)S(1)} %collective-permute-done.4.got_ref, bf16[256,1024]{1,0:T(8,128)(2,1)S(1)} %get-tuple-element.31.act_ref, bf16[256,1024]{1,0:T(8,128)(2,1)S(1)} %collective-permute-done.5.act2_ref, ...), custom_call_target="tpu_custom_call" | custom-call | flops 536870912 | bytes 3670016 | tf_op jit(solution)/shard_map/pallas_call | solution.py:31
  37.1 8.8 %all-to-all-start = ((bf16[32,16,1152]{2,1,0:T(8,128)(2,1)}), bf16[32,16,1152]{2,1,0:T(8,128)(2,1)S(1)}, u32[]{:S(2)}, u32[]{:S(2)}) async-start(bf16[32,16,1152]{2,1,0:T(8,128)(2,1)} %bitcast.8), calls=%async_computation | async-start | bytes 2359296 | tf_op jit(solution)/shard_map/all_to_all | solution.py:395
  45.9 1.9 %collective-permute-start.2 = (f32[16,1024]{1,0:T(8,128)}, f32[16,1024]{1,0:T(8,128)S(1)}, u32[]{:S(2)}, u32[]{:S(2)}) collective-permute-start(f32[16,1024]{1,0:T(8,128)} %get-tuple-element.38), channel_id=1, source_target_pairs={{0,1},{1,2},{2,3},{3,4},{4,5},{5,6},{6,7},{7,8},{8,9},{9,10},{10,1... | collective-permute-start | bytes 196616 | tf_op jit(solution)/shard_map/ppermute | solution.py:315
  47.8 5.8 %collective-permute-start.3 = (f32[16,1024]{1,0:T(8,128)}, f32[16,1024]{1,0:T(8,128)S(1)}, u32[]{:S(2)}, u32[]{:S(2)}) collective-permute-start(f32[16,1024]{1,0:T(8,128)} %get-tuple-element.39), channel_id=1, source_target_pairs={{1,0},{2,1},{3,2},{4,3},{5,4},{6,5},{7,6},{8,7},{9,8},{10,9},{11,1... | collective-permute-start | bytes 196616 | tf_op jit(solution)/shard_map/ppermute | solution.py:315
  53.6 22.6 %collective-permute-done.2.bef_ref = f32[16,1024]{1,0:T(8,128)S(1)} collective-permute-done((f32[16,1024]{1,0:T(8,128)}, f32[16,1024]{1,0:T(8,128)S(1)}, u32[]{:S(2)}, u32[]{:S(2)}) %collective-permute-start.2) | collective-permute-done | bytes 65568 | tf_op jit(solution)/shard_map/ppermute | solution.py:315
  76.2 0.0 collective-permute-done.3.aft_ref
  76.2 0.0 copy-start.1
  76.2 1.0 copy-done.1
  77.2 0.0 copy-start.2
  77.2 1.2 copy-done.2
  78.5 8.6 %shard_map.104 = (bf16[256,1024]{1,0:T(8,128)(2,1)}, bf16[256,1024]{1,0:T(8,128)(2,1)}) custom-call(bf16[256,1024]{1,0:T(8,128)(2,1)S(1)} %copy-done.1, bf16[1024,1024]{1,0:T(8,128)(2,1)S(1)} %get-tuple-element.32.proj_ref, f32[256,1024]{1,0:T(8,128)S(1)} %copy-done.2, f32[16,1024]{1,0:T(8,128)S(1)} %collective-permute-done.2.bef_ref, ...), custom_call_target="tpu_custom_call" | custom-call | flops 561250304 | bytes 3145728 | tf_op jit(solution)/shard_map/pallas_call | solution.py:31
  87.1 0.0 all-to-all-done.landed_ref
  87.1 0.2 shard_map.106
  87.3 36.5 %all-gather = f32[192,1152]{1,0:T(8,128)S(1)} all-gather(f32[16,1152]{1,0:T(8,128)S(1)} %shard_map.106), channel_id=2, replica_groups=mesh['dp'=12,'y'=8,'x'=4,'core'=2] {'dp'}, dimensions={0}, use_global_device_ids=true | all-gather | bytes 958464 | tf_op jit(solution)/shard_map/all_gather | solution.py:408
  123.8 0.7 shard_map.107
Async XLA Ops:
  1.4 10.8 %collective-permute-start.1 = (bf16[16,1024]{1,0:T(8,128)(2,1)S(1)}, bf16[16,1024]{1,0:T(8,128)(2,1)S(1)}, u32[]{:S(2)}, u32[]{:S(2)}) collective-permute-start(bf16[16,1024]{1,0:T(8,128)(2,1)S(1)} %get-tuple-element.49), channel_id=1, source_target_pairs={{1,0},{2,1},{3,2},{4,3},{5,4},{6,5},{7,6},{8,7},{9,8},{10,9},{11,1... | collective-permute-start | bytes 98312 | tf_op jit(solution)/shard_map/ppermute | solution.py:315
  6.3 7.3 %collective-permute-start = (bf16[16,1024]{1,0:T(8,128)(2,1)S(1)}, bf16[16,1024]{1,0:T(8,128)(2,1)S(1)}, u32[]{:S(2)}, u32[]{:S(2)}) collective-permute-start(bf16[16,1024]{1,0:T(8,128)(2,1)S(1)} %get-tuple-element.50), channel_id=1, source_target_pairs={{0,1},{1,2},{2,3},{3,4},{4,5},{5,6},{6,7},{7,8},{8,9},{9,10},{10,1... | collective-permute-start | bytes 98312 | tf_op jit(solution)/shard_map/ppermute | solution.py:315
  20.9 13.8 %copy-start = (bf16[256,1024]{1,0:T(8,128)(2,1)}, bf16[256,1024]{1,0:T(8,128)(2,1)S(1)}, u32[]{:S(2)}) copy-start(bf16[256,1024]{1,0:T(8,128)(2,1)S(1)} %get-tuple-element.31.act_ref) | copy-start | bytes 1572868
  20.9 13.8 %collective-permute-start.5 = (bf16[256,1024]{1,0:T(8,128)(2,1)S(1)}, bf16[256,1024]{1,0:T(8,128)(2,1)S(1)}, u32[]{:S(2)}, u32[]{:S(2)}) collective-permute-start(bf16[256,1024]{1,0:T(8,128)(2,1)S(1)} %get-tuple-element.31.act_ref), channel_id=1, source_target_pairs={{0,1},{1,0},{2,3},{3,2},{4,5},{5,4},{6,7},{7,6},{8,9},{9,8},{10,11... | collective-permute-start | bytes 1572872 | tf_op jit(solution)/shard_map/ppermute | solution.py:371
  22.8 10.4 %collective-permute-start.4 = (bf16[512,256]{1,0:T(8,128)(2,1)S(1)}, bf16[512,256]{1,0:T(8,128)(2,1)S(1)}, u32[]{:S(2)}, u32[]{:S(2)}) collective-permute-start(bf16[512,256]{1,0:T(8,128)(2,1)S(1)} %get-tuple-element.43), channel_id=1, source_target_pairs={{0,1},{1,0},{2,3},{3,2},{4,5},{5,4},{6,7},{7,6},{8,9},{9,8},{10,11... | collective-permute-start | bytes 786440 | tf_op jit(solution)/shard_map/ppermute | solution.py:358
  31.3 3.4 %collective-permute-start.6 = (f32[512,128]{1,0:T(8,128)S(1)}, f32[512,128]{1,0:T(8,128)S(1)}, u32[]{:S(2)}, u32[]{:S(2)}) collective-permute-start(f32[512,128]{1,0:T(8,128)S(1)} %get-tuple-element.45), channel_id=1, source_target_pairs={{0,1},{1,0},{2,3},{3,2},{4,5},{5,4},{6,7},{7,6},{8,9},{9,8},{10,11... | collective-permute-start | bytes 786440 | tf_op jit(solution)/shard_map/ppermute | solution.py:388
  37.1 50.1 %all-to-all-start = ((bf16[32,16,1152]{2,1,0:T(8,128)(2,1)}), bf16[32,16,1152]{2,1,0:T(8,128)(2,1)S(1)}, u32[]{:S(2)}, u32[]{:S(2)}) async-start(bf16[32,16,1152]{2,1,0:T(8,128)(2,1)} %bitcast.8), calls=%async_computation | async-start | bytes 2359296 | tf_op jit(solution)/shard_map/all_to_all | solution.py:395
  45.9 30.3 %collective-permute-start.2 = (f32[16,1024]{1,0:T(8,128)}, f32[16,1024]{1,0:T(8,128)S(1)}, u32[]{:S(2)}, u32[]{:S(2)}) collective-permute-start(f32[16,1024]{1,0:T(8,128)} %get-tuple-element.38), channel_id=1, source_target_pairs={{0,1},{1,2},{2,3},{3,4},{4,5},{5,6},{6,7},{7,8},{8,9},{9,10},{10,1... | collective-permute-start | bytes 196616 | tf_op jit(solution)/shard_map/ppermute | solution.py:315
  47.8 28.4 %collective-permute-start.3 = (f32[16,1024]{1,0:T(8,128)}, f32[16,1024]{1,0:T(8,128)S(1)}, u32[]{:S(2)}, u32[]{:S(2)}) collective-permute-start(f32[16,1024]{1,0:T(8,128)} %get-tuple-element.39), channel_id=1, source_target_pairs={{1,0},{2,1},{3,2},{4,3},{5,4},{6,5},{7,6},{8,7},{9,8},{10,9},{11,1... | collective-permute-start | bytes 196616 | tf_op jit(solution)/shard_map/ppermute | solution.py:315
  76.2 1.0 copy-start.1
  77.2 1.2 copy-start.2

commit v3 on v2

v3 whole, which is shorter than its diff:
```python
import math
from functools import partial

import jax
import jax.numpy as jnp
from jax import lax
from jax.experimental import pallas as pl
from jax.experimental.pallas import tpu as pltpu
from jax.sharding import Mesh
from jax.sharding import PartitionSpec as P


EPS = 1e-05
LANES = 128
NEAR = 16
WIDE = 32
ROWS = 32
BF = jnp.bfloat16
F32 = jnp.float32


def call(kernel, outs, scratch=(), flops=0, moved=0, trans=0, hbm=(), far=0, limit=9):
    def run(*args):
        specs = [
            pl.BlockSpec(memory_space=pltpu.HBM if i in hbm else pltpu.VMEM)
            for i in range(len(args))
        ]
        args = [
            pltpu.with_memory_space_constraint(arg, pltpu.HBM) if i in hbm else arg
            for i, arg in enumerate(args)
        ]
        return pl.pallas_call(
            kernel,
            out_shape=outs,
            in_specs=specs,
            out_specs=jax.tree.unflatten(
                jax.tree.structure(outs),
                [
                    pl.BlockSpec(memory_space=pltpu.HBM if i < far else pltpu.VMEM)
                    for i in range(len(jax.tree.leaves(outs)))
                ],
            ),
            scratch_shapes=list(scratch),
            compiler_params=pltpu.CompilerParams(vmem_limit_bytes=limit * 1024 * 1024),
            cost_estimate=pl.CostEstimate(flops=flops, bytes_accessed=moved, transcendentals=trans),
        )(*args)

    return run


def deal(core, at, even, odd, mine_ref, other_ref):
    mine_ref[at : at + even.shape[0], :] = jnp.where(core == 0, even, odd)
    other_ref[at : at + even.shape[0], :] = jnp.where(core == 0, odd, even)


def place_of(axes):
    index = lax.axis_index(axes[0])
    for axis in axes[1:]:
        index = index * lax.axis_size(axis) + lax.axis_index(axis)
    return index


def matmul_into(out_ref, pairs, transposed=False):
    part = 256
    dims = (((1,), (1,)), ((), ())) if transposed else (((1,), (0,)), ((), ()))
    for n in range(out_ref.shape[1] // part):
        at = slice(n * part, (n + 1) * part)
        total = None
        for left, right in pairs:
            term = lax.dot_general(
                left[...], right[at, :] if transposed else right[:, at], dims, preferred_element_type=F32
            )
            total = term if total is None else total + term
        out_ref[:, at] = total.astype(out_ref.dtype)


def ends_kernel(hid_hbm, cot_hbm, up_ref, down_ref, sems):
    length = hid_hbm.shape[0]
    pairs = (
        (hid_hbm.at[length - WIDE : length], up_ref.at[0:WIDE]),
        (cot_hbm.at[length - NEAR : length], up_ref.at[WIDE : WIDE + NEAR]),
        (hid_hbm.at[0:WIDE], down_ref.at[0:WIDE]),
        (cot_hbm.at[0:NEAR], down_ref.at[WIDE : WIDE + NEAR]),
    )
    copies = [pltpu.make_async_copy(src, dst, sems.at[i]) for i, (src, dst) in enumerate(pairs)]
    for copy in copies:
        copy.start()
    for copy in copies:
        copy.wait()


def first_kernel(
    own, ids_hbm, cot_hbm, hid_hbm, proj_hbm, kern_hbm, gain_hbm,
    mine_ref, other_ref, seg_ref, mid_ref, ga_ref, kern_ref, gain_ref,
    ids_ref, cot_ref, hid_ref, proj_ref, sems,
):
    pairs = (
        (cot_hbm, cot_ref), (ids_hbm, ids_ref), (hid_hbm, hid_ref),
        (kern_hbm, kern_ref), (gain_hbm, gain_ref), (proj_hbm, proj_ref),
    )
    copies = [pltpu.make_async_copy(src, dst, sems.at[i]) for i, (src, dst) in enumerate(pairs)]
    for copy in copies:
        copy.start()
    copies[0].wait()
    core = lax.axis_index("core")
    length, width = cot_ref.shape
    for b in range(width // LANES):
        turned = cot_ref[:, b * LANES : (b + 1) * LANES].T
        for j in range(LANES // (2 * own)):
            at = 2 * own * j
            even, odd = turned[at : at + own], turned[at + own : at + 2 * own]
            deal(core, (b * (LANES // (2 * own)) + j) * own, even, odd, mine_ref, other_ref)
    copies[1].wait()
    index = place_of(SEQ)
    lines = length // LANES
    last = ids_ref.shape[0] - 1

    def column(line, outside):
        row = ids_ref[pl.ds(jnp.clip(line, 0, last), 1), :].astype(F32)
        square = jnp.broadcast_to(row, (LANES, LANES)).T
        return jnp.where(outside, -1.0, square)

    head = column(lines * index - 1, index == 0)
    seg_ref[0:WIDE, :] = head[LANES - WIDE :]
    for j in range(lines):
        seg_ref[WIDE + j * LANES : WIDE + (j + 1) * LANES, :] = column(lines * index + j, False)
    tail = column(lines * index + lines, lines * index + lines > last)
    seg_ref[WIDE + length : 2 * WIDE + length, :] = tail[:WIDE]
    copies[2].wait()
    for b in range(width // LANES):
        mid_ref[b] = hid_ref[:, b * LANES : (b + 1) * LANES].astype(F32)
    for copy in copies[3:]:
        copy.wait()
    matmul_into(ga_ref, ((cot_ref, proj_ref),))


def convolved(win, wr, seg_ref, sr, kern_ref, rows):
    taps, width = kern_ref.shape
    blocks = width // LANES
    centre = seg_ref[pl.ds(sr + taps // 2, rows), :]
    acc = [jnp.zeros((rows, LANES), F32) for _ in range(blocks)]
    for k in range(taps):
        same = seg_ref[pl.ds(sr + k, rows), :] == centre
        for b in range(blocks):
            term = win[b, pl.ds(wr + k, rows), :] * kern_ref[k : k + 1, b * LANES : (b + 1) * LANES]
            acc[b] = acc[b] + jnp.where(same, term, 0.0)
    return acc


def mean_of(parts, width):
    total = parts[0]
    for part in parts[1:]:
        total = total + part
    return jnp.sum(total, axis=1, keepdims=True) * (1.0 / width)


def normalised(acc, width):
    mean = mean_of(acc, width)
    acc = [a - mean for a in acc]
    inv = lax.rsqrt(mean_of([a * a for a in acc], width) + EPS)
    return [a * inv for a in acc], inv


def gate_back(grad, normed, gain):
    gated = normed * gain
    sigma = jax.nn.sigmoid(gated)
    return grad * sigma * (1.0 + gated * (1.0 - sigma))


def forward_kernel(
    mid_ref, bef_ref, aft_ref, seg_ref, kern_ref, gain_ref, other_ref, pack_ref, norm_ref, inv_ref, win
):
    taps, width = kern_ref.shape
    length = norm_ref.shape[0]
    blocks = width // LANES
    for b in range(blocks):
        lanes = slice(b * LANES, (b + 1) * LANES)
        win[b, 0:WIDE, :] = bef_ref[0:WIDE, lanes].astype(F32)
        win[b, WIDE : WIDE + length, :] = mid_ref[b]
        win[b, WIDE + length :, :] = aft_ref[0:WIDE, lanes].astype(F32)
    for j in range(width // length):
        rows = other_ref.shape[0] * length // width
        pack_ref[length:, j * length : (j + 1) * length] = other_ref[j * rows : (j + 1) * rows, :]
    off = WIDE - taps // 2

    def step(i, carry):
        r0 = pl.multiple_of(i * ROWS, ROWS)
        normed, inv = normalised(convolved(win, r0 + off, seg_ref, r0 + off, kern_ref, ROWS), width)
        inv_ref[pl.ds(r0, ROWS), :] = jnp.broadcast_to(inv, (ROWS, LANES))
        for b in range(blocks):
            lanes = slice(b * LANES, (b + 1) * LANES)
            norm_ref[pl.ds(r0, ROWS), lanes] = normed[b]
            gated = normed[b] * gain_ref[:, lanes]
            pack_ref[pl.ds(r0, ROWS), lanes] = (gated * jax.nn.sigmoid(gated)).astype(BF)
        return carry

    lax.fori_loop(0, length // ROWS, step, 0)


def product_kernel(own, mine_ref, pack_ref, pack2_ref, small_ref, small2_ref, out_hbm, out_ref, sems):
    rows, length = mine_ref.shape
    width = pack_ref.shape[1]
    count = rows // own
    part = 256
    deep = rows * length // width
    got = [pack2_ref[length:, j * length : (j + 1) * length] for j in range(rows // deep)]
    got = jnp.concatenate(got, axis=0)
    copies = []

    def send(first, last):
        at = slice(first, last)
        copies.append(pltpu.make_async_copy(out_ref.at[:, at], out_hbm.at[:, at], sems.at[len(copies)]))
        copies[-1].start()

    line = width // LANES * own
    small = (small_ref[...] + small2_ref[...]).astype(BF)
    out_ref[:, line:, :] = small.reshape(count, own // 2, LANES)
    send(line, line + own // 2)
    for n in range(width // part):
        at = slice(n * part, (n + 1) * part)
        total = jnp.dot(mine_ref[...], pack_ref[0:length, at], preferred_element_type=F32)
        total = total + jnp.dot(got, pack2_ref[0:length, at], preferred_element_type=F32)
        total = total.astype(BF).reshape(count, own, part)
        for b in range(part // LANES):
            line = (n * (part // LANES) + b) * own
            out_ref[:, line : line + own, :] = total[:, :, b * LANES : (b + 1) * LANES]
        send(n * (part // LANES) * own, (n + 1) * (part // LANES) * own)
    for copy in copies:
        copy.wait()


def taps_kernel(
    own, ga_ref, norm_ref, inv_ref, gain_ref, seg_ref, win,
    gm_hbm, mine_ref, other_ref, kacc, gg_ref, gm_ref, sems,
):
    length, width = norm_ref.shape
    taps = kacc.shape[0]
    blocks = width // LANES
    group = 4
    off = WIDE - taps // 2
    gg_ref[...] = jnp.zeros(gg_ref.shape, F32)
    kacc[...] = jnp.zeros(kacc.shape, F32)

    def rows_of(value):
        rows8 = value[0:8]
        for r in range(8, ROWS, 8):
            rows8 = rows8 + value[r : r + 8]
        return rows8

    def step(i, carry):
        r0 = pl.multiple_of(i * ROWS, ROWS)
        at = pl.ds(r0, ROWS)
        sum_a = jnp.zeros((ROWS, LANES), F32)
        sum_b = jnp.zeros((ROWS, LANES), F32)
        for b in range(blocks):
            lanes = slice(b * LANES, (b + 1) * LANES)
            gain = gain_ref[:, lanes]
            normed = norm_ref[at, lanes]
            gg = gate_back(ga_ref[at, lanes], normed, gain)
            gg_ref[:, lanes] = gg_ref[:, lanes] + rows_of(gg * normed)
            gn = gg * gain
            sum_a = sum_a + gn
            sum_b = sum_b + gn * normed
            gm_ref[at, lanes] = gn
        mean_a = jnp.sum(sum_a, axis=1, keepdims=True) * (1.0 / width)
        mean_b = jnp.sum(sum_b, axis=1, keepdims=True) * (1.0 / width)
        inv = inv_ref[at, :]
        centre = seg_ref[pl.ds(r0 + WIDE, ROWS), :]
        for g in range(blocks // group):
            grads = {}
            for b in range(g * group, (g + 1) * group):
                lanes = slice(b * LANES, (b + 1) * LANES)
                grads[b] = inv * (gm_ref[at, lanes] - mean_a - norm_ref[at, lanes] * mean_b)
                gm_ref[at, lanes] = grads[b]
            for k in range(taps):
                same = seg_ref[pl.ds(r0 + off + k, ROWS), :] == centre
                for b, grad in grads.items():
                    lanes = slice(b * LANES, (b + 1) * LANES)
                    prod = jnp.where(same, win[b, pl.ds(r0 + off + k, ROWS), :], 0.0) * grad
                    kacc[k, :, lanes] = kacc[k, :, lanes] + rows_of(prod)
        pltpu.make_async_copy(gm_ref.at[at], gm_hbm.at[at], sems.at[i]).start()
        return carry

    count = length // ROWS
    lax.fori_loop(0, count, step, 0)
    core = lax.axis_index("core")
    half = own // 2
    upper = (lax.broadcasted_iota(jnp.int32, (taps + 1, LANES), 1) // half) % 2 == 1
    for b in range(blocks):
        lanes = slice(b * LANES, (b + 1) * LANES)
        rows = [jnp.sum(kacc[k, :, lanes], axis=0, keepdims=True) for k in range(taps)]
        rows.append(jnp.sum(gg_ref[:, lanes], axis=0, keepdims=True))
        rows = jnp.concatenate(rows, axis=0)
        pad = jnp.zeros((LANES - 2 * (taps + 1), LANES), F32)
        turned = jnp.concatenate([jnp.where(upper, 0.0, rows), jnp.where(upper, rows, 0.0), pad], axis=0).T
        for j in range(LANES // (2 * own)):
            at = 2 * own * j
            even = turned[at : at + half] + turned[at + half : at + own]
            odd = turned[at + own : at + own + half] + turned[at + own + half : at + 2 * own]
            deal(core, (b * (LANES // (2 * own)) + j) * half, even, odd, mine_ref, other_ref)
    for i in range(count):
        at = pl.ds(i * ROWS, ROWS)
        pltpu.make_async_copy(gm_ref.at[at], gm_hbm.at[at], sems.at[i]).wait()


def back_kernel(
    pack_ref, proj_ref, gm_ref, bef_ref, aft_ref, seg_ref, kern_ref, gain_ref, hid_hbm,
    out_ref, gh_ref, gwin, hwin, hid_ref, ga_ref, sems,
):
    taps, width = kern_ref.shape
    length = gh_ref.shape[0]
    blocks = width // LANES
    copies = (
        pltpu.make_async_copy(hid_hbm.at[0:WIDE], hid_ref.at[0], sems.at[0]),
        pltpu.make_async_copy(hid_hbm.at[length - WIDE : length], hid_ref.at[1], sems.at[1]),
    )
    for copy in copies:
        copy.start()
    matmul_into(out_ref, ((pack_ref.at[0:length], proj_ref),), transposed=True)
    matmul_into(ga_ref.at[0:NEAR], ((bef_ref.at[WIDE:], proj_ref),))
    matmul_into(ga_ref.at[NEAR:], ((aft_ref.at[WIDE:], proj_ref),))
    for copy in copies:
        copy.wait()
    for b in range(blocks):
        lanes = slice(b * LANES, (b + 1) * LANES)
        gwin[b, NEAR : NEAR + length, :] = gm_ref[:, lanes]
        hwin[b, 0:WIDE, :] = bef_ref[0:WIDE, lanes].astype(F32)
        hwin[b, WIDE : 2 * WIDE, :] = hid_ref[0, :, lanes].astype(F32)
        hwin[b, 2 * WIDE : 3 * WIDE, :] = hid_ref[1, :, lanes].astype(F32)
        hwin[b, 3 * WIDE :, :] = aft_ref[0:WIDE, lanes].astype(F32)
    reach = taps // 2
    sides = (
        (NEAR - reach, NEAR - reach, 0, 0),
        (3 * WIDE - reach, WIDE + length - reach, NEAR, NEAR + length),
    )
    for wr, sr, ar, to in sides:
        normed, inv = normalised(convolved(hwin, wr, seg_ref, sr, kern_ref, NEAR), width)
        grads = []
        for b in range(blocks):
            lanes = slice(b * LANES, (b + 1) * LANES)
            gain = gain_ref[:, lanes]
            grads.append(gate_back(ga_ref[ar : ar + NEAR, lanes], normed[b], gain) * gain)
        mean_a = mean_of(grads, width)
        mean_b = mean_of([g * n for g, n in zip(grads, normed)], width)
        for b in range(blocks):
            gwin[b, to : to + NEAR, :] = inv * (grads[b] - mean_a - normed[b] * mean_b)

    def step(i, carry):
        r0 = pl.multiple_of(i * ROWS, ROWS)
        centre = seg_ref[pl.ds(r0 + WIDE, ROWS), :]
        acc = [jnp.zeros((ROWS, LANES), F32) for _ in range(blocks)]
        for k in range(taps):
            line = NEAR + reach - k
            same = seg_ref[pl.ds(r0 + line + WIDE - NEAR, ROWS), :] == centre
            for b in range(blocks):
                w = kern_ref[k : k + 1, b * LANES : (b + 1) * LANES]
                term = gwin[b, pl.ds(r0 + line, ROWS), :] * w
                acc[b] = acc[b] + jnp.where(same, term, 0.0)
        for b in range(blocks):
            gh_ref[pl.ds(r0, ROWS), b * LANES : (b + 1) * LANES] = acc[b].astype(BF)
        return carry

    lax.fori_loop(0, length // ROWS, step, 0)


def add_kernel(landed_ref, out_ref):
    total = landed_ref[0].astype(F32)
    for j in range(1, landed_ref.shape[0]):
        total = total + landed_ref[j].astype(F32)
    out_ref[...] = total


def final_kernel(factor, taps, all_ref, weight_ref, small_ref, gain_ref):
    total = all_ref[0]
    for j in range(1, all_ref.shape[0]):
        total = total + all_ref[j]
    total = total * factor
    own, width = weight_ref.shape
    for b in range(width // LANES):
        weight_ref[:, b * LANES : (b + 1) * LANES] = total[b * own : (b + 1) * own, :]
    tail = total[width // LANES * own :, :]
    tail = jnp.concatenate([tail[:, : taps + 1], tail[:, taps + 1 : 2 * (taps + 1)]], axis=0)
    small_ref[...] = tail[:, :taps]
    wide = jnp.concatenate([tail, jnp.zeros((own, LANES - taps - 1), F32)], axis=1)
    gain_ref[...] = wide.T[taps : taps + 1, :]


SEQ = ("y", "x", "core")


def shifted(value, steps):
    count = lax.axis_size("y") * lax.axis_size("x") * lax.axis_size("core")
    first, last = max(0, -steps), min(count, count - steps)
    return lax.ppermute(value, SEQ, [(i, i + steps) for i in range(first, last)])


def inner(hidden, segment_ids, kernel, norm_gain, projection, cotangent):
    frames = hidden[0]
    length, width = frames.shape
    taps = kernel.shape[0]
    cot = cotangent[0]
    ny, nx = lax.axis_size("y"), lax.axis_size("x")
    own = width // (ny * nx * 2)
    swap = [(0, 1), (1, 0)]
    big = 2 * length * width * width
    vec = length * width * taps
    shape = jax.ShapeDtypeStruct
    rows_win = length + 2 * WIDE
    blocks = width // LANES
    window = (blocks, rows_win, LANES)
    lines = (blocks * own) + own // 2

    message = shape((WIDE + NEAR, width), BF)
    up, down = call(
        ends_kernel, (message, message), [pltpu.SemaphoreType.DMA((4,))], moved=512 * width, hbm=(0, 1)
    )(frames, cot)
    before = shifted(up, 1)
    after = shifted(down, -1)
    half = shape((width // 2, length), BF)
    ids = segment_ids.reshape(-1, LANES)
    mine, other, seg, mid, grad_act, kern, gain = call(
        partial(first_kernel, own),
        (
            half,
            half,
            shape((rows_win, LANES), F32),
            shape((blocks, length, LANES), F32),
            shape((length, width), F32),
            shape((taps, width), F32),
            shape((1, width), F32),
        ),
        [
            pltpu.VMEM(ids.shape, ids.dtype),
            pltpu.VMEM((length, width), BF),
            pltpu.VMEM((length, width), BF),
            pltpu.VMEM((width, width), BF),
            pltpu.SemaphoreType.DMA((6,)),
        ],
        flops=big,
        moved=12 * length * width,
        hbm=range(6),
    )(ids, cot, frames, projection, kernel, norm_gain[None, :])
    pack, normed, inv, win = call(
        forward_kernel,
        (
            shape((length + length // 2, width), BF),
            shape((length, width), F32),
            shape((length, LANES), F32),
            shape(window, F32),
        ),
        flops=3 * vec,
        moved=8 * length * width,
        trans=2 * length * width,
    )(mid, before, after, seg, kern, gain, other)
    pack2 = lax.ppermute(pack, "core", swap)
    dealt = shape((width // 4, LANES), F32)
    grad_mixed, small, small_other = call(
        partial(taps_kernel, own),
        (pltpu.HBM((length, width), F32), dealt, dealt),
        [
            pltpu.VMEM((taps, 8, width), F32),
            pltpu.VMEM((8, width), F32),
            pltpu.VMEM((length, width), F32),
            pltpu.SemaphoreType.DMA((length // ROWS,)),
        ],
        far=1,
        flops=3 * vec,
        moved=16 * length * width,
        trans=2 * length * width,
    )(grad_act, normed, inv, gain, seg, win)
    small2 = lax.ppermute(small_other, "core", swap)
    weight = call(
        partial(product_kernel, own),
        pltpu.HBM((ny * nx, lines, LANES), BF),
        [pltpu.VMEM((ny * nx, lines, LANES), BF), pltpu.SemaphoreType.DMA((width // 256 + 1,))],
        far=1,
        flops=big,
        moved=2 * (width * width + 3 * length * width),
    )(mine, pack, pack2, small, small2)
    landed = lax.all_to_all(weight, ("y", "x"), split_axis=0, concat_axis=0, tiled=True)
    conv_out, grad_hidden = call(
        back_kernel,
        (shape((length, width), BF), shape((length, width), BF)),
        [
            pltpu.VMEM((blocks, length + 2 * NEAR, LANES), F32),
            pltpu.VMEM((blocks, 4 * WIDE, LANES), F32),
            pltpu.VMEM((2, WIDE, width), BF),
            pltpu.VMEM((2 * NEAR, width), F32),
            pltpu.SemaphoreType.DMA((2,)),
        ],
        flops=3 * vec + big,
        moved=12 * length * width,
        hbm=(8,),
    )(pack, projection, grad_mixed, before, after, seg, kern, gain, frames)
    share = call(add_kernel, shape((lines, LANES), F32), moved=80 * own * width)(landed)
    everyone = lax.all_gather(share, "dp")
    factor = 1.0 / math.sqrt(length * ny * nx * 2 * lax.axis_size("dp"))
    grad_weight, grad_kernel, grad_gain = call(
        partial(final_kernel, factor, taps),
        (shape((own, width), F32), shape((own, taps), F32), shape((1, own), F32)),
        moved=64 * own * width,
    )(everyone)
    return conv_out[None], grad_hidden[None], grad_weight, grad_kernel, grad_gain[0]


def solution(mesh):
    dp, seq = mesh.devices.shape
    fine = Mesh(mesh.devices.reshape(dp, 8, seq // 16, 2), ("dp",) + SEQ)
    rows = P("dp", SEQ, None)
    in_specs = (rows, P("dp", None), P(), P(), P(), rows)
    out_specs = (rows, rows, P(SEQ, None), P(SEQ, None), P(SEQ))
    return jax.shard_map(inner, mesh=fine, in_specs=in_specs, out_specs=out_specs, check_vma=False)
```

time: 125 us -> 112 us (0.90)
  the two profiles are of different devices: /device:TPU:40 before, /device:TPU:4 now
where the time goes in v3:
time: 112 us
  blocking collectives  37.6 us (34%)
  Pallas kernels  27.6 us (25%)
  starting transfers between devices  22.9 us (20%)
  waiting for transfers between devices  18.4 us (16%)
  local copies, waits for them, and re-layouts  4.16 us (4%)
    all_gather x1, blocking collectives, inner(): everyone = lax.all_gather(share, 'dp')  37.6 us
    pallas_call x8, Pallas kernels, run(): pl.pallas_call(kernel, out_shape=outs, in_specs=specs, out_specs=jax.tree...  27.6 us
    all_to_all x1, waiting for transfers between devices, inner(): lax.all_to_all(weight, ('y', 'x'), split_axis=0, concat_axis=0, tiled=True)  17.1 us
    all_to_all x1, starting transfers between devices, inner(): lax.all_to_all(weight, ('y', 'x'), split_axis=0, concat_axis=0, tiled=True)  12.7 us
    ppermute x2, starting transfers between devices, shifted(): lax.ppermute(value, SEQ, [(i, i + steps) for i in range(first, last)])  5.56 us
    unnamed x16, local copies, waits for them, and re-layouts  4.16 us
    ppermute x1, starting transfers between devices, inner(): pack2 = lax.ppermute(pack, 'core', swap)  2.67 us
  transfers between devices with their start and end apart: 5, of which 2 were waited for; matrix products, arithmetic and copies ran while one was open for 0% of the time, Pallas kernels for 15%

profile of v3, /device:TPU:4, one launch (start us, length us, event | category | flops | bytes accessed | tf_op | source)
XLA Modules:
  0.0 111.5 jit_solution(15191955509468891515)
XLA Ops:
  0.6 0.9 shard_map.102
  1.6 1.9 %collective-permute-start = (bf16[48,1024]{1,0:T(8,128)(2,1)S(1)}, bf16[48,1024]{1,0:T(8,128)(2,1)S(1)}, u32[]{:S(2)}, u32[]{:S(2)}) collective-permute-start(bf16[48,1024]{1,0:T(8,128)(2,1)S(1)} %get-tuple-element.27), channel_id=1, source_target_pairs={{0,1},{1,2},{2,3},{3,4},{4,5},{5,6},{6,7},{7,8},{8,9},{9,10},{10,1... | collective-permute-start | bytes 294920 | tf_op jit(solution)/shard_map/ppermute | solution.py:394
  3.5 3.6 %collective-permute-start.1 = (bf16[48,1024]{1,0:T(8,128)(2,1)S(1)}, bf16[48,1024]{1,0:T(8,128)(2,1)S(1)}, u32[]{:S(2)}, u32[]{:S(2)}) collective-permute-start(bf16[48,1024]{1,0:T(8,128)(2,1)S(1)} %get-tuple-element.28), channel_id=1, source_target_pairs={{1,0},{2,1},{3,2},{4,3},{5,4},{6,5},{7,6},{8,7},{9,8},{10,9},{11,1... | collective-permute-start | bytes 294920 | tf_op jit(solution)/shard_map/ppermute | solution.py:394
  7.1 2.8 %shard_map.101 = (bf16[512,256]{1,0:T(8,128)(2,1)S(1)}, bf16[512,256]{1,0:T(8,128)(2,1)S(1)}, f32[320,128]{1,0:T(8,128)S(1)}, f32[8,256,128]{2,1,0:T(8,128)S(1)}...) custom-call(s32[128,128]{1,0:T(8,128)} %bitcast.14, bf16[256,1024]{1,0:T(8,128)(2,1)} %bitcast.13, ...), custom_call_target="tpu_custom_call" | custom-call | flops 536870912 | bytes 3145728 | tf_op jit(solution)/shard_map/pallas_call | solution.py:32
  9.9 0.0 collective-permute-done.bef_ref
  9.9 0.0 copy-start.4
  9.9 0.0 collective-permute-done.1.aft_ref
  10.0 0.0 copy-start.6
  10.0 7.2 %shard_map.103 = (bf16[384,1024]{1,0:T(8,128)(2,1)S(1)}, f32[256,1024]{1,0:T(8,128)S(1)}, f32[256,128]{1,0:T(8,128)S(1)}, f32[8,320,128]{2,1,0:T(8,128)S(1)}) custom-call(f32[8,256,128]{2,1,0:T(8,128)S(1)} %get-tuple-element.26.mid_ref, bf16[48,1024]{1,0:T(8,128)(2,1)S(1)} %collective-permute-done.bef_ref, ...), custom_call_target="tpu_custom_call" | custom-call | flops 24379392 | bytes 2097152 | tf_op jit(solution)/shard_map/pallas_call | solution.py:32
  17.2 0.0 copy-start.1
  17.2 2.7 %collective-permute-start.2 = (bf16[384,1024]{1,0:T(8,128)(2,1)S(1)}, bf16[384,1024]{1,0:T(8,128)(2,1)S(1)}, u32[]{:S(2)}, u32[]{:S(2)}) collective-permute-start(bf16[384,1024]{1,0:T(8,128)(2,1)S(1)} %get-tuple-element.33.pack_ref), channel_id=1, source_target_pairs={{0,1},{1,0},{2,3},{3,2},{4,5},{5,4},{6,7},{7,6},{8,9},{9,8},{10,11... | collective-permute-start | bytes 2359304 | tf_op jit(solution)/shard_map/ppermute | solution.py:455
  19.9 5.7 %shard_map.104 = (f32[256,1024]{1,0:T(8,128)}, f32[256,128]{1,0:T(8,128)S(1)}, f32[256,128]{1,0:T(8,128)S(1)}) custom-call(f32[256,1024]{1,0:T(8,128)S(1)} %get-tuple-element.34.ga_ref, f32[256,1024]{1,0:T(8,128)S(1)} %get-tuple-element.35.norm_ref, f32[256,128]{1,0:T(8,128)S(1)} %get-tuple-element.36.inv_ref, f32[1,1024]{1,0:T(1,128)S(1)} %get-tuple-element.31.gain_ref, ...), custom_call_target="tpu_custom_call" | custom-call | flops 24379392 | bytes 4194304 | tf_op jit(solution)/shard_map/pallas_call | solution.py:32
  25.6 0.0 copy-done.4
  25.6 0.0 copy-done.6
  25.6 1.9 %collective-permute-start.3 = (f32[256,128]{1,0:T(8,128)S(1)}, f32[256,128]{1,0:T(8,128)S(1)}, u32[]{:S(2)}, u32[]{:S(2)}) collective-permute-start(f32[256,128]{1,0:T(8,128)S(1)} %get-tuple-element.43), channel_id=1, source_target_pairs={{0,1},{1,0},{2,3},{3,2},{4,5},{5,4},{6,7},{7,6},{8,9},{9,8},{10,11... | collective-permute-start | bytes 393224 | tf_op jit(solution)/shard_map/ppermute | solution.py:471
  27.5 1.3 %collective-permute-done.3.small2_ref = f32[256,128]{1,0:T(8,128)S(1)} collective-permute-done((f32[256,128]{1,0:T(8,128)S(1)}, f32[256,128]{1,0:T(8,128)S(1)}, u32[]{:S(2)}, u32[]{:S(2)}) %collective-permute-start.3) | collective-permute-done | bytes 131104 | tf_op jit(solution)/shard_map/ppermute | solution.py:471
  28.8 0.0 collective-permute-done.2.pack2_ref
  28.8 0.0 copy-done.1
  28.8 1.6 %shard_map.106 = bf16[32,136,128]{2,1,0:T(8,128)(2,1)} custom-call(bf16[512,256]{1,0:T(8,128)(2,1)S(1)} %get-tuple-element.41.mine_ref, bf16[384,1024]{1,0:T(8,128)(2,1)S(1)} %get-tuple-element.33.pack_ref, bf16[384,1024]{1,0:T(8,128)(2,1)S(1)} %collective-permute-done.2.pack2_ref, f32[256,128]{1,0:T(8,128)S(1)} %get-tuple-element.42.small_ref, ...), custom_call_target="tpu_custom_call" | custom-call | flops 536870912 | bytes 3670016 | tf_op jit(solution)/shard_map/pallas_call | solution.py:32
  30.5 0.0 copy-start
  30.5 12.7 %all-to-all-start = ((bf16[32,136,128]{2,1,0:T(8,128)(2,1)}), bf16[32,136,128]{2,1,0:T(8,128)(2,1)S(1)}, u32[]{:S(2)}, u32[]{:S(2)}) async-start(bf16[32,136,128]{2,1,0:T(8,128)(2,1)} %shard_map.106), calls=%async_computation | async-start | bytes 2228224 | tf_op jit(solution)/shard_map/all_to_all | solution.py:480
  43.2 0.0 copy-done
  43.2 0.0 copy-start.2
  43.2 1.1 %copy-done.2 = bf16[384,1024]{1,0:T(8,128)(2,1)S(1)} copy-done((bf16[384,1024]{1,0:T(8,128)(2,1)S(1)}, bf16[384,1024]{1,0:T(8,128)(2,1)}, u32[]{:S(2)}) %copy-start.2) | copy-done | bytes 786456
  44.3 0.0 copy-start.3
  44.4 1.2 %copy-done.3 = f32[256,1024]{1,0:T(8,128)S(1)} copy-done((f32[256,1024]{1,0:T(8,128)S(1)}, f32[256,1024]{1,0:T(8,128)}, u32[]{:S(2)}) %copy-start.3) | copy-done | bytes 1048600
  45.6 0.0 copy-start.5
  45.6 0.9 copy-done.5
  46.5 0.0 copy-start.7
  46.5 0.9 copy-done.7
  47.4 8.5 %shard_map.105 = (bf16[256,1024]{1,0:T(8,128)(2,1)}, bf16[256,1024]{1,0:T(8,128)(2,1)}) custom-call(bf16[384,1024]{1,0:T(8,128)(2,1)S(1)} %copy-done.2, bf16[1024,1024]{1,0:T(8,128)(2,1)S(1)} %copy-done, f32[256,1024]{1,0:T(8,128)S(1)} %copy-done.3, bf16[48,1024]{1,0:T(8,128)(2,1)S(1)} %copy-done.5, bf16[48,1024]{1,0:T(8,128)(2,1)S(1)} %copy-done.7, ...), custom_call_target="tpu_custom_call" | custom-call | flops 561250304 | bytes 3145728 | tf_op jit(solution)/shard_map/pallas_call | solution.py:32
  55.9 17.1 %all-to-all-done.landed_ref = bf16[32,136,128]{2,1,0:T(8,128)(2,1)S(1)} async-done(((bf16[32,136,128]{2,1,0:T(8,128)(2,1)}), bf16[32,136,128]{2,1,0:T(8,128)(2,1)S(1)}, u32[]{:S(2)}, u32[]{:S(2)}) %all-to-all-start) | async-done | bytes 1114144 | tf_op jit(solution)/shard_map/all_to_all | solution.py:480
  73.0 0.2 shard_map.107
  73.1 37.6 %all-gather = f32[1632,128]{1,0:T(8,128)S(1)} all-gather(f32[136,128]{1,0:T(8,128)S(1)} %shard_map.107), channel_id=2, replica_groups=mesh['dp'=12,'y'=8,'x'=4,'core'=2] {'dp'}, dimensions={0}, use_global_device_ids=true | all-gather | bytes 905216 | tf_op jit(solution)/shard_map/all_gather | solution.py:496
  110.8 0.7 shard_map.108
Async XLA Ops:
  1.6 8.4 %collective-permute-start = (bf16[48,1024]{1,0:T(8,128)(2,1)S(1)}, bf16[48,1024]{1,0:T(8,128)(2,1)S(1)}, u32[]{:S(2)}, u32[]{:S(2)}) collective-permute-start(bf16[48,1024]{1,0:T(8,128)(2,1)S(1)} %get-tuple-element.27), channel_id=1, source_target_pairs={{0,1},{1,2},{2,3},{3,4},{4,5},{5,6},{6,7},{7,8},{8,9},{9,10},{10,1... | collective-permute-start | bytes 294920 | tf_op jit(solution)/shard_map/ppermute | solution.py:394
  3.5 6.5 %collective-permute-start.1 = (bf16[48,1024]{1,0:T(8,128)(2,1)S(1)}, bf16[48,1024]{1,0:T(8,128)(2,1)S(1)}, u32[]{:S(2)}, u32[]{:S(2)}) collective-permute-start(bf16[48,1024]{1,0:T(8,128)(2,1)S(1)} %get-tuple-element.28), channel_id=1, source_target_pairs={{1,0},{2,1},{3,2},{4,3},{5,4},{6,5},{7,6},{8,7},{9,8},{10,9},{11,1... | collective-permute-start | bytes 294920 | tf_op jit(solution)/shard_map/ppermute | solution.py:394
  9.9 15.6 %copy-start.4 = (bf16[48,1024]{1,0:T(8,128)(2,1)}, bf16[48,1024]{1,0:T(8,128)(2,1)S(1)}, u32[]{:S(2)}) copy-start(bf16[48,1024]{1,0:T(8,128)(2,1)S(1)} %collective-permute-done.bef_ref) | copy-start | bytes 294916
  10.0 15.6 %copy-start.6 = (bf16[48,1024]{1,0:T(8,128)(2,1)}, bf16[48,1024]{1,0:T(8,128)(2,1)S(1)}, u32[]{:S(2)}) copy-start(bf16[48,1024]{1,0:T(8,128)(2,1)S(1)} %collective-permute-done.1.aft_ref) | copy-start | bytes 294916
  17.2 11.6 %copy-start.1 = (bf16[384,1024]{1,0:T(8,128)(2,1)}, bf16[384,1024]{1,0:T(8,128)(2,1)S(1)}, u32[]{:S(2)}) copy-start(bf16[384,1024]{1,0:T(8,128)(2,1)S(1)} %get-tuple-element.33.pack_ref) | copy-start | bytes 2359300
  17.2 11.6 %collective-permute-start.2 = (bf16[384,1024]{1,0:T(8,128)(2,1)S(1)}, bf16[384,1024]{1,0:T(8,128)(2,1)S(1)}, u32[]{:S(2)}, u32[]{:S(2)}) collective-permute-start(bf16[384,1024]{1,0:T(8,128)(2,1)S(1)} %get-tuple-element.33.pack_ref), channel_id=1, source_target_pairs={{0,1},{1,0},{2,3},{3,2},{4,5},{5,4},{6,7},{7,6},{8,9},{9,8},{10,11... | collective-permute-start | bytes 2359304 | tf_op jit(solution)/shard_map/ppermute | solution.py:455
  25.6 3.2 %collective-permute-start.3 = (f32[256,128]{1,0:T(8,128)S(1)}, f32[256,128]{1,0:T(8,128)S(1)}, u32[]{:S(2)}, u32[]{:S(2)}) collective-permute-start(f32[256,128]{1,0:T(8,128)S(1)} %get-tuple-element.43), channel_id=1, source_target_pairs={{0,1},{1,0},{2,3},{3,2},{4,5},{5,4},{6,7},{7,6},{8,9},{9,8},{10,11... | collective-permute-start | bytes 393224 | tf_op jit(solution)/shard_map/ppermute | solution.py:471
  30.5 12.7 %copy-start = (bf16[1024,1024]{1,0:T(8,128)(2,1)S(1)}, bf16[1024,1024]{1,0:T(8,128)(2,1)}, u32[]{:S(2)}) copy-start(bf16[1024,1024]{1,0:T(8,128)(2,1)} %proj_ref.1) | copy-start | bytes 6291460
  30.5 42.5 %all-to-all-start = ((bf16[32,136,128]{2,1,0:T(8,128)(2,1)}), bf16[32,136,128]{2,1,0:T(8,128)(2,1)S(1)}, u32[]{:S(2)}, u32[]{:S(2)}) async-start(bf16[32,136,128]{2,1,0:T(8,128)(2,1)} %shard_map.106), calls=%async_computation | async-start | bytes 2228224 | tf_op jit(solution)/shard_map/all_to_all | solution.py:480
  43.2 1.1 %copy-start.2 = (bf16[384,1024]{1,0:T(8,128)(2,1)S(1)}, bf16[384,1024]{1,0:T(8,128)(2,1)}, u32[]{:S(2)}) copy-start(bf16[384,1024]{1,0:T(8,128)(2,1)} %copy-done.1) | copy-start | bytes 2359300
  44.3 1.2 %copy-start.3 = (f32[256,1024]{1,0:T(8,128)S(1)}, f32[256,1024]{1,0:T(8,128)}, u32[]{:S(2)}) copy-start(f32[256,1024]{1,0:T(8,128)} %get-tuple-element.38.gm_ref) | copy-start | bytes 3145732
  45.6 0.9 copy-start.5
  46.5 0.9 copy-start.7

commit v4 on v3

--- a/solution.py
+++ b/solution.py
@@ -367,13 +367,13 @@
     total = landed_ref[0].astype(F32)
     for j in range(1, landed_ref.shape[0]):
         total = total + landed_ref[j].astype(F32)
-    out_ref[...] = total
+    out_ref[...] = total.astype(BF)
 
 
 def final_kernel(factor, taps, all_ref, weight_ref, small_ref, gain_ref):
-    total = all_ref[0]
+    total = all_ref[0].astype(F32)
     for j in range(1, all_ref.shape[0]):
-        total = total + all_ref[j]
+        total = total + all_ref[j].astype(F32)
     total = total * factor
     own, width = weight_ref.shape
     for b in range(width // LANES):
@@ -492,7 +492,7 @@
         moved=12 * length * width,
         hbm=(8,),
     )(pack, projection, grad_mixed, before, after, seg, kern, gain, frames)
-    share = call(add_kernel, shape((lines, LANES), F32), moved=80 * own * width)(landed)
+    share = call(add_kernel, shape((lines, LANES), BF), moved=80 * own * width)(landed)
     everyone = lax.all_gather(share, "dp")
     factor = 1.0 / math.sqrt(length * ny * nx * 2 * lax.axis_size("dp"))
     grad_weight, grad_kernel, grad_gain = call(

time: 112 us -> 109 us (0.973)
  the two profiles are of different devices: /device:TPU:4 before, /device:TPU:2 now
where the time goes in v4:
time: 109 us; the launch traced here: 108 us
  blocking collectives  34.5 us (32%)
  Pallas kernels  27.6 us (25%)
  starting transfers between devices  22.9 us (21%)
  waiting for transfers between devices  18.4 us (17%)
  local copies, waits for them, and re-layouts  4.16 us (4%)
    all_gather x1, blocking collectives, inner(): everyone = lax.all_gather(share, 'dp')  34.5 us
    pallas_call x8, Pallas kernels, run(): pl.pallas_call(kernel, out_shape=outs, in_specs=specs, out_specs=jax.tree...  27.6 us
    all_to_all x1, waiting for transfers between devices, inner(): lax.all_to_all(weight, ('y', 'x'), split_axis=0, concat_axis=0, tiled=True)  17.1 us
    all_to_all x1, starting transfers between devices, inner(): lax.all_to_all(weight, ('y', 'x'), split_axis=0, concat_axis=0, tiled=True)  12.4 us
    ppermute x2, starting transfers between devices, shifted(): lax.ppermute(value, SEQ, [(i, i + steps) for i in range(first, last)])  5.56 us
    unnamed x16, local copies, waits for them, and re-layouts  4.16 us
    ppermute x1, starting transfers between devices, inner(): pack2 = lax.ppermute(pack, 'core', swap)  2.97 us
  transfers between devices with their start and end apart: 5, of which 2 were waited for; matrix products, arithmetic and copies ran while one was open for 0% of the time, Pallas kernels for 16%

profile of v4, /device:TPU:2, one launch (start us, length us, event | category | flops | bytes accessed | tf_op | source)
XLA Modules:
  0.0 108.4 jit_solution(17286094018750838949)
XLA Ops:
  0.6 0.9 shard_map.102
  1.6 1.9 %collective-permute-start = (bf16[48,1024]{1,0:T(8,128)(2,1)S(1)}, bf16[48,1024]{1,0:T(8,128)(2,1)S(1)}, u32[]{:S(2)}, u32[]{:S(2)}) collective-permute-start(bf16[48,1024]{1,0:T(8,128)(2,1)S(1)} %get-tuple-element.27), channel_id=1, source_target_pairs={{0,1},{1,2},{2,3},{3,4},{4,5},{5,6},{6,7},{7,8},{8,9},{9,10},{10,1... | collective-permute-start | bytes 294920 | tf_op jit(solution)/shard_map/ppermute | solution.py:394
  3.5 3.6 %collective-permute-start.1 = (bf16[48,1024]{1,0:T(8,128)(2,1)S(1)}, bf16[48,1024]{1,0:T(8,128)(2,1)S(1)}, u32[]{:S(2)}, u32[]{:S(2)}) collective-permute-start(bf16[48,1024]{1,0:T(8,128)(2,1)S(1)} %get-tuple-element.28), channel_id=1, source_target_pairs={{1,0},{2,1},{3,2},{4,3},{5,4},{6,5},{7,6},{8,7},{9,8},{10,9},{11,1... | collective-permute-start | bytes 294920 | tf_op jit(solution)/shard_map/ppermute | solution.py:394
  7.1 2.8 %shard_map.101 = (bf16[512,256]{1,0:T(8,128)(2,1)S(1)}, bf16[512,256]{1,0:T(8,128)(2,1)S(1)}, f32[320,128]{1,0:T(8,128)S(1)}, f32[8,256,128]{2,1,0:T(8,128)S(1)}...) custom-call(s32[128,128]{1,0:T(8,128)} %bitcast.14, bf16[256,1024]{1,0:T(8,128)(2,1)} %bitcast.13, ...), custom_call_target="tpu_custom_call" | custom-call | flops 536870912 | bytes 3145728 | tf_op jit(solution)/shard_map/pallas_call | solution.py:32
  9.9 0.0 collective-permute-done.bef_ref
  9.9 0.0 copy-start.4
  9.9 0.0 collective-permute-done.1.aft_ref
  10.0 0.0 copy-start.6
  10.0 7.2 %shard_map.103 = (bf16[384,1024]{1,0:T(8,128)(2,1)S(1)}, f32[256,1024]{1,0:T(8,128)S(1)}, f32[256,128]{1,0:T(8,128)S(1)}, f32[8,320,128]{2,1,0:T(8,128)S(1)}) custom-call(f32[8,256,128]{2,1,0:T(8,128)S(1)} %get-tuple-element.26.mid_ref, bf16[48,1024]{1,0:T(8,128)(2,1)S(1)} %collective-permute-done.bef_ref, ...), custom_call_target="tpu_custom_call" | custom-call | flops 24379392 | bytes 2097152 | tf_op jit(solution)/shard_map/pallas_call | solution.py:32
  17.2 0.0 copy-start.1
  17.2 3.0 %collective-permute-start.2 = (bf16[384,1024]{1,0:T(8,128)(2,1)S(1)}, bf16[384,1024]{1,0:T(8,128)(2,1)S(1)}, u32[]{:S(2)}, u32[]{:S(2)}) collective-permute-start(bf16[384,1024]{1,0:T(8,128)(2,1)S(1)} %get-tuple-element.33.pack_ref), channel_id=1, source_target_pairs={{0,1},{1,0},{2,3},{3,2},{4,5},{5,4},{6,7},{7,6},{8,9},{9,8},{10,11... | collective-permute-start | bytes 2359304 | tf_op jit(solution)/shard_map/ppermute | solution.py:455
  20.2 5.7 %shard_map.104 = (f32[256,1024]{1,0:T(8,128)}, f32[256,128]{1,0:T(8,128)S(1)}, f32[256,128]{1,0:T(8,128)S(1)}) custom-call(f32[256,1024]{1,0:T(8,128)S(1)} %get-tuple-element.34.ga_ref, f32[256,1024]{1,0:T(8,128)S(1)} %get-tuple-element.35.norm_ref, f32[256,128]{1,0:T(8,128)S(1)} %get-tuple-element.36.inv_ref, f32[1,1024]{1,0:T(1,128)S(1)} %get-tuple-element.31.gain_ref, ...), custom_call_target="tpu_custom_call" | custom-call | flops 24379392 | bytes 4194304 | tf_op jit(solution)/shard_map/pallas_call | solution.py:32
  25.9 0.0 copy-done.4
  25.9 0.0 copy-done.6
  25.9 1.9 %collective-permute-start.3 = (f32[256,128]{1,0:T(8,128)S(1)}, f32[256,128]{1,0:T(8,128)S(1)}, u32[]{:S(2)}, u32[]{:S(2)}) collective-permute-start(f32[256,128]{1,0:T(8,128)S(1)} %get-tuple-element.43), channel_id=1, source_target_pairs={{0,1},{1,0},{2,3},{3,2},{4,5},{5,4},{6,7},{7,6},{8,9},{9,8},{10,11... | collective-permute-start | bytes 393224 | tf_op jit(solution)/shard_map/ppermute | solution.py:471
  27.8 1.3 %collective-permute-done.3.small2_ref = f32[256,128]{1,0:T(8,128)S(1)} collective-permute-done((f32[256,128]{1,0:T(8,128)S(1)}, f32[256,128]{1,0:T(8,128)S(1)}, u32[]{:S(2)}, u32[]{:S(2)}) %collective-permute-start.3) | collective-permute-done | bytes 131104 | tf_op jit(solution)/shard_map/ppermute | solution.py:471
  29.1 0.0 collective-permute-done.2.pack2_ref
  29.1 0.0 copy-done.1
  29.1 1.7 %shard_map.106 = bf16[32,136,128]{2,1,0:T(8,128)(2,1)} custom-call(bf16[512,256]{1,0:T(8,128)(2,1)S(1)} %get-tuple-element.41.mine_ref, bf16[384,1024]{1,0:T(8,128)(2,1)S(1)} %get-tuple-element.33.pack_ref, bf16[384,1024]{1,0:T(8,128)(2,1)S(1)} %collective-permute-done.2.pack2_ref, f32[256,128]{1,0:T(8,128)S(1)} %get-tuple-element.42.small_ref, ...), custom_call_target="tpu_custom_call" | custom-call | flops 536870912 | bytes 3670016 | tf_op jit(solution)/shard_map/pallas_call | solution.py:32
  30.8 0.0 copy-start
  30.8 12.4 %all-to-all-start = ((bf16[32,136,128]{2,1,0:T(8,128)(2,1)}), bf16[32,136,128]{2,1,0:T(8,128)(2,1)S(1)}, u32[]{:S(2)}, u32[]{:S(2)}) async-start(bf16[32,136,128]{2,1,0:T(8,128)(2,1)} %shard_map.106), calls=%async_computation | async-start | bytes 2228224 | tf_op jit(solution)/shard_map/all_to_all | solution.py:480
  43.2 0.0 copy-done
  43.2 0.0 copy-start.2
  43.3 1.1 %copy-done.2 = bf16[384,1024]{1,0:T(8,128)(2,1)S(1)} copy-done((bf16[384,1024]{1,0:T(8,128)(2,1)S(1)}, bf16[384,1024]{1,0:T(8,128)(2,1)}, u32[]{:S(2)}) %copy-start.2) | copy-done | bytes 786456
  44.4 0.0 copy-start.3
  44.4 1.2 %copy-done.3 = f32[256,1024]{1,0:T(8,128)S(1)} copy-done((f32[256,1024]{1,0:T(8,128)S(1)}, f32[256,1024]{1,0:T(8,128)}, u32[]{:S(2)}) %copy-start.3) | copy-done | bytes 1048600
  45.6 0.0 copy-start.5
  45.6 0.9 copy-done.5
  46.5 0.0 copy-start.7
  46.5 0.9 copy-done.7
  47.4 8.5 %shard_map.105 = (bf16[256,1024]{1,0:T(8,128)(2,1)}, bf16[256,1024]{1,0:T(8,128)(2,1)}) custom-call(bf16[384,1024]{1,0:T(8,128)(2,1)S(1)} %copy-done.2, bf16[1024,1024]{1,0:T(8,128)(2,1)S(1)} %copy-done, f32[256,1024]{1,0:T(8,128)S(1)} %copy-done.3, bf16[48,1024]{1,0:T(8,128)(2,1)S(1)} %copy-done.5, bf16[48,1024]{1,0:T(8,128)(2,1)S(1)} %copy-done.7, ...), custom_call_target="tpu_custom_call" | custom-call | flops 561250304 | bytes 3145728 | tf_op jit(solution)/shard_map/pallas_call | solution.py:32
  55.9 17.1 %all-to-all-done.landed_ref = bf16[32,136,128]{2,1,0:T(8,128)(2,1)S(1)} async-done(((bf16[32,136,128]{2,1,0:T(8,128)(2,1)}), bf16[32,136,128]{2,1,0:T(8,128)(2,1)S(1)}, u32[]{:S(2)}, u32[]{:S(2)}) %all-to-all-start) | async-done | bytes 1114144 | tf_op jit(solution)/shard_map/all_to_all | solution.py:480
  73.0 0.2 shard_map.107
  73.2 34.5 %all-gather = bf16[1632,128]{1,0:T(8,128)(2,1)S(1)} all-gather(bf16[136,128]{1,0:T(8,128)(2,1)S(1)} %shard_map.107), channel_id=2, replica_groups=mesh['dp'=12,'y'=8,'x'=4,'core'=2] {'dp'}, dimensions={0}, use_global_device_ids=true | all-gather | bytes 452608 | tf_op jit(solution)/shard_map/all_gather | solution.py:496
  107.7 0.7 shard_map.108
Async XLA Ops:
  1.6 8.4 %collective-permute-start = (bf16[48,1024]{1,0:T(8,128)(2,1)S(1)}, bf16[48,1024]{1,0:T(8,128)(2,1)S(1)}, u32[]{:S(2)}, u32[]{:S(2)}) collective-permute-start(bf16[48,1024]{1,0:T(8,128)(2,1)S(1)} %get-tuple-element.27), channel_id=1, source_target_pairs={{0,1},{1,2},{2,3},{3,4},{4,5},{5,6},{6,7},{7,8},{8,9},{9,10},{10,1... | collective-permute-start | bytes 294920 | tf_op jit(solution)/shard_map/ppermute | solution.py:394
  3.5 6.5 %collective-permute-start.1 = (bf16[48,1024]{1,0:T(8,128)(2,1)S(1)}, bf16[48,1024]{1,0:T(8,128)(2,1)S(1)}, u32[]{:S(2)}, u32[]{:S(2)}) collective-permute-start(bf16[48,1024]{1,0:T(8,128)(2,1)S(1)} %get-tuple-element.28), channel_id=1, source_target_pairs={{1,0},{2,1},{3,2},{4,3},{5,4},{6,5},{7,6},{8,7},{9,8},{10,9},{11,1... | collective-permute-start | bytes 294920 | tf_op jit(solution)/shard_map/ppermute | solution.py:394
  9.9 15.9 %copy-start.4 = (bf16[48,1024]{1,0:T(8,128)(2,1)}, bf16[48,1024]{1,0:T(8,128)(2,1)S(1)}, u32[]{:S(2)}) copy-start(bf16[48,1024]{1,0:T(8,128)(2,1)S(1)} %collective-permute-done.bef_ref) | copy-start | bytes 294916
  10.0 15.9 %copy-start.6 = (bf16[48,1024]{1,0:T(8,128)(2,1)}, bf16[48,1024]{1,0:T(8,128)(2,1)S(1)}, u32[]{:S(2)}) copy-start(bf16[48,1024]{1,0:T(8,128)(2,1)S(1)} %collective-permute-done.1.aft_ref) | copy-start | bytes 294916
  17.2 11.9 %copy-start.1 = (bf16[384,1024]{1,0:T(8,128)(2,1)}, bf16[384,1024]{1,0:T(8,128)(2,1)S(1)}, u32[]{:S(2)}) copy-start(bf16[384,1024]{1,0:T(8,128)(2,1)S(1)} %get-tuple-element.33.pack_ref) | copy-start | bytes 2359300
  17.2 11.9 %collective-permute-start.2 = (bf16[384,1024]{1,0:T(8,128)(2,1)S(1)}, bf16[384,1024]{1,0:T(8,128)(2,1)S(1)}, u32[]{:S(2)}, u32[]{:S(2)}) collective-permute-start(bf16[384,1024]{1,0:T(8,128)(2,1)S(1)} %get-tuple-element.33.pack_ref), channel_id=1, source_target_pairs={{0,1},{1,0},{2,3},{3,2},{4,5},{5,4},{6,7},{7,6},{8,9},{9,8},{10,11... | collective-permute-start | bytes 2359304 | tf_op jit(solution)/shard_map/ppermute | solution.py:455
  25.9 3.2 %collective-permute-start.3 = (f32[256,128]{1,0:T(8,128)S(1)}, f32[256,128]{1,0:T(8,128)S(1)}, u32[]{:S(2)}, u32[]{:S(2)}) collective-permute-start(f32[256,128]{1,0:T(8,128)S(1)} %get-tuple-element.43), channel_id=1, source_target_pairs={{0,1},{1,0},{2,3},{3,2},{4,5},{5,4},{6,7},{7,6},{8,9},{9,8},{10,11... | collective-permute-start | bytes 393224 | tf_op jit(solution)/shard_map/ppermute | solution.py:471
  30.8 12.5 %copy-start = (bf16[1024,1024]{1,0:T(8,128)(2,1)S(1)}, bf16[1024,1024]{1,0:T(8,128)(2,1)}, u32[]{:S(2)}) copy-start(bf16[1024,1024]{1,0:T(8,128)(2,1)} %proj_ref.1) | copy-start | bytes 6291460
  30.8 42.2 %all-to-all-start = ((bf16[32,136,128]{2,1,0:T(8,128)(2,1)}), bf16[32,136,128]{2,1,0:T(8,128)(2,1)S(1)}, u32[]{:S(2)}, u32[]{:S(2)}) async-start(bf16[32,136,128]{2,1,0:T(8,128)(2,1)} %shard_map.106), calls=%async_computation | async-start | bytes 2228224 | tf_op jit(solution)/shard_map/all_to_all | solution.py:480
  43.2 1.1 %copy-start.2 = (bf16[384,1024]{1,0:T(8,128)(2,1)S(1)}, bf16[384,1024]{1,0:T(8,128)(2,1)}, u32[]{:S(2)}) copy-start(bf16[384,1024]{1,0:T(8,128)(2,1)} %copy-done.1) | copy-start | bytes 2359300
  44.4 1.2 %copy-start.3 = (f32[256,1024]{1,0:T(8,128)S(1)}, f32[256,1024]{1,0:T(8,128)}, u32[]{:S(2)}) copy-start(f32[256,1024]{1,0:T(8,128)} %get-tuple-element.38.gm_ref) | copy-start | bytes 3145732
  45.6 0.9 copy-start.5
  46.5 0.9 copy-start.7

commit v5 on v4

--- a/solution.py
+++ b/solution.py
@@ -15,6 +15,7 @@
 NEAR = 16
 WIDE = 32
 ROWS = 32
+GROUP = 4
 BF = jnp.bfloat16
 F32 = jnp.float32
 
@@ -134,16 +135,23 @@
     matmul_into(ga_ref, ((cot_ref, proj_ref),))
 
 
-def convolved(win, wr, seg_ref, sr, kern_ref, rows):
+def convolved(win, wr, seg_ref, sr, kern_ref, rows, flipped=False):
     taps, width = kern_ref.shape
     blocks = width // LANES
     centre = seg_ref[pl.ds(sr + taps // 2, rows), :]
     acc = [jnp.zeros((rows, LANES), F32) for _ in range(blocks)]
-    for k in range(taps):
-        same = seg_ref[pl.ds(sr + k, rows), :] == centre
-        for b in range(blocks):
-            term = win[b, pl.ds(wr + k, rows), :] * kern_ref[k : k + 1, b * LANES : (b + 1) * LANES]
-            acc[b] = acc[b] + jnp.where(same, term, 0.0)
+    for g in range(0, blocks, GROUP):
+        for shift in range(8):
+            own = range(shift, taps, 8)
+            deep = rows + 8 * (len(own) - 1)
+            segs = seg_ref[pl.ds(sr + shift, deep), :]
+            wins = {b: win[b, pl.ds(wr + shift, deep), :] for b in range(g, g + GROUP)}
+            for q, k in enumerate(own):
+                same = segs[8 * q : 8 * q + rows] == centre
+                tap = taps - 1 - k if flipped else k
+                for b, lot in wins.items():
+                    term = lot[8 * q : 8 * q + rows] * kern_ref[tap : tap + 1, b * LANES : (b + 1) * LANES]
+                    acc[b] = acc[b] + jnp.where(same, term, 0.0)
     return acc
 
 
@@ -272,12 +280,17 @@
                 lanes = slice(b * LANES, (b + 1) * LANES)
                 grads[b] = inv * (gm_ref[at, lanes] - mean_a - norm_ref[at, lanes] * mean_b)
                 gm_ref[at, lanes] = grads[b]
-            for k in range(taps):
-                same = seg_ref[pl.ds(r0 + off + k, ROWS), :] == centre
-                for b, grad in grads.items():
-                    lanes = slice(b * LANES, (b + 1) * LANES)
-                    prod = jnp.where(same, win[b, pl.ds(r0 + off + k, ROWS), :], 0.0) * grad
-                    kacc[k, :, lanes] = kacc[k, :, lanes] + rows_of(prod)
+            for shift in range(8):
+                ks = range(shift, taps, 8)
+                deep = ROWS + 8 * (len(ks) - 1)
+                segs = seg_ref[pl.ds(r0 + off + shift, deep), :]
+                wins = {b: win[b, pl.ds(r0 + off + shift, deep), :] for b in grads}
+                for q, k in enumerate(ks):
+                    same = segs[8 * q : 8 * q + ROWS] == centre
+                    for b, grad in grads.items():
+                        lanes = slice(b * LANES, (b + 1) * LANES)
+                        prod = jnp.where(same, wins[b][8 * q : 8 * q + ROWS], 0.0) * grad
+                        kacc[k, :, lanes] = kacc[k, :, lanes] + rows_of(prod)
         pltpu.make_async_copy(gm_ref.at[at], gm_hbm.at[at], sems.at[i]).start()
         return carry
 
@@ -347,15 +360,7 @@
 
     def step(i, carry):
         r0 = pl.multiple_of(i * ROWS, ROWS)
-        centre = seg_ref[pl.ds(r0 + WIDE, ROWS), :]
-        acc = [jnp.zeros((ROWS, LANES), F32) for _ in range(blocks)]
-        for k in range(taps):
-            line = NEAR + reach - k
-            same = seg_ref[pl.ds(r0 + line + WIDE - NEAR, ROWS), :] == centre
-            for b in range(blocks):
-                w = kern_ref[k : k + 1, b * LANES : (b + 1) * LANES]
-                term = gwin[b, pl.ds(r0 + line, ROWS), :] * w
-                acc[b] = acc[b] + jnp.where(same, term, 0.0)
+        acc = convolved(gwin, r0 + NEAR - reach, seg_ref, r0 + WIDE - reach, kern_ref, ROWS, True)
         for b in range(blocks):
             gh_ref[pl.ds(r0, ROWS), b * LANES : (b + 1) * LANES] = acc[b].astype(BF)
         return carry
@@ -367,7 +372,9 @@
     total = landed_ref[0].astype(F32)
     for j in range(1, landed_ref.shape[0]):
         total = total + landed_ref[j].astype(F32)
-    out_ref[...] = total.astype(BF)
+    total = total.astype(BF)
+    for j in range(out_ref.shape[0]):
+        out_ref[j] = total
 
 
 def final_kernel(factor, taps, all_ref, weight_ref, small_ref, gain_ref):
@@ -386,6 +393,7 @@
 
 
 SEQ = ("y", "x", "core")
+Z = ("zfar", "znear")
 
 
 def shifted(value, steps):
@@ -492,9 +500,12 @@
         moved=12 * length * width,
         hbm=(8,),
     )(pack, projection, grad_mixed, before, after, seg, kern, gain, frames)
-    share = call(add_kernel, shape((lines, LANES), BF), moved=80 * own * width)(landed)
-    everyone = lax.all_gather(share, "dp")
-    factor = 1.0 / math.sqrt(length * ny * nx * 2 * lax.axis_size("dp"))
+    near, far = lax.axis_size("znear"), lax.axis_size("zfar")
+    copies = call(add_kernel, shape((near, lines, LANES), BF), moved=80 * own * width)(landed)
+    copies = lax.all_to_all(copies, "znear", split_axis=0, concat_axis=0, tiled=True)
+    share = call(add_kernel, shape((far, lines, LANES), BF), moved=20 * own * width)(copies)
+    everyone = lax.all_to_all(share, "zfar", split_axis=0, concat_axis=0, tiled=True)
+    factor = 1.0 / math.sqrt(length * ny * nx * 2 * near * far)
     grad_weight, grad_kernel, grad_gain = call(
         partial(final_kernel, factor, taps),
         (shape((own, width), F32), shape((own, taps), F32), shape((1, own), F32)),
@@ -505,8 +516,8 @@
 
 def solution(mesh):
     dp, seq = mesh.devices.shape
-    fine = Mesh(mesh.devices.reshape(dp, 8, seq // 16, 2), ("dp",) + SEQ)
-    rows = P("dp", SEQ, None)
-    in_specs = (rows, P("dp", None), P(), P(), P(), rows)
+    fine = Mesh(mesh.devices.reshape(dp // 4, 4, 8, seq // 16, 2), Z + SEQ)
+    rows = P(Z, SEQ, None)
+    in_specs = (rows, P(Z, None), P(), P(), P(), rows)
     out_specs = (rows, rows, P(SEQ, None), P(SEQ, None), P(SEQ))
     return jax.shard_map(inner, mesh=fine, in_specs=in_specs, out_specs=out_specs, check_vma=False)

time: 109 us -> 109 us (level)
  the two profiles are of different devices: /device:TPU:2 before, /device:TPU:8 now
where the time goes in v5:
time: 109 us
  blocking collectives  55.9 us (51%)
  Pallas kernels  26.8 us (25%)
  starting transfers between devices  23.2 us (21%)
  local copies, waits for them, and re-layouts  1.23 us (1%)
    all_to_all x1, blocking collectives, inner(): lax.all_to_all(weight, ('y', 'x'), split_axis=0, concat_axis=0, tiled=True)  42.2 us
    pallas_call x9, Pallas kernels, run(): pl.pallas_call(kernel, out_shape=outs, in_specs=specs, out_specs=jax.tree...  26.8 us
    all_to_all x1, blocking collectives, inner(): lax.all_to_all(copies, 'znear', split_axis=0, concat_axis=0, tiled=True)  13.7 us
    all_to_all x1, starting transfers between devices, inner(): lax.all_to_all(share, 'zfar', split_axis=0, concat_axis=0, tiled=True)  11.2 us
    ppermute x2, starting transfers between devices, shifted(): lax.ppermute(value, SEQ, [(i, i + steps) for i in range(first, last)])  7.67 us
    ppermute x1, starting transfers between devices, inner(): small2 = lax.ppermute(small_other, 'core', swap)  2.41 us
  transfers between devices with their start and end apart: 5, of which 1 were waited for; matrix products, arithmetic and copies ran while one was open for 0% of the time, Pallas kernels for 15%

profile of v5, /device:TPU:8, one launch (start us, length us, event | category | flops | bytes accessed | tf_op | source)
XLA Modules:
  0.0 108.9 jit_solution(6765773179888805122)
XLA Ops:
  0.6 0.9 shard_map.102
  1.6 1.9 %collective-permute-start = (bf16[48,1024]{1,0:T(8,128)(2,1)S(1)}, bf16[48,1024]{1,0:T(8,128)(2,1)S(1)}, u32[]{:S(2)}, u32[]{:S(2)}) collective-permute-start(bf16[48,1024]{1,0:T(8,128)(2,1)S(1)} %get-tuple-element.27), channel_id=1, source_target_pairs={{0,1},{1,2},{2,3},{3,4},{4,5},{5,6},{6,7},{7,8},{8,9},{9,10},{10,1... | collective-permute-start | bytes 294920 | tf_op jit(solution)/shard_map/ppermute | solution.py:402
  3.5 5.8 %collective-permute-start.1 = (bf16[48,1024]{1,0:T(8,128)(2,1)S(1)}, bf16[48,1024]{1,0:T(8,128)(2,1)S(1)}, u32[]{:S(2)}, u32[]{:S(2)}) collective-permute-start(bf16[48,1024]{1,0:T(8,128)(2,1)S(1)} %get-tuple-element.28), channel_id=1, source_target_pairs={{1,0},{2,1},{3,2},{4,3},{5,4},{6,5},{7,6},{8,7},{9,8},{10,9},{11,1... | collective-permute-start | bytes 294920 | tf_op jit(solution)/shard_map/ppermute | solution.py:402
  9.3 2.8 %shard_map.101 = (bf16[512,256]{1,0:T(8,128)(2,1)S(1)}, bf16[512,256]{1,0:T(8,128)(2,1)S(1)}, f32[320,128]{1,0:T(8,128)S(1)}, f32[8,256,128]{2,1,0:T(8,128)S(1)}...) custom-call(s32[128,128]{1,0:T(8,128)} %bitcast.12, bf16[256,1024]{1,0:T(8,128)(2,1)} %bitcast.11, ...), custom_call_target="tpu_custom_call" | custom-call | flops 536870912 | bytes 3145728 | tf_op jit(solution)/shard_map/pallas_call | solution.py:33
  12.0 0.0 collective-permute-done.bef_ref
  12.0 0.0 collective-permute-done.1.aft_ref
  12.1 6.5 %shard_map.103 = (bf16[384,1024]{1,0:T(8,128)(2,1)S(1)}, f32[256,1024]{1,0:T(8,128)S(1)}, f32[256,128]{1,0:T(8,128)S(1)}, f32[8,320,128]{2,1,0:T(8,128)S(1)}) custom-call(f32[8,256,128]{2,1,0:T(8,128)S(1)} %get-tuple-element.26.mid_ref, bf16[48,1024]{1,0:T(8,128)(2,1)S(1)} %collective-permute-done.bef_ref, ...), custom_call_target="tpu_custom_call" | custom-call | flops 24379392 | bytes 2097152 | tf_op jit(solution)/shard_map/pallas_call | solution.py:33
  18.6 1.9 %collective-permute-start.2 = (bf16[384,1024]{1,0:T(8,128)(2,1)S(1)}, bf16[384,1024]{1,0:T(8,128)(2,1)S(1)}, u32[]{:S(2)}, u32[]{:S(2)}) collective-permute-start(bf16[384,1024]{1,0:T(8,128)(2,1)S(1)} %get-tuple-element.33.pack_ref), channel_id=1, source_target_pairs={{0,1},{1,0},{2,3},{3,2},{4,5},{5,4},{6,7},{7,6},{8,9},{9,8},{10,11... | collective-permute-start | bytes 2359304 | tf_op jit(solution)/shard_map/ppermute | solution.py:463
  20.5 5.2 %shard_map.104 = (f32[256,1024]{1,0:T(8,128)}, f32[256,128]{1,0:T(8,128)S(1)}, f32[256,128]{1,0:T(8,128)S(1)}) custom-call(f32[256,1024]{1,0:T(8,128)S(1)} %get-tuple-element.34.ga_ref, f32[256,1024]{1,0:T(8,128)S(1)} %get-tuple-element.35.norm_ref, f32[256,128]{1,0:T(8,128)S(1)} %get-tuple-element.36.inv_ref, f32[1,1024]{1,0:T(1,128)S(1)} %get-tuple-element.31.gain_ref, ...), custom_call_target="tpu_custom_call" | custom-call | flops 24379392 | bytes 4194304 | tf_op jit(solution)/shard_map/pallas_call | solution.py:33
  25.7 2.4 %collective-permute-start.3 = (f32[256,128]{1,0:T(8,128)S(1)}, f32[256,128]{1,0:T(8,128)S(1)}, u32[]{:S(2)}, u32[]{:S(2)}) collective-permute-start(f32[256,128]{1,0:T(8,128)S(1)} %get-tuple-element.43), channel_id=1, source_target_pairs={{0,1},{1,0},{2,3},{3,2},{4,5},{5,4},{6,7},{7,6},{8,9},{9,8},{10,11... | collective-permute-start | bytes 393224 | tf_op jit(solution)/shard_map/ppermute | solution.py:479
  28.1 1.0 collective-permute-done.3.small2_ref
  29.1 0.0 collective-permute-done.2.pack2_ref
  29.1 1.6 %shard_map.106 = bf16[32,136,128]{2,1,0:T(8,128)(2,1)} custom-call(bf16[512,256]{1,0:T(8,128)(2,1)S(1)} %get-tuple-element.41.mine_ref, bf16[384,1024]{1,0:T(8,128)(2,1)S(1)} %get-tuple-element.33.pack_ref, bf16[384,1024]{1,0:T(8,128)(2,1)S(1)} %collective-permute-done.2.pack2_ref, f32[256,128]{1,0:T(8,128)S(1)} %get-tuple-element.42.small_ref, ...), custom_call_target="tpu_custom_call" | custom-call | flops 536870912 | bytes 3670016 | tf_op jit(solution)/shard_map/pallas_call | solution.py:33
  30.7 0.0 copy-start
  30.8 42.2 %all_to_all.15.landed_ref = bf16[32,136,128]{2,1,0:T(8,128)(2,1)S(1)} all-to-all(bf16[32,136,128]{2,1,0:T(8,128)(2,1)} %shard_map.106), channel_id=1, replica_groups=mesh['zfar'=3,'znear'=4,'y'=8,'x'=4,'core'=2] {'y','x'}, dimensions={0} | all-to-all | bytes 2228224 | tf_op jit(solution)/shard_map/all_to_all | solution.py:488
  73.0 0.2 shard_map.107
  73.2 13.7 %all_to_all.16.landed_ref = bf16[4,136,128]{2,1,0:T(8,128)(2,1)S(1)} all-to-all(bf16[4,136,128]{2,1,0:T(8,128)(2,1)S(1)} %shard_map.107), channel_id=1, replica_groups=mesh['zfar'=3,'znear'=4,'y'=8,'x'=4,'core'=2] {'znear'}, dimensions={0} | all-to-all | bytes 278528 | tf_op jit(solution)/shard_map/all_to_all | solution.py:505
  86.8 0.7 shard_map.108
  87.5 11.2 %all-to-all-start.2 = ((bf16[3,136,128]{2,1,0:T(8,128)(2,1)}), bf16[3,136,128]{2,1,0:T(8,128)(2,1)S(1)}, u32[]{:S(2)}, u32[]{:S(2)}) async-start(bf16[3,136,128]{2,1,0:T(8,128)(2,1)} %shard_map.108), calls=%async_computation.2 | async-start | bytes 208896 | tf_op jit(solution)/shard_map/all_to_all | solution.py:507
  98.7 0.0 copy-done
  98.7 0.0 copy-start.1
  98.7 1.2 %copy-done.1 = f32[256,1024]{1,0:T(8,128)S(1)} copy-done((f32[256,1024]{1,0:T(8,128)S(1)}, f32[256,1024]{1,0:T(8,128)}, u32[]{:S(2)}) %copy-start.1) | copy-done | bytes 1048600
  100.0 8.2 %shard_map.105 = (bf16[256,1024]{1,0:T(8,128)(2,1)}, bf16[256,1024]{1,0:T(8,128)(2,1)}) custom-call(bf16[384,1024]{1,0:T(8,128)(2,1)S(1)} %get-tuple-element.33.pack_ref, bf16[1024,1024]{1,0:T(8,128)(2,1)S(1)} %copy-done, f32[256,1024]{1,0:T(8,128)S(1)} %copy-done.1, bf16[48,1024]{1,0:T(8,128)(2,1)S(1)} %collective-permute-done.bef_ref, ...), custom_call_target="tpu_custom_call" | custom-call | flops 561250304 | bytes 3145728 | tf_op jit(solution)/shard_map/pallas_call | solution.py:33
  108.2 0.0 all-to-all-done.2.all_ref
  108.2 0.7 shard_map.109
Async XLA Ops:
  1.6 10.5 %collective-permute-start = (bf16[48,1024]{1,0:T(8,128)(2,1)S(1)}, bf16[48,1024]{1,0:T(8,128)(2,1)S(1)}, u32[]{:S(2)}, u32[]{:S(2)}) collective-permute-start(bf16[48,1024]{1,0:T(8,128)(2,1)S(1)} %get-tuple-element.27), channel_id=1, source_target_pairs={{0,1},{1,2},{2,3},{3,4},{4,5},{5,6},{6,7},{7,8},{8,9},{9,10},{10,1... | collective-permute-start | bytes 294920 | tf_op jit(solution)/shard_map/ppermute | solution.py:402
  3.5 8.5 %collective-permute-start.1 = (bf16[48,1024]{1,0:T(8,128)(2,1)S(1)}, bf16[48,1024]{1,0:T(8,128)(2,1)S(1)}, u32[]{:S(2)}, u32[]{:S(2)}) collective-permute-start(bf16[48,1024]{1,0:T(8,128)(2,1)S(1)} %get-tuple-element.28), channel_id=1, source_target_pairs={{1,0},{2,1},{3,2},{4,3},{5,4},{6,5},{7,6},{8,7},{9,8},{10,9},{11,1... | collective-permute-start | bytes 294920 | tf_op jit(solution)/shard_map/ppermute | solution.py:402
  18.6 10.5 %collective-permute-start.2 = (bf16[384,1024]{1,0:T(8,128)(2,1)S(1)}, bf16[384,1024]{1,0:T(8,128)(2,1)S(1)}, u32[]{:S(2)}, u32[]{:S(2)}) collective-permute-start(bf16[384,1024]{1,0:T(8,128)(2,1)S(1)} %get-tuple-element.33.pack_ref), channel_id=1, source_target_pairs={{0,1},{1,0},{2,3},{3,2},{4,5},{5,4},{6,7},{7,6},{8,9},{9,8},{10,11... | collective-permute-start | bytes 2359304 | tf_op jit(solution)/shard_map/ppermute | solution.py:463
  25.7 3.4 %collective-permute-start.3 = (f32[256,128]{1,0:T(8,128)S(1)}, f32[256,128]{1,0:T(8,128)S(1)}, u32[]{:S(2)}, u32[]{:S(2)}) collective-permute-start(f32[256,128]{1,0:T(8,128)S(1)} %get-tuple-element.43), channel_id=1, source_target_pairs={{0,1},{1,0},{2,3},{3,2},{4,5},{5,4},{6,7},{7,6},{8,9},{9,8},{10,11... | collective-permute-start | bytes 393224 | tf_op jit(solution)/shard_map/ppermute | solution.py:479
  30.7 68.0 %copy-start = (bf16[1024,1024]{1,0:T(8,128)(2,1)S(1)}, bf16[1024,1024]{1,0:T(8,128)(2,1)}, u32[]{:S(2)}) copy-start(bf16[1024,1024]{1,0:T(8,128)(2,1)} %proj_ref.1) | copy-start | bytes 6291460
  87.5 20.7 %all-to-all-start.2 = ((bf16[3,136,128]{2,1,0:T(8,128)(2,1)}), bf16[3,136,128]{2,1,0:T(8,128)(2,1)S(1)}, u32[]{:S(2)}, u32[]{:S(2)}) async-start(bf16[3,136,128]{2,1,0:T(8,128)(2,1)} %shard_map.108), calls=%async_computation.2 | async-start | bytes 208896 | tf_op jit(solution)/shard_map/all_to_all | solution.py:507
  98.7 1.2 %copy-start.1 = (f32[256,1024]{1,0:T(8,128)S(1)}, f32[256,1024]{1,0:T(8,128)}, u32[]{:S(2)}) copy-start(f32[256,1024]{1,0:T(8,128)} %get-tuple-element.38.gm_ref) | copy-start | bytes 3145732

commit v6 on v5

--- a/solution.py
+++ b/solution.py
@@ -75,19 +75,25 @@
         out_ref[:, at] = total.astype(out_ref.dtype)
 
 
-def ends_kernel(hid_hbm, cot_hbm, up_ref, down_ref, sems):
+def ends_kernel(hid_hbm, cot_hbm, mate_ref, outer_ref, sems):
     length = hid_hbm.shape[0]
-    pairs = (
-        (hid_hbm.at[length - WIDE : length], up_ref.at[0:WIDE]),
-        (cot_hbm.at[length - NEAR : length], up_ref.at[WIDE : WIDE + NEAR]),
-        (hid_hbm.at[0:WIDE], down_ref.at[0:WIDE]),
-        (cot_hbm.at[0:NEAR], down_ref.at[WIDE : WIDE + NEAR]),
-    )
-    copies = [pltpu.make_async_copy(src, dst, sems.at[i]) for i, (src, dst) in enumerate(pairs)]
+    core = lax.axis_index("core")
+    copies = []
+    for end, dst in ((core == 0, mate_ref), (core == 1, outer_ref)):
+        for src, rows, to in ((hid_hbm, WIDE, 0), (cot_hbm, NEAR, WIDE)):
+            at = pl.multiple_of(jnp.where(end, length - rows, 0), NEAR)
+            copies.append(
+                pltpu.make_async_copy(src.at[pl.ds(at, rows)], dst.at[to : to + rows], sems.at[len(copies)])
+            )
     for copy in copies:
         copy.start()
     for copy in copies:
         copy.wait()
+
+
+def sorted_ends(mate, outer):
+    core = lax.axis_index("core")
+    return jnp.where(core == 0, outer, mate), jnp.where(core == 0, mate, outer)
 
 
 def first_kernel(
@@ -176,16 +182,17 @@
 
 
 def forward_kernel(
-    mid_ref, bef_ref, aft_ref, seg_ref, kern_ref, gain_ref, other_ref, pack_ref, norm_ref, inv_ref, win
+    mid_ref, mate_ref, outer_ref, seg_ref, kern_ref, gain_ref, other_ref, pack_ref, norm_ref, inv_ref, win
 ):
     taps, width = kern_ref.shape
     length = norm_ref.shape[0]
     blocks = width // LANES
     for b in range(blocks):
         lanes = slice(b * LANES, (b + 1) * LANES)
-        win[b, 0:WIDE, :] = bef_ref[0:WIDE, lanes].astype(F32)
+        before, after = sorted_ends(mate_ref[0:WIDE, lanes].astype(F32), outer_ref[0:WIDE, lanes].astype(F32))
+        win[b, 0:WIDE, :] = before
         win[b, WIDE : WIDE + length, :] = mid_ref[b]
-        win[b, WIDE + length :, :] = aft_ref[0:WIDE, lanes].astype(F32)
+        win[b, WIDE + length :, :] = after
     for j in range(width // length):
         rows = other_ref.shape[0] * length // width
         pack_ref[length:, j * length : (j + 1) * length] = other_ref[j * rows : (j + 1) * rows, :]
@@ -317,7 +324,7 @@
 
 
 def back_kernel(
-    pack_ref, proj_ref, gm_ref, bef_ref, aft_ref, seg_ref, kern_ref, gain_ref, hid_hbm,
+    pack_ref, proj_ref, gm_ref, mate_ref, outer_ref, seg_ref, kern_ref, gain_ref, hid_hbm,
     out_ref, gh_ref, gwin, hwin, hid_ref, ga_ref, sems,
 ):
     taps, width = kern_ref.shape
@@ -330,29 +337,31 @@
     for copy in copies:
         copy.start()
     matmul_into(out_ref, ((pack_ref.at[0:length], proj_ref),), transposed=True)
-    matmul_into(ga_ref.at[0:NEAR], ((bef_ref.at[WIDE:], proj_ref),))
-    matmul_into(ga_ref.at[NEAR:], ((aft_ref.at[WIDE:], proj_ref),))
+    matmul_into(ga_ref.at[0:NEAR], ((mate_ref.at[WIDE:], proj_ref),))
+    matmul_into(ga_ref.at[NEAR:], ((outer_ref.at[WIDE:], proj_ref),))
     for copy in copies:
         copy.wait()
     for b in range(blocks):
         lanes = slice(b * LANES, (b + 1) * LANES)
         gwin[b, NEAR : NEAR + length, :] = gm_ref[:, lanes]
-        hwin[b, 0:WIDE, :] = bef_ref[0:WIDE, lanes].astype(F32)
+        before, after = sorted_ends(mate_ref[0:WIDE, lanes].astype(F32), outer_ref[0:WIDE, lanes].astype(F32))
+        hwin[b, 0:WIDE, :] = before
         hwin[b, WIDE : 2 * WIDE, :] = hid_ref[0, :, lanes].astype(F32)
         hwin[b, 2 * WIDE : 3 * WIDE, :] = hid_ref[1, :, lanes].astype(F32)
-        hwin[b, 3 * WIDE :, :] = aft_ref[0:WIDE, lanes].astype(F32)
+        hwin[b, 3 * WIDE :, :] = after
     reach = taps // 2
     sides = (
-        (NEAR - reach, NEAR - reach, 0, 0),
-        (3 * WIDE - reach, WIDE + length - reach, NEAR, NEAR + length),
+        (NEAR - reach, NEAR - reach, 0),
+        (3 * WIDE - reach, WIDE + length - reach, NEAR + length),
     )
-    for wr, sr, ar, to in sides:
+    for side, (wr, sr, to) in enumerate(sides):
         normed, inv = normalised(convolved(hwin, wr, seg_ref, sr, kern_ref, NEAR), width)
         grads = []
         for b in range(blocks):
             lanes = slice(b * LANES, (b + 1) * LANES)
             gain = gain_ref[:, lanes]
-            grads.append(gate_back(ga_ref[ar : ar + NEAR, lanes], normed[b], gain) * gain)
+            grad = sorted_ends(ga_ref[0:NEAR, lanes], ga_ref[NEAR:, lanes])[side]
+            grads.append(gate_back(grad, normed[b], gain) * gain)
         mean_a = mean_of(grads, width)
         mean_b = mean_of([g * n for g, n in zip(grads, normed)], width)
         for b in range(blocks):
@@ -372,9 +381,7 @@
     total = landed_ref[0].astype(F32)
     for j in range(1, landed_ref.shape[0]):
         total = total + landed_ref[j].astype(F32)
-    total = total.astype(BF)
-    for j in range(out_ref.shape[0]):
-        out_ref[j] = total
+    out_ref[...] = total.astype(BF)
 
 
 def final_kernel(factor, taps, all_ref, weight_ref, small_ref, gain_ref):
@@ -393,13 +400,6 @@
 
 
 SEQ = ("y", "x", "core")
-Z = ("zfar", "znear")
-
-
-def shifted(value, steps):
-    count = lax.axis_size("y") * lax.axis_size("x") * lax.axis_size("core")
-    first, last = max(0, -steps), min(count, count - steps)
-    return lax.ppermute(value, SEQ, [(i, i + steps) for i in range(first, last)])
 
 
 def inner(hidden, segment_ids, kernel, norm_gain, projection, cotangent):
@@ -408,7 +408,8 @@
     taps = kernel.shape[0]
     cot = cotangent[0]
     ny, nx = lax.axis_size("y"), lax.axis_size("x")
-    own = width // (ny * nx * 2)
+    seqs = ny * nx * 2
+    own = width // seqs
     swap = [(0, 1), (1, 0)]
     big = 2 * length * width * width
     vec = length * width * taps
@@ -419,11 +420,11 @@
     lines = (blocks * own) + own // 2
 
     message = shape((WIDE + NEAR, width), BF)
-    up, down = call(
+    to_mate, to_outer = call(
         ends_kernel, (message, message), [pltpu.SemaphoreType.DMA((4,))], moved=512 * width, hbm=(0, 1)
     )(frames, cot)
-    before = shifted(up, 1)
-    after = shifted(down, -1)
+    mate = lax.ppermute(to_mate, "core", swap)
+    outer = lax.ppermute(to_outer, SEQ, [(i, i + 1 if i % 2 else i - 1) for i in range(1, seqs - 1)])
     half = shape((width // 2, length), BF)
     ids = segment_ids.reshape(-1, LANES)
     mine, other, seg, mid, grad_act, kern, gain = call(
@@ -459,7 +460,7 @@
         flops=3 * vec,
         moved=8 * length * width,
         trans=2 * length * width,
-    )(mid, before, after, seg, kern, gain, other)
+    )(mid, mate, outer, seg, kern, gain, other)
     pack2 = lax.ppermute(pack, "core", swap)
     dealt = shape((width // 4, LANES), F32)
     grad_mixed, small, small_other = call(
@@ -499,13 +500,10 @@
         flops=3 * vec + big,
         moved=12 * length * width,
         hbm=(8,),
-    )(pack, projection, grad_mixed, before, after, seg, kern, gain, frames)
-    near, far = lax.axis_size("znear"), lax.axis_size("zfar")
-    copies = call(add_kernel, shape((near, lines, LANES), BF), moved=80 * own * width)(landed)
-    copies = lax.all_to_all(copies, "znear", split_axis=0, concat_axis=0, tiled=True)
-    share = call(add_kernel, shape((far, lines, LANES), BF), moved=20 * own * width)(copies)
-    everyone = lax.all_to_all(share, "zfar", split_axis=0, concat_axis=0, tiled=True)
-    factor = 1.0 / math.sqrt(length * ny * nx * 2 * near * far)
+    )(pack, projection, grad_mixed, mate, outer, seg, kern, gain, frames)
+    share = call(add_kernel, shape((lines, LANES), BF), moved=80 * own * width)(landed)
+    everyone = lax.all_gather(share, "dp")
+    factor = 1.0 / math.sqrt(length * ny * nx * 2 * lax.axis_size("dp"))
     grad_weight, grad_kernel, grad_gain = call(
         partial(final_kernel, factor, taps),
         (shape((own, width), F32), shape((own, taps), F32), shape((1, own), F32)),
@@ -516,8 +514,8 @@
 
 def solution(mesh):
     dp, seq = mesh.devices.shape
-    fine = Mesh(mesh.devices.reshape(dp // 4, 4, 8, seq // 16, 2), Z + SEQ)
-    rows = P(Z, SEQ, None)
-    in_specs = (rows, P(Z, None), P(), P(), P(), rows)
+    fine = Mesh(mesh.devices.reshape(dp, 8, seq // 16, 2), ("dp",) + SEQ)
+    rows = P("dp", SEQ, None)
+    in_specs = (rows, P("dp", None), P(), P(), P(), rows)
     out_specs = (rows, rows, P(SEQ, None), P(SEQ, None), P(SEQ))
     return jax.shard_map(inner, mesh=fine, in_specs=in_specs, out_specs=out_specs, check_vma=False)

time: 109 us -> 106 us (0.972)
  the two profiles are of different devices: /device:TPU:8 before, /device:TPU:2 now
where the time goes in v6:
time: 106 us
  blocking collectives  33.8 us (32%)
  Pallas kernels  26.2 us (25%)
  starting transfers between devices  22.9 us (22%)
  waiting for transfers between devices  18 us (17%)
  local copies, waits for them, and re-layouts  4.16 us (4%)
    all_gather x1, blocking collectives, inner(): everyone = lax.all_gather(share, 'dp')  33.8 us
    pallas_call x8, Pallas kernels, run(): pl.pallas_call(kernel, out_shape=outs, in_specs=specs, out_specs=jax.tree...  26.2 us
    all_to_all x1, waiting for transfers between devices, inner(): lax.all_to_all(weight, ('y', 'x'), split_axis=0, concat_axis=0, tiled=True)  17.1 us
    ppermute x1, starting transfers between devices, inner(): lax.ppermute(to_outer, SEQ, [(i, i + 1 if i % 2 else i - 1) for i in rang...  11.5 us
    all_to_all x1, starting transfers between devices, inner(): lax.all_to_all(weight, ('y', 'x'), split_axis=0, concat_axis=0, tiled=True)  5.17 us
    unnamed x16, local copies, waits for them, and re-layouts  4.16 us
    ppermute x1, starting transfers between devices, inner(): small2 = lax.ppermute(small_other, 'core', swap)  2.41 us
  transfers between devices with their start and end apart: 5, of which 2 were waited for; matrix products, arithmetic and copies ran while one was open for 0% of the time, Pallas kernels for 15%

profile of v6, /device:TPU:2, one launch (start us, length us, event | category | flops | bytes accessed | tf_op | source)
XLA Modules:
  0.0 105.9 jit_solution(9880116560195190395)
XLA Ops:
  0.6 0.9 shard_map.102
  1.6 1.9 %collective-permute-start = (bf16[48,1024]{1,0:T(8,128)(2,1)S(1)}, bf16[48,1024]{1,0:T(8,128)(2,1)S(1)}, u32[]{:S(2)}, u32[]{:S(2)}) collective-permute-start(bf16[48,1024]{1,0:T(8,128)(2,1)S(1)} %get-tuple-element.27), channel_id=1, source_target_pairs={{0,1},{1,0},{2,3},{3,2},{4,5},{5,4},{6,7},{7,6},{8,9},{9,8},{10,11... | collective-permute-start | bytes 294920 | tf_op jit(solution)/shard_map/ppermute | solution.py:426
  3.5 11.5 %collective-permute-start.1 = (bf16[48,1024]{1,0:T(8,128)(2,1)S(1)}, bf16[48,1024]{1,0:T(8,128)(2,1)S(1)}, u32[]{:S(2)}, u32[]{:S(2)}) collective-permute-start(bf16[48,1024]{1,0:T(8,128)(2,1)S(1)} %get-tuple-element.28), channel_id=1, source_target_pairs={{1,2},{2,1},{3,4},{4,3},{5,6},{6,5},{7,8},{8,7},{9,10},{10,9},{11,... | collective-permute-start | bytes 294920 | tf_op jit(solution)/shard_map/ppermute | solution.py:427
  15.0 2.8 %shard_map.101 = (bf16[512,256]{1,0:T(8,128)(2,1)S(1)}, bf16[512,256]{1,0:T(8,128)(2,1)S(1)}, f32[320,128]{1,0:T(8,128)S(1)}, f32[8,256,128]{2,1,0:T(8,128)S(1)}...) custom-call(s32[128,128]{1,0:T(8,128)} %bitcast.14, bf16[256,1024]{1,0:T(8,128)(2,1)} %bitcast.13, ...), custom_call_target="tpu_custom_call" | custom-call | flops 536870912 | bytes 3145728 | tf_op jit(solution)/shard_map/pallas_call | solution.py:33
  17.8 0.0 collective-permute-done.mate_ref
  17.8 0.0 copy-start.4
  17.8 0.0 collective-permute-done.1.outer_ref
  17.9 0.0 copy-start.6
  17.9 6.5 %shard_map.103 = (bf16[384,1024]{1,0:T(8,128)(2,1)S(1)}, f32[256,1024]{1,0:T(8,128)S(1)}, f32[256,128]{1,0:T(8,128)S(1)}, f32[8,320,128]{2,1,0:T(8,128)S(1)}) custom-call(f32[8,256,128]{2,1,0:T(8,128)S(1)} %get-tuple-element.26.mid_ref, bf16[48,1024]{1,0:T(8,128)(2,1)S(1)} %collective-permute-done.mate_ref, ...), custom_call_target="tpu_custom_call" | custom-call | flops 24379392 | bytes 2097152 | tf_op jit(solution)/shard_map/pallas_call | solution.py:33
  24.4 0.0 copy-start.1
  24.4 1.9 %collective-permute-start.2 = (bf16[384,1024]{1,0:T(8,128)(2,1)S(1)}, bf16[384,1024]{1,0:T(8,128)(2,1)S(1)}, u32[]{:S(2)}, u32[]{:S(2)}) collective-permute-start(bf16[384,1024]{1,0:T(8,128)(2,1)S(1)} %get-tuple-element.33.pack_ref), channel_id=1, source_target_pairs={{0,1},{1,0},{2,3},{3,2},{4,5},{5,4},{6,7},{7,6},{8,9},{9,8},{10,11... | collective-permute-start | bytes 2359304 | tf_op jit(solution)/shard_map/ppermute | solution.py:464
  26.3 5.2 %shard_map.104 = (f32[256,1024]{1,0:T(8,128)}, f32[256,128]{1,0:T(8,128)S(1)}, f32[256,128]{1,0:T(8,128)S(1)}) custom-call(f32[256,1024]{1,0:T(8,128)S(1)} %get-tuple-element.34.ga_ref, f32[256,1024]{1,0:T(8,128)S(1)} %get-tuple-element.35.norm_ref, f32[256,128]{1,0:T(8,128)S(1)} %get-tuple-element.36.inv_ref, f32[1,1024]{1,0:T(1,128)S(1)} %get-tuple-element.31.gain_ref, ...), custom_call_target="tpu_custom_call" | custom-call | flops 24379392 | bytes 4194304 | tf_op jit(solution)/shard_map/pallas_call | solution.py:33
  31.5 0.0 copy-done.4
  31.5 0.0 copy-done.6
  31.5 2.4 %collective-permute-start.3 = (f32[256,128]{1,0:T(8,128)S(1)}, f32[256,128]{1,0:T(8,128)S(1)}, u32[]{:S(2)}, u32[]{:S(2)}) collective-permute-start(f32[256,128]{1,0:T(8,128)S(1)} %get-tuple-element.43), channel_id=1, source_target_pairs={{0,1},{1,0},{2,3},{3,2},{4,5},{5,4},{6,7},{7,6},{8,9},{9,8},{10,11... | collective-permute-start | bytes 393224 | tf_op jit(solution)/shard_map/ppermute | solution.py:480
  34.0 1.0 collective-permute-done.3.small2_ref
  34.9 0.0 collective-permute-done.2.pack2_ref
  34.9 0.0 copy-done.1
  34.9 1.6 %shard_map.106 = bf16[32,136,128]{2,1,0:T(8,128)(2,1)} custom-call(bf16[512,256]{1,0:T(8,128)(2,1)S(1)} %get-tuple-element.41.mine_ref, bf16[384,1024]{1,0:T(8,128)(2,1)S(1)} %get-tuple-element.33.pack_ref, bf16[384,1024]{1,0:T(8,128)(2,1)S(1)} %collective-permute-done.2.pack2_ref, f32[256,128]{1,0:T(8,128)S(1)} %get-tuple-element.42.small_ref, ...), custom_call_target="tpu_custom_call" | custom-call | flops 536870912 | bytes 3670016 | tf_op jit(solution)/shard_map/pallas_call | solution.py:33
  36.6 0.0 copy-start
  36.6 5.2 %all-to-all-start = ((bf16[32,136,128]{2,1,0:T(8,128)(2,1)}), bf16[32,136,128]{2,1,0:T(8,128)(2,1)S(1)}, u32[]{:S(2)}, u32[]{:S(2)}) async-start(bf16[32,136,128]{2,1,0:T(8,128)(2,1)} %shard_map.106), calls=%async_computation | async-start | bytes 2228224 | tf_op jit(solution)/shard_map/all_to_all | solution.py:489
  41.8 0.0 copy-done
  41.8 0.0 copy-start.2
  41.8 1.1 %copy-done.2 = bf16[384,1024]{1,0:T(8,128)(2,1)S(1)} copy-done((bf16[384,1024]{1,0:T(8,128)(2,1)S(1)}, bf16[384,1024]{1,0:T(8,128)(2,1)}, u32[]{:S(2)}) %copy-start.2) | copy-done | bytes 786456
  42.9 0.0 copy-start.3
  42.9 1.2 %copy-done.3 = f32[256,1024]{1,0:T(8,128)S(1)} copy-done((f32[256,1024]{1,0:T(8,128)S(1)}, f32[256,1024]{1,0:T(8,128)}, u32[]{:S(2)}) %copy-start.3) | copy-done | bytes 1048600
  44.1 0.0 copy-start.5
  44.2 0.9 copy-done.5
  45.0 0.0 copy-start.7
  45.0 0.9 copy-done.7
  45.9 8.3 %shard_map.105 = (bf16[256,1024]{1,0:T(8,128)(2,1)}, bf16[256,1024]{1,0:T(8,128)(2,1)}) custom-call(bf16[384,1024]{1,0:T(8,128)(2,1)S(1)} %copy-done.2, bf16[1024,1024]{1,0:T(8,128)(2,1)S(1)} %copy-done, f32[256,1024]{1,0:T(8,128)S(1)} %copy-done.3, bf16[48,1024]{1,0:T(8,128)(2,1)S(1)} %copy-done.5, bf16[48,1024]{1,0:T(8,128)(2,1)S(1)} %copy-done.7, ...), custom_call_target="tpu_custom_call" | custom-call | flops 561250304 | bytes 3145728 | tf_op jit(solution)/shard_map/pallas_call | solution.py:33
  54.2 17.1 %all-to-all-done.landed_ref = bf16[32,136,128]{2,1,0:T(8,128)(2,1)S(1)} async-done(((bf16[32,136,128]{2,1,0:T(8,128)(2,1)}), bf16[32,136,128]{2,1,0:T(8,128)(2,1)S(1)}, u32[]{:S(2)}, u32[]{:S(2)}) %all-to-all-start) | async-done | bytes 1114144 | tf_op jit(solution)/shard_map/all_to_all | solution.py:489
  71.3 0.2 shard_map.107
  71.4 33.8 %all-gather = bf16[1632,128]{1,0:T(8,128)(2,1)S(1)} all-gather(bf16[136,128]{1,0:T(8,128)(2,1)S(1)} %shard_map.107), channel_id=2, replica_groups=mesh['dp'=12,'y'=8,'x'=4,'core'=2] {'dp'}, dimensions={0}, use_global_device_ids=true | all-gather | bytes 452608 | tf_op jit(solution)/shard_map/all_gather | solution.py:505
  105.2 0.7 shard_map.108
Async XLA Ops:
  1.6 16.2 %collective-permute-start = (bf16[48,1024]{1,0:T(8,128)(2,1)S(1)}, bf16[48,1024]{1,0:T(8,128)(2,1)S(1)}, u32[]{:S(2)}, u32[]{:S(2)}) collective-permute-start(bf16[48,1024]{1,0:T(8,128)(2,1)S(1)} %get-tuple-element.27), channel_id=1, source_target_pairs={{0,1},{1,0},{2,3},{3,2},{4,5},{5,4},{6,7},{7,6},{8,9},{9,8},{10,11... | collective-permute-start | bytes 294920 | tf_op jit(solution)/shard_map/ppermute | solution.py:426
  3.5 14.3 %collective-permute-start.1 = (bf16[48,1024]{1,0:T(8,128)(2,1)S(1)}, bf16[48,1024]{1,0:T(8,128)(2,1)S(1)}, u32[]{:S(2)}, u32[]{:S(2)}) collective-permute-start(bf16[48,1024]{1,0:T(8,128)(2,1)S(1)} %get-tuple-element.28), channel_id=1, source_target_pairs={{1,2},{2,1},{3,4},{4,3},{5,6},{6,5},{7,8},{8,7},{9,10},{10,9},{11,... | collective-permute-start | bytes 294920 | tf_op jit(solution)/shard_map/ppermute | solution.py:427
  17.8 13.7 %copy-start.4 = (bf16[48,1024]{1,0:T(8,128)(2,1)}, bf16[48,1024]{1,0:T(8,128)(2,1)S(1)}, u32[]{:S(2)}) copy-start(bf16[48,1024]{1,0:T(8,128)(2,1)S(1)} %collective-permute-done.mate_ref) | copy-start | bytes 294916
  17.9 13.7 %copy-start.6 = (bf16[48,1024]{1,0:T(8,128)(2,1)}, bf16[48,1024]{1,0:T(8,128)(2,1)S(1)}, u32[]{:S(2)}) copy-start(bf16[48,1024]{1,0:T(8,128)(2,1)S(1)} %collective-permute-done.1.outer_ref) | copy-start | bytes 294916
  24.4 10.5 %copy-start.1 = (bf16[384,1024]{1,0:T(8,128)(2,1)}, bf16[384,1024]{1,0:T(8,128)(2,1)S(1)}, u32[]{:S(2)}) copy-start(bf16[384,1024]{1,0:T(8,128)(2,1)S(1)} %get-tuple-element.33.pack_ref) | copy-start | bytes 2359300
  24.4 10.5 %collective-permute-start.2 = (bf16[384,1024]{1,0:T(8,128)(2,1)S(1)}, bf16[384,1024]{1,0:T(8,128)(2,1)S(1)}, u32[]{:S(2)}, u32[]{:S(2)}) collective-permute-start(bf16[384,1024]{1,0:T(8,128)(2,1)S(1)} %get-tuple-element.33.pack_ref), channel_id=1, source_target_pairs={{0,1},{1,0},{2,3},{3,2},{4,5},{5,4},{6,7},{7,6},{8,9},{9,8},{10,11... | collective-permute-start | bytes 2359304 | tf_op jit(solution)/shard_map/ppermute | solution.py:464
  31.5 3.4 %collective-permute-start.3 = (f32[256,128]{1,0:T(8,128)S(1)}, f32[256,128]{1,0:T(8,128)S(1)}, u32[]{:S(2)}, u32[]{:S(2)}) collective-permute-start(f32[256,128]{1,0:T(8,128)S(1)} %get-tuple-element.43), channel_id=1, source_target_pairs={{0,1},{1,0},{2,3},{3,2},{4,5},{5,4},{6,7},{7,6},{8,9},{9,8},{10,11... | collective-permute-start | bytes 393224 | tf_op jit(solution)/shard_map/ppermute | solution.py:480
  36.6 5.2 %copy-start = (bf16[1024,1024]{1,0:T(8,128)(2,1)S(1)}, bf16[1024,1024]{1,0:T(8,128)(2,1)}, u32[]{:S(2)}) copy-start(bf16[1024,1024]{1,0:T(8,128)(2,1)} %proj_ref.1) | copy-start | bytes 6291460
  36.6 34.7 %all-to-all-start = ((bf16[32,136,128]{2,1,0:T(8,128)(2,1)}), bf16[32,136,128]{2,1,0:T(8,128)(2,1)S(1)}, u32[]{:S(2)}, u32[]{:S(2)}) async-start(bf16[32,136,128]{2,1,0:T(8,128)(2,1)} %shard_map.106), calls=%async_computation | async-start | bytes 2228224 | tf_op jit(solution)/shard_map/all_to_all | solution.py:489
  41.8 1.1 %copy-start.2 = (bf16[384,1024]{1,0:T(8,128)(2,1)S(1)}, bf16[384,1024]{1,0:T(8,128)(2,1)}, u32[]{:S(2)}) copy-start(bf16[384,1024]{1,0:T(8,128)(2,1)} %copy-done.1) | copy-start | bytes 2359300
  42.9 1.2 %copy-start.3 = (f32[256,1024]{1,0:T(8,128)S(1)}, f32[256,1024]{1,0:T(8,128)}, u32[]{:S(2)}) copy-start(f32[256,1024]{1,0:T(8,128)} %get-tuple-element.38.gm_ref) | copy-start | bytes 3145732
  44.1 0.9 copy-start.5
  45.0 0.9 copy-start.7
